TPU v7x, 256 devices: a whole 4x4x8 slice. The times are simulated.
256 devices in a mesh: seq: 64 (over z, y, core), head: 4 (over x).
Axes of the slice: x: 4, y: 4, z: 8, core: 2. Of those that a mesh axis runs over, the one named last changes fastest.
Arguments:
- queries: bfloat16 [32768, 2048], P('seq', 'head'), may hold values from -8 to 8
- keys: bfloat16 [32768, 1024], P('seq', 'head'), may hold values from -8 to 8
- values: bfloat16 [32768, 1024], P('seq', 'head'), may hold values from -6 to 6
- output_gradient: bfloat16 [32768, 2048], P('seq', 'head'), may hold values from -6 to 6
- key_exponents: int32 [256, 8], P('seq', 'head'), may hold values from -1 to 1
- value_exponents: int32 [256, 8], P('seq', 'head'), may hold values from -1 to 1
- key_matrix: bfloat16 [5376, 1024], P(None, 'head'), may hold values from -0.1875 to 0.1875
- value_matrix: bfloat16 [5376, 1024], P(None, 'head'), may hold values from -0.1875 to 0.1875
Outputs:
- query_grad: bfloat16 [32768, 2048], P('seq', 'head')
- input_grad: bfloat16 [5376, 32768], P('head', 'seq')
All inputs are finite; a program needn't handle non-finite values.
Results may differ from a plain program's by a relative error of at most 0.015.
Values may be sent and summed in bfloat16 or wider, within the bound.
No kernel may reach another device: no remote copies, remote signals or barrier semaphores. Data moves between devices by JAX's collectives and lax.ppermute only.
A program may use at most 64 MiB of HBM per device.

v0:
```python
import jax
import jax.numpy as jnp
from jax import lax
from jax.sharding import PartitionSpec as P

HEAD_SIZE = 128
QUERY_SCALE = 168
ATTEND_WINDOW = 1024
SCALE_BLOCK = 128


def passed_along(value, axis, steps):
    count = lax.axis_size(axis)
    first, last = (max(0, -steps), min(count, count - steps))
    return lax.ppermute(value, axis, [(source, source + steps) for source in range(first, last)])


def cut_along(shard, dim, peers):
    before, after = (shard.shape[:dim], shard.shape[dim + 1 :])
    return jnp.moveaxis(shard.reshape(*before, peers, -1, *after), dim, 0)


def sum_at_owner(shard, axis, dim):
    tiles = cut_along(shard, dim, lax.axis_size(axis))
    arrived = lax.all_to_all(tiles, axis, split_axis=0, concat_axis=0, tiled=True)
    return arrived.astype(jnp.float32).sum(axis=0)


def power_of_two(exponents):
    return jnp.where(exponents > 0, 2.0, jnp.where(exponents < 0, 0.5, 1.0)).astype(jnp.float32)


def dequantize(stored, exponents):
    row_count = stored.shape[0]
    head_count = exponents.shape[1]
    factor = jnp.repeat(power_of_two(exponents), SCALE_BLOCK, axis=0)
    shaped = (
        stored.astype(jnp.float32).reshape(row_count, head_count, HEAD_SIZE) * factor[:, :, None]
    )
    return (shaped.reshape(row_count, head_count * HEAD_SIZE).astype(jnp.bfloat16), factor)


def window_means(raw_window, first_target, target_count, first_source):
    target_at = first_target + jnp.arange(target_count, dtype=jnp.int32)
    source_at = first_source + jnp.arange(raw_window.shape[0], dtype=jnp.int32)
    distance = target_at[:, None] - source_at[None, :]
    band = ((distance >= 0) & (distance < ATTEND_WINDOW)).astype(jnp.bfloat16)
    sums = jnp.dot(band, raw_window, preferred_element_type=jnp.float32)
    counts = jnp.clip(target_at + 1, 1, ATTEND_WINDOW).astype(jnp.float32)
    return sums / counts[:, None]


def attend(query_rows, grad_rows, smooth_window, value_window, first_key, first_query):
    token_count = query_rows.shape[0]
    key_count = smooth_window.shape[0]
    key_value_heads = smooth_window.shape[1] // HEAD_SIZE
    group_width = query_rows.shape[1] // (key_value_heads * HEAD_SIZE)
    score_scale = QUERY_SCALE ** (-0.5)
    query_at = first_query + jnp.arange(token_count, dtype=jnp.int32)
    key_at = first_key + jnp.arange(key_count, dtype=jnp.int32)
    distance = query_at[:, None] - key_at[None, :]
    allowed = (distance >= 0) & (distance < ATTEND_WINDOW) & (key_at[None, :] >= 0)
    query_head_count = query_rows.reshape(
        token_count, key_value_heads, group_width, HEAD_SIZE
    ).transpose(1, 2, 0, 3)
    gradient_heads = grad_rows.reshape(
        token_count, key_value_heads, group_width, HEAD_SIZE
    ).transpose(1, 2, 0, 3)
    key_heads = smooth_window.reshape(key_count, key_value_heads, HEAD_SIZE).transpose(1, 0, 2)
    value_heads = value_window.reshape(key_count, key_value_heads, HEAD_SIZE).transpose(1, 0, 2)

    def one_head(operands):
        head_queries, head_grads, head_keys, head_values = operands
        scores = (
            jnp.einsum("gqd,kd->gqk", head_queries, head_keys, preferred_element_type=jnp.float32)
            * score_scale
        )
        scores = jnp.where(allowed, scores, -jnp.inf)
        highest = jnp.max(scores, axis=-1, keepdims=True)
        weights = jnp.exp(scores - highest)
        shares = weights / jnp.sum(weights, axis=-1, keepdims=True)
        rounded = shares.astype(jnp.bfloat16)
        attended = jnp.einsum(
            "gqk,kd->gqd", rounded, head_values, preferred_element_type=jnp.float32
        )
        row_dot = jnp.sum(attended * head_grads.astype(jnp.float32), axis=-1, keepdims=True)
        share_grad = jnp.einsum(
            "gqd,kd->gqk", head_grads, head_values, preferred_element_type=jnp.float32
        )
        score_grad = (shares * (share_grad - row_dot)).astype(jnp.bfloat16)
        query_part = (
            score_scale
            * jnp.einsum("gqk,kd->qgd", score_grad, head_keys, preferred_element_type=jnp.float32)
        ).astype(jnp.bfloat16)
        key_part = score_scale * jnp.einsum(
            "gqk,gqd->kd", score_grad, head_queries, preferred_element_type=jnp.float32
        )
        value_part = jnp.einsum(
            "gqk,gqd->kd", rounded, head_grads, preferred_element_type=jnp.float32
        )
        return (query_part, key_part, value_part)

    query_part, key_part, value_part = lax.map(
        one_head, (query_head_count, gradient_heads, key_heads, value_heads)
    )
    query_grad = query_part.transpose(1, 0, 2, 3).reshape(
        token_count, key_value_heads * group_width * HEAD_SIZE
    )
    key_grad = key_part.transpose(1, 0, 2).reshape(key_count, key_value_heads * HEAD_SIZE)
    value_grad = value_part.transpose(1, 0, 2).reshape(key_count, key_value_heads * HEAD_SIZE)
    return (query_grad, key_grad, value_grad)


def local(
    queries, keys, values, output_gradient, key_exponents, value_exponents, key_matrix, value_matrix
):
    token_count = queries.shape[0]
    reach = ATTEND_WINDOW // token_count
    first_query = lax.axis_index("seq") * token_count
    first_key = first_query - reach * token_count
    exact_keys, key_multiplier = dequantize(keys, key_exponents)
    exact_values, value_multiplier = dequantize(values, value_exponents)
    raw_pieces = [passed_along(exact_keys, "seq", distance) for distance in range(reach, 0, -1)]
    raw_window = jnp.concatenate(raw_pieces + [exact_keys], 0)
    means = window_means(raw_window, first_query, token_count, first_key)
    smooth_own = (exact_keys.astype(jnp.float32) - means).astype(jnp.bfloat16)
    smooth_pieces = []
    value_pieces = []
    for distance in range(reach, 0, -1):
        smooth_piece, value_piece = passed_along((smooth_own, exact_values), "seq", distance)
        smooth_pieces.append(smooth_piece)
        value_pieces.append(value_piece)
    smooth_window = jnp.concatenate(smooth_pieces + [smooth_own], 0)
    value_window = jnp.concatenate(value_pieces + [exact_values], 0)
    query_grad, key_window_grad, value_window_grad = attend(
        queries, output_gradient, smooth_window, value_window, first_key, first_query
    )

    def slot_rows(array, distance):
        begin_row = (reach - distance) * token_count
        return array[begin_row : begin_row + token_count]

    key_grad = slot_rows(key_window_grad, 0)
    value_grad = slot_rows(value_window_grad, 0)
    for distance in range(1, reach + 1):
        moved_key, moved_value = (
            passed_along(
                slot_rows(key_window_grad, distance).astype(jnp.bfloat16), "seq", -distance
            ).astype(jnp.float32),
            passed_along(
                slot_rows(value_window_grad, distance).astype(jnp.bfloat16), "seq", -distance
            ).astype(jnp.float32),
        )
        key_grad = key_grad + moved_key
        value_grad = value_grad + moved_value
    scaled_keys = (key_grad * jnp.repeat(key_multiplier, HEAD_SIZE, axis=1)).astype(jnp.bfloat16)
    scaled_values = (value_grad * jnp.repeat(value_multiplier, HEAD_SIZE, axis=1)).astype(
        jnp.bfloat16
    )
    key_columns = scaled_keys.T
    value_columns = scaled_values.T
    input_grad = sum_at_owner(
        (
            jnp.dot(key_matrix, key_columns, preferred_element_type=jnp.float32)
            + jnp.dot(value_matrix, value_columns, preferred_element_type=jnp.float32)
        ).astype(jnp.bfloat16),
        "head",
        0,
    )
    return (query_grad, input_grad.astype(jnp.bfloat16))


def solution(mesh):
    in_specs = (
        P("seq", "head"),
        P("seq", "head"),
        P("seq", "head"),
        P("seq", "head"),
        P("seq", "head"),
        P("seq", "head"),
        P(None, "head"),
        P(None, "head"),
    )
    out_specs = (P("seq", "head"), P("head", "seq"))
    return jax.shard_map(local, mesh=mesh, in_specs=in_specs, out_specs=out_specs, check_vma=False)
```

profile of v0, /device:TPU:128, one launch (start us, length us, event | category | flops | bytes accessed | tf_op | source)
XLA Modules:
  0.0 198.0 jit_solution(133981653833102000)
XLA Ops:
  2.7 1.9 collective-permute-start.5
  4.6 3.5 %collective-permute-start.4 = (bf16[512,256]{0,1:T(8,128)(2,1)S(1)}, bf16[512,256]{0,1:T(8,128)(2,1)}, u32[]{:S(2)}, u32[]{:S(2)}) collective-permute-start(bf16[512,256]{0,1:T(8,128)(2,1)S(1)} %fusion.76), channel_id=1, source_target_pairs={{0,8},{4,12},{8,16},{12,20},{16,24},{20,28},{24,32},{28,36},{32,40... | collective-permute-start | bytes 786440 | tf_op jit(solution)/shard_map/ppermute | solution.py:15
  12.1 3.3 %collective-permute-start.1 = (bf16[512,256]{1,0:T(8,128)(2,1)}, bf16[512,256]{1,0:T(8,128)(2,1)}, u32[]{:S(2)}, u32[]{:S(2)}) collective-permute-start(bf16[512,256]{1,0:T(8,128)(2,1)} %fusion.78), channel_id=1, source_target_pairs={{0,4},{4,8},{8,12},{12,16},{16,20},{20,24},{24,28},{28,32},{32,36}... | collective-permute-start | bytes 786440 | tf_op jit(solution)/shard_map/ppermute | solution.py:15
  15.4 3.2 %collective-permute-start = (bf16[512,256]{1,0:T(8,128)(2,1)}, bf16[512,256]{1,0:T(8,128)(2,1)}, u32[]{:S(2)}, u32[]{:S(2)}) collective-permute-start(bf16[512,256]{1,0:T(8,128)(2,1)} %fusion.78), channel_id=1, source_target_pairs={{0,8},{4,12},{8,16},{12,20},{16,24},{20,28},{24,32},{28,36},{32,40... | collective-permute-start | bytes 786440 | tf_op jit(solution)/shard_map/ppermute | solution.py:15
  18.6 4.7 %collective-permute-done.1 = bf16[512,256]{1,0:T(8,128)(2,1)} collective-permute-done((bf16[512,256]{1,0:T(8,128)(2,1)}, bf16[512,256]{1,0:T(8,128)(2,1)}, u32[]{:S(2)}, u32[]{:S(2)}) %collective-permute-start.1) | collective-permute-done | bytes 262176 | tf_op jit(solution)/shard_map/ppermute | solution.py:15
  23.4 6.0 %collective-permute-done = bf16[512,256]{1,0:T(8,128)(2,1)} collective-permute-done((bf16[512,256]{1,0:T(8,128)(2,1)}, bf16[512,256]{1,0:T(8,128)(2,1)}, u32[]{:S(2)}, u32[]{:S(2)}) %collective-permute-start) | collective-permute-done | bytes 262176 | tf_op jit(solution)/shard_map/ppermute | solution.py:15
  29.4 2.8 %fusion.68 = bf16[512,256]{1,0:T(8,128)(2,1)} fusion(s32[1536]{0:T(1024)S(1)} %iota_add_fusion, s32[512]{0:T(512)S(1)} %iota_add_fusion.1, bf16[512,256]{1,0:T(8,128)(2,1)} %fusion.78, bf16[512,256]{1,0:T(8,128)(2,1)} %collective-permute-done.1, bf16[512,256]{1,0:T(8,128)(2,1)} %collective-permute-done, f32[512]{0:T(512)S(1)} %clamp_convert_fusion), kind=kOutput, calls=%fused_computation.68 | convolution fusion | flops 408682496 | bytes 1058816 | tf_op jit(solution)/shard_map/dot_general | solution.py:48
  38.4 2.0 pad_maximum_fusion
  40.4 3.4 %collective-permute-done.3 = bf16[512,256]{1,0:T(8,128)(2,1)} collective-permute-done((bf16[512,256]{1,0:T(8,128)(2,1)}, bf16[512,256]{1,0:T(8,128)(2,1)}, u32[]{:S(2)}, u32[]{:S(2)}) %collective-permute-start.3) | collective-permute-done | bytes 262176 | tf_op jit(solution)/shard_map/ppermute | solution.py:15
  43.8 5.1 %collective-permute-done.2 = bf16[512,256]{1,0:T(8,128)(2,1)} collective-permute-done((bf16[512,256]{1,0:T(8,128)(2,1)}, bf16[512,256]{1,0:T(8,128)(2,1)}, u32[]{:S(2)}, u32[]{:S(2)}) %collective-permute-start.2) | collective-permute-done | bytes 262176 | tf_op jit(solution)/shard_map/ppermute | solution.py:15
  48.9 2.1 %bitcast_bitcast_fusion = bf16[2,1536,128]{2,1,0:T(8,128)(2,1)} fusion(bf16[512,256]{1,0:T(8,128)(2,1)} %fusion.68, bf16[512,256]{1,0:T(8,128)(2,1)} %collective-permute-done.3, bf16[512,256]{1,0:T(8,128)(2,1)} %collective-permute-done.2), kind=kLoop, calls=%fused_computation.69 | loop fusion | flops 2359296 | bytes 1572864 | tf_op jit(solution)/shard_map/transpose | solution.py:69
  51.1 40.0 %while.15 = (s32[]{:T(128)}, bf16[2,512,2,128]{1,3,2,0:T(8,128)(2,1)}, f32[2,1536,128]{2,1,0:T(8,128)}, f32[2,1536,128]{1,2,0:T(8,128)}, bf16[2,1536,128]{2,1,0:...) while((s32[]{:T(128)}, ...), condition=%wide.region_4.5_spmd.clone, body=%wide.region_0.4_spmd.clone.sunk | while | flops 2436432384 | bytes 113294400 | solution.py:103
  53.6 6.2 %fusion.132 = (f32[2,512]{1,0:T(2,128)S(1)}, f32[2,512,1536]{2,1,0:T(8,128)}) fusion(pred[512,1536]{1,0:T(8,128)(4,1)S(1)} %fusion.131, bf16[2,1536,128]{2,1,0:T(8,128)(2,1)} %get-tuple-element.219, s32[]{:T(128)S(6)} %copy.81, bf16[2,2,512,128]{2,3,1,0:T(8,128)(2,1)} %get-tuple-element.220), kind=kOutput, calls=%fused_computation.109.clone.1 | convolution fusion | flops 408946176 | bytes 7738368 | tf_op jit(solution)/shard_map/while/body/eval_jaxpr/sub | solution.py:80
  59.8 3.8 %fusion.133 = bf16[2,512,1536]{2,1,0:T(8,128)(2,1)S(1)} fusion(f32[2,512,1536]{2,1,0:T(8,128)} %get-tuple-element.189, f32[2,512]{1,0:T(2,128)S(1)} %get-tuple-element.190), kind=kLoop, calls=%fused_computation.14.clone.1 | loop fusion | flops 3145728 | bytes 9441280 | tf_op jit(solution)/shard_map/while/body/eval_jaxpr/convert_element_type | solution.py:82
  73.6 6.2 %fusion.132 = (f32[2,512]{1,0:T(2,128)S(1)}, f32[2,512,1536]{2,1,0:T(8,128)}) fusion(pred[512,1536]{1,0:T(8,128)(4,1)S(1)} %fusion.131, bf16[2,1536,128]{2,1,0:T(8,128)(2,1)} %get-tuple-element.219, s32[]{:T(128)S(6)} %copy.81, bf16[2,2,512,128]{2,3,1,0:T(8,128)(2,1)} %get-tuple-element.220), kind=kOutput, calls=%fused_computation.109.clone.1 | convolution fusion | flops 408946176 | bytes 7738368 | tf_op jit(solution)/shard_map/while/body/eval_jaxpr/sub | solution.py:80
  79.8 3.8 %fusion.133 = bf16[2,512,1536]{2,1,0:T(8,128)(2,1)S(1)} fusion(f32[2,512,1536]{2,1,0:T(8,128)} %get-tuple-element.189, f32[2,512]{1,0:T(2,128)S(1)} %get-tuple-element.190), kind=kLoop, calls=%fused_computation.14.clone.1 | loop fusion | flops 3145728 | bytes 9441280 | tf_op jit(solution)/shard_map/while/body/eval_jaxpr/convert_element_type | solution.py:82
  99.9 2.1 %collective-permute-start.6 = (bf16[512,256]{1,0:T(8,128)(2,1)S(1)}, bf16[512,256]{1,0:T(8,128)(2,1)S(1)}, u32[]{:S(2)}, u32[]{:S(2)}) collective-permute-start(bf16[512,256]{1,0:T(8,128)(2,1)S(1)} %bitcast.199), channel_id=1, source_target_pairs={{4,0},{8,4},{12,8},{16,12},{20,16},{24,20},{28,24},{32,28},{36,32}... | collective-permute-start | bytes 786440 | tf_op jit(solution)/shard_map/ppermute | solution.py:15
  103.0 3.4 %collective-permute-done.8 = bf16[512,256]{0,1:T(8,128)(2,1)S(1)} collective-permute-done((bf16[512,256]{0,1:T(8,128)(2,1)S(1)}, bf16[512,256]{0,1:T(8,128)(2,1)S(1)}, u32[]{:S(2)}, u32[]{:S(2)}) %collective-permute-start.8) | collective-permute-done | bytes 262176 | tf_op jit(solution)/shard_map/ppermute | solution.py:15
  108.2 3.2 %collective-permute-done.7 = bf16[512,256]{1,0:T(8,128)(2,1)S(1)} collective-permute-done((bf16[512,256]{1,0:T(8,128)(2,1)S(1)}, bf16[512,256]{1,0:T(8,128)(2,1)S(1)}, u32[]{:S(2)}, u32[]{:S(2)}) %collective-permute-start.7) | collective-permute-done | bytes 262176 | tf_op jit(solution)/shard_map/ppermute | solution.py:15
  112.1 4.2 %fusion.54 = bf16[5376,512]{0,1:T(8,128)(2,1)} fusion(f32[512,5376]{1,0:T(8,128)S(1)} %fusion.92, bf16[5376,256]{1,0:T(8,128)(2,1)S(1)} %copy-done.14, bf16[512,256]{1,0:T(8,128)(2,1)S(1)} %collective-permute-done.7, bf16[512,256]{1,0:T(8,128)(2,1)S(1)} %collective-permute-done.6, f32[64,8,2,128]{3,2,1,0:T(2,128)S(1)} %bitcast.193, ...), kind=kOutput, calls=%fused_computation.57 | convolution fusion | flops 1415577600 | bytes 20840448 | tf_op jit(solution)/shard_map/dot_general | solution.py:164
  116.2 8.3 %copy.40 = bf16[5376,512]{1,0:T(8,128)(2,1)} copy(bf16[5376,512]{0,1:T(8,128)(2,1)} %fusion.54) | data formatting | bytes 11010048 | tf_op jit(solution)/shard_map/convert_element_type | solution.py:166
  124.6 5.3 %all-to-all-start = ((bf16[4,1344,512]{2,1,0:T(8,128)(2,1)}), bf16[4,1344,512]{2,1,0:T(8,128)(2,1)}, u32[]{:S(2)}, u32[]{:S(2)}) async-start(bf16[4,1344,512]{2,1,0:T(8,128)(2,1)} %bitcast.189), calls=%async_computation | async-start | bytes 11010048 | tf_op jit(solution)/shard_map/all_to_all | solution.py:25
  130.8 62.3 %all-to-all-done = bf16[4,1344,512]{2,1,0:T(8,128)(2,1)} async-done(((bf16[4,1344,512]{2,1,0:T(8,128)(2,1)}), bf16[4,1344,512]{2,1,0:T(8,128)(2,1)}, u32[]{:S(2)}, u32[]{:S(2)}) %all-to-all-start) | async-done | bytes 5505056 | tf_op jit(solution)/shard_map/all_to_all | solution.py:25
  193.1 4.9 %reduce_sum.30 = bf16[1344,512]{1,0:T(8,128)(2,1)} reduce(bf16[4,1344,512]{2,1,0:T(8,128)(2,1)} %all-to-all-done, bf16[]{:T(256)} %constant.25.clone.1), dimensions={0}, to_apply=%region_5.6 | reduce | flops 2064384 | bytes 6881282 | tf_op jit(solution)/shard_map/reduce_sum | solution.py:26
  (132 shorter events, 45.1 us)
Async XLA Ops:
  0.6 105.9 %copy-start = (bf16[5376,256]{1,0:T(8,128)(2,1)S(1)}, bf16[5376,256]{1,0:T(8,128)(2,1)}, u32[]{:S(2)}) copy-start(bf16[5376,256]{1,0:T(8,128)(2,1)} %param.17) | copy-start | bytes 8257540
  1.6 17.0 %copy-start.22 = (f32[1,2,4,128]{3,1,2,0:T(2,128)}, f32[1,2,4,128]{3,1,2,0:T(2,128)S(1)}, u32[]{:S(2)}) copy-start(f32[1,2,4,128]{3,1,2,0:T(2,128)S(1)} %copy.71) | copy-start | bytes 12292
  2.7 35.7 %collective-permute-start.5 = (bf16[512,256]{0,1:T(8,128)(2,1)S(1)}, bf16[512,256]{0,1:T(8,128)(2,1)}, u32[]{:S(2)}, u32[]{:S(2)}) collective-permute-start(bf16[512,256]{0,1:T(8,128)(2,1)S(1)} %fusion.76), channel_id=1, source_target_pairs={{0,4},{4,8},{8,12},{12,16},{16,20},{20,24},{24,28},{28,32},{32,36}... | collective-permute-start | bytes 786440 | tf_op jit(solution)/shard_map/ppermute | solution.py:15
  4.6 33.8 %collective-permute-start.4 = (bf16[512,256]{0,1:T(8,128)(2,1)S(1)}, bf16[512,256]{0,1:T(8,128)(2,1)}, u32[]{:S(2)}, u32[]{:S(2)}) collective-permute-start(bf16[512,256]{0,1:T(8,128)(2,1)S(1)} %fusion.76), channel_id=1, source_target_pairs={{0,8},{4,12},{8,16},{12,20},{16,24},{20,28},{24,32},{28,36},{32,40... | collective-permute-start | bytes 786440 | tf_op jit(solution)/shard_map/ppermute | solution.py:15
  12.1 11.3 %collective-permute-start.1 = (bf16[512,256]{1,0:T(8,128)(2,1)}, bf16[512,256]{1,0:T(8,128)(2,1)}, u32[]{:S(2)}, u32[]{:S(2)}) collective-permute-start(bf16[512,256]{1,0:T(8,128)(2,1)} %fusion.78), channel_id=1, source_target_pairs={{0,4},{4,8},{8,12},{12,16},{16,20},{20,24},{24,28},{28,32},{32,36}... | collective-permute-start | bytes 786440 | tf_op jit(solution)/shard_map/ppermute | solution.py:15
  15.4 14.0 %collective-permute-start = (bf16[512,256]{1,0:T(8,128)(2,1)}, bf16[512,256]{1,0:T(8,128)(2,1)}, u32[]{:S(2)}, u32[]{:S(2)}) collective-permute-start(bf16[512,256]{1,0:T(8,128)(2,1)} %fusion.78), channel_id=1, source_target_pairs={{0,8},{4,12},{8,16},{12,20},{16,24},{20,28},{24,32},{28,36},{32,40... | collective-permute-start | bytes 786440 | tf_op jit(solution)/shard_map/ppermute | solution.py:15
  18.6 17.5 %copy-start.16 = (bf16[512,512]{1,0:T(8,128)(2,1)S(1)}, bf16[512,512]{1,0:T(8,128)(2,1)}, u32[]{:S(2)}) copy-start(bf16[512,512]{1,0:T(8,128)(2,1)} %param.10) | copy-start | bytes 1572868
  32.2 11.6 %collective-permute-start.3 = (bf16[512,256]{1,0:T(8,128)(2,1)}, bf16[512,256]{1,0:T(8,128)(2,1)}, u32[]{:S(2)}, u32[]{:S(2)}) collective-permute-start(bf16[512,256]{1,0:T(8,128)(2,1)} %fusion.68), channel_id=1, source_target_pairs={{0,4},{4,8},{8,12},{12,16},{16,20},{20,24},{24,28},{28,32},{32,36}... | collective-permute-start | bytes 786440 | tf_op jit(solution)/shard_map/ppermute | solution.py:15
  34.2 14.8 %collective-permute-start.2 = (bf16[512,256]{1,0:T(8,128)(2,1)}, bf16[512,256]{1,0:T(8,128)(2,1)}, u32[]{:S(2)}, u32[]{:S(2)}) collective-permute-start(bf16[512,256]{1,0:T(8,128)(2,1)} %fusion.68), channel_id=1, source_target_pairs={{0,8},{4,12},{8,16},{12,20},{16,24},{20,28},{24,32},{28,36},{32,40... | collective-permute-start | bytes 786440 | tf_op jit(solution)/shard_map/ppermute | solution.py:15
  59.8 3.8 %copy-start.5 = (bf16[1,2,512,128]{3,2,1,0:T(8,128)(2,1)S(1)}, bf16[1,2,512,128]{3,2,1,0:T(8,128)(2,1)}, u32[]{:S(2)}) copy-start(bf16[1,2,512,128]{3,2,1,0:T(8,128)(2,1)} %copy.73) | copy-start | bytes 786436 | tf_op jit(solution)/shard_map/while
  59.8 3.8 %copy-start.15 = (bf16[2,1536,128]{1,2,0:T(8,128)(2,1)S(1)}, bf16[2,1536,128]{1,2,0:T(8,128)(2,1)}, u32[]{:S(2)}) copy-start(bf16[2,1536,128]{1,2,0:T(8,128)(2,1)} %get-tuple-element.222) | copy-start | bytes 2359300 | tf_op jit(solution)/shard_map/while
  59.8 4.9 %copy-start.1 = (f32[2,512,1536]{2,1,0:T(8,128)S(1)}, f32[2,512,1536]{2,1,0:T(8,128)}, u32[]{:S(2)}) copy-start(f32[2,512,1536]{2,1,0:T(8,128)} %get-tuple-element.189) | copy-start | bytes 18874372 | tf_op jit(solution)/shard_map/while
  79.8 3.8 %copy-start.15 = (bf16[2,1536,128]{1,2,0:T(8,128)(2,1)S(1)}, bf16[2,1536,128]{1,2,0:T(8,128)(2,1)}, u32[]{:S(2)}) copy-start(bf16[2,1536,128]{1,2,0:T(8,128)(2,1)} %get-tuple-element.222) | copy-start | bytes 2359300 | tf_op jit(solution)/shard_map/while
  79.8 4.9 %copy-start.1 = (f32[2,512,1536]{2,1,0:T(8,128)S(1)}, f32[2,512,1536]{2,1,0:T(8,128)}, u32[]{:S(2)}) copy-start(f32[2,512,1536]{2,1,0:T(8,128)} %get-tuple-element.189) | copy-start | bytes 18874372 | tf_op jit(solution)/shard_map/while
  91.1 5.5 %copy-start.11 = (f32[2,1536,128]{2,1,0:T(8,128)S(1)}, f32[2,1536,128]{2,1,0:T(8,128)}, u32[]{:S(2)}) copy-start(f32[2,1536,128]{2,1,0:T(8,128)} %get-tuple-element.52) | copy-start | bytes 4718596
  92.7 13.7 %copy-start.23 = (f32[1,2,4,128]{3,1,2,0:T(2,128)S(1)}, f32[1,2,4,128]{3,1,2,0:T(2,128)}, u32[]{:S(2)}) copy-start(f32[1,2,4,128]{3,1,2,0:T(2,128)} %copy-done.22) | copy-start | bytes 12292
  92.8 10.2 %collective-permute-start.9 = (bf16[512,256]{0,1:T(8,128)(2,1)S(1)}, bf16[512,256]{0,1:T(8,128)(2,1)S(1)}, u32[]{:S(2)}, u32[]{:S(2)}) collective-permute-start(bf16[512,256]{0,1:T(8,128)(2,1)S(1)} %bitcast.202), channel_id=1, source_target_pairs={{8,0},{12,4},{16,8},{20,12},{24,16},{28,20},{32,24},{36,28},{40,32... | collective-permute-start | bytes 786440 | tf_op jit(solution)/shard_map/ppermute | solution.py:15
  94.7 11.7 %collective-permute-start.8 = (bf16[512,256]{0,1:T(8,128)(2,1)S(1)}, bf16[512,256]{0,1:T(8,128)(2,1)S(1)}, u32[]{:S(2)}, u32[]{:S(2)}) collective-permute-start(bf16[512,256]{0,1:T(8,128)(2,1)S(1)} %bitcast.201), channel_id=1, source_target_pairs={{4,0},{8,4},{12,8},{16,12},{20,16},{24,20},{28,24},{32,28},{36,32}... | collective-permute-start | bytes 786440 | tf_op jit(solution)/shard_map/ppermute | solution.py:15
  98.0 13.4 %collective-permute-start.7 = (bf16[512,256]{1,0:T(8,128)(2,1)S(1)}, bf16[512,256]{1,0:T(8,128)(2,1)S(1)}, u32[]{:S(2)}, u32[]{:S(2)}) collective-permute-start(bf16[512,256]{1,0:T(8,128)(2,1)S(1)} %bitcast.200), channel_id=1, source_target_pairs={{8,0},{12,4},{16,8},{20,12},{24,16},{28,20},{32,24},{36,28},{40,32... | collective-permute-start | bytes 786440 | tf_op jit(solution)/shard_map/ppermute | solution.py:15
  99.9 12.1 %collective-permute-start.6 = (bf16[512,256]{1,0:T(8,128)(2,1)S(1)}, bf16[512,256]{1,0:T(8,128)(2,1)S(1)}, u32[]{:S(2)}, u32[]{:S(2)}) collective-permute-start(bf16[512,256]{1,0:T(8,128)(2,1)S(1)} %bitcast.199), channel_id=1, source_target_pairs={{4,0},{8,4},{12,8},{16,12},{20,16},{24,20},{28,24},{32,28},{36,32}... | collective-permute-start | bytes 786440 | tf_op jit(solution)/shard_map/ppermute | solution.py:15
  106.5 5.5 %copy-start.8 = (f32[512,2,128]{2,1,0:T(2,128)S(1)}, f32[512,2,128]{2,1,0:T(2,128)}, u32[]{:S(2)}) copy-start(f32[512,2,128]{2,1,0:T(2,128)} %copy-done.7) | copy-start | bytes 1572868
  106.5 5.5 %copy-start.14 = (bf16[5376,256]{1,0:T(8,128)(2,1)S(1)}, bf16[5376,256]{1,0:T(8,128)(2,1)}, u32[]{:S(2)}) copy-start(bf16[5376,256]{1,0:T(8,128)(2,1)} %param.16) | copy-start | bytes 8257540
  124.5 5.3 %copy-start.19 = (bf16[2,512,2,128]{1,3,2,0:T(8,128)(2,1)S(1)}, bf16[2,512,2,128]{1,3,2,0:T(8,128)(2,1)}, u32[]{:S(2)}) copy-start(bf16[2,512,2,128]{1,3,2,0:T(8,128)(2,1)} %get-tuple-element.51) | copy-start | bytes 1572868
  124.6 68.5 %all-to-all-start = ((bf16[4,1344,512]{2,1,0:T(8,128)(2,1)}), bf16[4,1344,512]{2,1,0:T(8,128)(2,1)}, u32[]{:S(2)}, u32[]{:S(2)}) async-start(bf16[4,1344,512]{2,1,0:T(8,128)(2,1)} %bitcast.189), calls=%async_computation | async-start | bytes 11010048 | tf_op jit(solution)/shard_map/all_to_all | solution.py:25
  (26 other events, 43.1 us)
where the time goes:
time: 200 us; the launch traced here: 198 us
  waiting for transfers between devices  89.8 us (45%)
  matrix products  31.3 us (16%)
  starting transfers between devices  28.9 us (14%)
  local copies, waits for them, and re-layouts  23.4 us (12%)
  other arithmetic  23.4 us (12%)
    all_to_all x1, waiting for transfers between devices, sum_at_owner(): lax.all_to_all(tiles, axis, split_axis=0, concat_axis=0, tiled=True)  62.3 us
    ppermute x10, waiting for transfers between devices, passed_along(): lax.ppermute(value, axis, [(source, source + steps) for source in range(f...  27.5 us
    ppermute x10, starting transfers between devices, passed_along(): lax.ppermute(value, axis, [(source, source + steps) for source in range(f...  23.6 us
    sub x2, matrix products, one_head(): weights = jnp.exp(scores - highest)  12.4 us
    convert_element_type x1, local copies, waits for them, and re-layouts, local(): input_grad = sum_at_owner((jnp.dot(key_matrix, key_columns, preferred_ele...  8.33 us
    convert_element_type x2, other arithmetic, one_head(): rounded = shares.astype(jnp.bfloat16)  7.51 us
    while x60, local copies, waits for them, and re-layouts  6.07 us
    all_to_all x1, starting transfers between devices, sum_at_owner(): lax.all_to_all(tiles, axis, split_axis=0, concat_axis=0, tiled=True)  5.26 us
  transfers between devices with their start and end apart: 11, of which 9 were waited for; matrix products, arithmetic and copies ran while one was open for 7% of the time, Pallas kernels for 0%

commit v1 on v0

v1 whole, which is shorter than its diff:
```python
import functools

import jax
import jax.numpy as jnp
from jax import lax
from jax.experimental import pallas as pl
from jax.experimental.pallas import tpu as pltpu
from jax.sharding import PartitionSpec as P

HEAD_SIZE = 128
QUERY_SCALE = 168
ATTEND_WINDOW = 1024
SCALE_BLOCK = 128
TILE = 256
BLOCK = 512
WINDOW_ROWS = 3 * BLOCK
HALF_ROWS = 672
LOG2_E = 1.4426950408889634
MEBI = 1024 * 1024

NN = (((1,), (0,)), ((), ()))
NT = (((1,), (1,)), ((), ()))


def product(left, right, dims):
    return lax.dot_general(left, right, dims, preferred_element_type=jnp.float32)


def vmem_call(kernel, out_shapes, inputs, in_specs=None, scratch=(), mebibytes=8):
    whole = pl.BlockSpec(memory_space=pltpu.VMEM)
    return pl.pallas_call(
        kernel,
        out_shape=out_shapes,
        in_specs=in_specs if in_specs is not None else [whole] * len(inputs),
        out_specs=jax.tree.map(lambda _: whole, out_shapes),
        scratch_shapes=list(scratch),
        cost_estimate=pl.CostEstimate(flops=1, bytes_accessed=1, transcendentals=0),
        compiler_params=pltpu.CompilerParams(vmem_limit_bytes=mebibytes * MEBI),
    )(*inputs)


def shape_of(rows, columns, dtype=jnp.bfloat16):
    return jax.ShapeDtypeStruct((rows, columns), dtype)


SMEM = pl.BlockSpec(memory_space=pltpu.SMEM)
VMEM = pl.BlockSpec(memory_space=pltpu.VMEM)
HBM = pl.BlockSpec(memory_space=pltpu.MemorySpace.HBM)


def factor_of(exponent):
    return jnp.where(exponent > 0, 2.0, jnp.where(exponent < 0, 0.5, 1.0)).astype(jnp.float32)


def dequantize_kernel(key_exps, value_exps, keys, values, key_out, value_out, total_out, key_in, value_in, arrivals):
    fetch_keys = pltpu.make_async_copy(keys, key_in, arrivals.at[0])
    fetch_values = pltpu.make_async_copy(values, value_in, arrivals.at[1])
    fetch_keys.start()
    fetch_values.start()
    for part, (fetch, source, exponents, target) in enumerate(
        ((fetch_keys, key_in, key_exps, key_out), (fetch_values, value_in, value_exps, value_out))
    ):
        fetch.wait()
        for head in range(2):
            lanes = slice(head * HEAD_SIZE, (head + 1) * HEAD_SIZE)
            total = jnp.zeros((1, HEAD_SIZE), jnp.float32)
            for block in range(BLOCK // SCALE_BLOCK):
                rows = slice(block * SCALE_BLOCK, (block + 1) * SCALE_BLOCK)
                scaled = source[rows, lanes].astype(jnp.float32) * factor_of(exponents[head, block])
                target[rows, lanes] = scaled.astype(jnp.bfloat16)
                if part == 0:
                    total = total + jnp.sum(scaled, axis=0, keepdims=True)
            if part == 0:
                total_out[:, lanes] = jnp.broadcast_to(total, (8, HEAD_SIZE))


def smooth_kernel(place, own, older, total, smooth_out):
    first = place[0] * BLOCK
    row = lax.broadcasted_iota(jnp.int32, (BLOCK, BLOCK), 0)
    column = lax.broadcasted_iota(jnp.int32, (BLOCK, BLOCK), 1)
    upto = (column <= row).astype(jnp.float32).astype(jnp.bfloat16)
    after = (column > row).astype(jnp.float32).astype(jnp.bfloat16)
    sums = product(upto, own[...], NN) + product(after, older[...], NN) + total[0:1, :]
    position = first + lax.broadcasted_iota(jnp.int32, (BLOCK, 1), 0)
    counts = jnp.minimum(position + 1, ATTEND_WINDOW).astype(jnp.float32)
    smooth_out[...] = (own[...].astype(jnp.float32) - sums / counts).astype(jnp.bfloat16)


def attend_kernel(
    head, place, queries, grads, keys2, last, keys0, values2, values0,
    query_grad, grad2, grad1, grad0,
    key_rows, value_rows, key_cols, value_cols, weights, shares_out, score_out,
):
    scale = QUERY_SCALE ** (-0.5)
    index = place[0]
    lanes = slice(head * HEAD_SIZE, (head + 1) * HEAD_SIZE)
    last_lanes = slice(256 + head * HEAD_SIZE, 256 + (head + 1) * HEAD_SIZE)
    for at, source in enumerate((keys2, last, keys0)):
        key_rows[at * BLOCK : (at + 1) * BLOCK, :] = source[:, lanes]
    for at, source in enumerate((values2, last, values0)):
        value_rows[at * BLOCK : (at + 1) * BLOCK, :] = source[:, last_lanes if at == 1 else lanes]
    eye = (
        lax.broadcasted_iota(jnp.int32, (HEAD_SIZE, HEAD_SIZE), 0)
        == lax.broadcasted_iota(jnp.int32, (HEAD_SIZE, HEAD_SIZE), 1)
    ).astype(jnp.float32).astype(jnp.bfloat16)
    key_cols[...] = product(eye, key_rows[...], NT).astype(jnp.bfloat16)
    value_cols[...] = product(eye, value_rows[...], NT).astype(jnp.bfloat16)
    key_at = lax.broadcasted_iota(jnp.int32, (TILE, TILE), 0)
    query_at = lax.broadcasted_iota(jnp.int32, (TILE, TILE), 1)
    lowest = -jnp.inf

    for member in range(2):
        for tile in range(BLOCK // TILE):
            rows = slice(tile * TILE, (tile + 1) * TILE)
            columns = slice((2 * head + member) * HEAD_SIZE, (2 * head + member + 1) * HEAD_SIZE)
            query = queries[rows, columns]
            grad = grads[rows, columns]
            grad_cols = product(eye, grad, NT)
            part = 2 * member + tile
            place_at = slice(part * TILE, (part + 1) * TILE)
            valid = [index >= 2, index >= 2, index >= 1, index >= 1, None, None]
            highest = jnp.full((1, TILE), lowest, jnp.float32)
            for step in range(5):
                source = tile + step
                at = slice(step * TILE, (step + 1) * TILE)
                scores = product(key_rows[source * TILE : (source + 1) * TILE, :], query, NT)
                if step == 0:
                    scores = jnp.where(key_at > query_at, scores, lowest)
                if step == 4:
                    scores = jnp.where(key_at <= query_at, scores, lowest)
                weights[part, at, :] = scores
                peak = jnp.max(scores, axis=0, keepdims=True)
                if valid[source] is not None:
                    peak = jnp.where(valid[source], peak, lowest)
                highest = jnp.maximum(highest, peak)
            factor = scale * LOG2_E
            shift = highest * factor
            total = jnp.zeros((1, TILE), jnp.float32)
            for step in range(5):
                source = tile + step
                at = slice(step * TILE, (step + 1) * TILE)
                off = shift if valid[source] is None else jnp.where(valid[source], shift, jnp.inf)
                weight = jnp.exp2(weights[part, at, :] * factor - off)
                weights[part, at, :] = weight
                total = total + jnp.sum(weight, axis=0, keepdims=True)
            inverse = 1.0 / total
            attended = jnp.zeros((HEAD_SIZE, TILE), jnp.float32)
            for step in range(5):
                source = tile + step
                rounded = (weights[part, step * TILE : (step + 1) * TILE, :] * inverse).astype(jnp.bfloat16)
                shares_out[source * TILE : (source + 1) * TILE, place_at] = rounded
                attended = attended + product(value_cols[:, source * TILE : (source + 1) * TILE], rounded, NN)
            row_dot = jnp.sum(attended * grad_cols, axis=0, keepdims=True)
            query_part = jnp.zeros((HEAD_SIZE, TILE), jnp.float32)
            for step in range(5):
                source = tile + step
                share_grad = product(value_rows[source * TILE : (source + 1) * TILE, :], grad, NT)
                share = weights[part, step * TILE : (step + 1) * TILE, :] * inverse
                score_grad = (share * (share_grad - row_dot)).astype(jnp.bfloat16)
                score_out[source * TILE : (source + 1) * TILE, place_at] = score_grad
                query_part = query_part + product(key_cols[:, source * TILE : (source + 1) * TILE], score_grad, NN)
            query_grad[rows, member * HEAD_SIZE : (member + 1) * HEAD_SIZE] = (
                (query_part * scale).T.astype(jnp.bfloat16)
            )

    for source in range(6):
        rows = slice(source * TILE, (source + 1) * TILE)
        out, first = ((grad2, 0), (grad1, 2), (grad0, 4))[source // 2]
        target = slice((source - first) * TILE, (source - first + 1) * TILE)
        if 1 <= source <= 4:
            parts = [(slice(member * BLOCK, (member + 1) * BLOCK), member, slice(0, BLOCK)) for member in range(2)]
        else:
            tile = 0 if source == 0 else 1
            parts = [
                (slice((2 * member + tile) * TILE, (2 * member + tile + 1) * TILE), member, slice(tile * TILE, (tile + 1) * TILE))
                for member in range(2)
            ]
        key_part = jnp.zeros((TILE, HEAD_SIZE), jnp.float32)
        value_part = jnp.zeros((TILE, HEAD_SIZE), jnp.float32)
        for place_at, member, query_rows in parts:
            columns = slice((2 * head + member) * HEAD_SIZE, (2 * head + member + 1) * HEAD_SIZE)
            key_part = key_part + product(score_out[rows, place_at], queries[query_rows, columns], NN)
            value_part = value_part + product(shares_out[rows, place_at], grads[query_rows, columns], NN)
        out[target, 0:HEAD_SIZE] = (key_part * scale).astype(out.dtype)
        out[target, HEAD_SIZE : 2 * HEAD_SIZE] = value_part.astype(out.dtype)


def merge_kernel(place, older, arrived, out):
    odd = (place[0] & 1).astype(jnp.float32)
    out[...] = (older[...] + odd * arrived[...].astype(jnp.float32)).astype(jnp.bfloat16)


def finish_kernel(head, place, key_exps, value_exps, own, sibling, later, out):
    even = (1 - (place[0] & 1)).astype(jnp.float32)
    for block in range(BLOCK // SCALE_BLOCK):
        rows = slice(block * SCALE_BLOCK, (block + 1) * SCALE_BLOCK)
        for part, exponents in ((0, key_exps), (1, value_exps)):
            at = (rows, slice(part * HEAD_SIZE, (part + 1) * HEAD_SIZE))
            total = own[at] + even * sibling[at].astype(jnp.float32) + later[at].astype(jnp.float32)
            out[at] = (total * factor_of(exponents[head, block])).astype(jnp.bfloat16)


def project_kernel(head, place, own, *rest):
    mine, other, pieces, out = rest[:3], rest[3:6], rest[6:10], rest[-1]
    core = place[0] & 1
    half = HALF_ROWS
    lanes = slice(head * HEAD_SIZE, (head + 1) * HEAD_SIZE)
    channels = jnp.concatenate([piece[...] for piece in pieces], axis=1)
    for half_at, matrices in ((core, mine), (1 - core, other)):
        rows = pl.ds(pl.multiple_of(half_at * half, 16), half)
        parts = [own[0, rows, lanes], own[1, rows, lanes]]
        for matrix in matrices:
            parts += [matrix[0:half, lanes], matrix[half : 2 * half, lanes]]
        total = product(jnp.concatenate(parts, axis=1), channels, NT)
        if len(rest) == 12:
            total = total + rest[10][rows, :]
        out[rows, :] = total.astype(out.dtype)


def fetch_kernel(place, keys, values, queries, grads, ready, sent1, sent2, sent3, own, query_out, grad_out, arrivals):
    half = HALF_ROWS
    core = place[0] & 1
    copies = []
    for steps, target in ((1, sent1), (2, sent2), (3, sent3)):
        begin = pl.multiple_of(((place[1] + steps) & 3) * (2 * half) + core * half, 16)
        for part, matrix in enumerate((keys, values)):
            copies.append((matrix.at[pl.ds(begin, half), :], target.at[pl.ds(part * half, half), :]))
    begin = pl.multiple_of(place[1] * (2 * half), 16)
    for part, matrix in enumerate((keys, values)):
        copies.append((matrix.at[pl.ds(begin, 2 * half), :], own.at[part]))
    copies += [(queries, query_out), (grads, grad_out)]
    started = [pltpu.make_async_copy(*pair, arrivals.at[at]) for at, pair in enumerate(copies)]
    for copy in started:
        copy.start()
    for copy in started:
        copy.wait()


def shift_pairs(count, steps):
    return [(at, at + steps) for at in range(max(0, -steps), min(count, count - steps))]


def local(
    queries, keys, values, output_gradient, key_exponents, value_exponents, key_matrix, value_matrix
):
    count = lax.axis_size("seq")
    groups = lax.axis_size("head")
    index = lax.axis_index("seq")
    place = jnp.stack([index, lax.axis_index("head")]).astype(jnp.int32)
    core = index & 1
    siblings = [(at, at ^ 1) for at in range(count)]

    def to_sibling(value):
        return lax.ppermute(value, "seq", siblings)

    def onward(value, steps):
        return lax.ppermute(value, "seq", shift_pairs(count, steps))

    key_exponents, value_exponents = key_exponents.T, value_exponents.T
    exact_keys, exact_values, key_total = vmem_call(
        dequantize_kernel,
        (shape_of(BLOCK, 256), shape_of(BLOCK, 256), shape_of(8, 256, jnp.float32)),
        (key_exponents, value_exponents, keys, values),
        in_specs=[SMEM, SMEM, HBM, HBM],
        mebibytes=60,
        scratch=[
            pltpu.VMEM((BLOCK, 256), jnp.bfloat16),
            pltpu.VMEM((BLOCK, 256), jnp.bfloat16),
            pltpu.SemaphoreType.DMA((2,)),
        ],
    )
    older_keys = onward(exact_keys, 2)
    last_total = onward(key_total, 1)

    model_rows = key_matrix.shape[0] // groups
    piece_shape = shape_of(model_rows, 256)
    *sent, own, queries, output_gradient = vmem_call(
        fetch_kernel,
        (piece_shape, piece_shape, piece_shape, jax.ShapeDtypeStruct((2, model_rows, 256), jnp.bfloat16), shape_of(BLOCK, 512), shape_of(BLOCK, 512)),
        (place, key_matrix, value_matrix, queries, output_gradient, exact_keys),
        in_specs=[SMEM] + [HBM] * 4 + [pl.BlockSpec(memory_space=pl.ANY)],
        scratch=[pltpu.SemaphoreType.DMA((10,))],
        mebibytes=57,
    )
    fetched = [
        lax.ppermute(piece, "head", [(at, (at + steps) % groups) for at in range(groups)])
        for steps, piece in zip(range(1, groups), sent)
    ]

    late_values, _ = lax.optimization_barrier((exact_values, last_total))
    older_values = onward(late_values, 2)
    older_keys, _ = lax.optimization_barrier((older_keys, own))
    smooth = vmem_call(
        smooth_kernel, shape_of(BLOCK, 256), (place, exact_keys, older_keys, last_total), in_specs=[SMEM, VMEM, VMEM, VMEM]
    )
    older_smooth = onward(smooth, 2)
    last = to_sibling(
        jnp.where(
            core == 0,
            jnp.concatenate([smooth, exact_values], axis=1),
            jnp.concatenate([older_smooth, older_values], axis=1),
        )
    )

    query_grads, gathered = [], []
    for head in range(2):
        if head == 1:
            queries, _ = lax.optimization_barrier((queries, back))
        query_part, grad2, grad1, grad0 = vmem_call(
            functools.partial(attend_kernel, head),
            (shape_of(BLOCK, 256), shape_of(BLOCK, 256, jnp.float32), shape_of(BLOCK, 256), shape_of(BLOCK, 256, jnp.float32)),
            (place, queries, output_gradient, older_smooth, last, smooth, older_values, exact_values),
            in_specs=[SMEM] + [VMEM] * 7,
            scratch=[
                pltpu.VMEM((WINDOW_ROWS, HEAD_SIZE), jnp.bfloat16),
                pltpu.VMEM((WINDOW_ROWS, HEAD_SIZE), jnp.bfloat16),
                pltpu.VMEM((HEAD_SIZE, WINDOW_ROWS), jnp.bfloat16),
                pltpu.VMEM((HEAD_SIZE, WINDOW_ROWS), jnp.bfloat16),
                pltpu.VMEM((4, 5 * TILE, TILE), jnp.float32),
                pltpu.VMEM((WINDOW_ROWS, 4 * TILE), jnp.bfloat16),
                pltpu.VMEM((WINDOW_ROWS, 4 * TILE), jnp.bfloat16),
            ],
            mebibytes=18,
        )
        query_grads.append(query_part)
        sibling_grad = to_sibling(grad1)
        back = vmem_call(merge_kernel, shape_of(BLOCK, 256), (place, grad2, sibling_grad), in_specs=[SMEM, VMEM, VMEM])
        later_grad = onward(back, -2)
        scaled = vmem_call(
            functools.partial(finish_kernel, head),
            shape_of(BLOCK, 256),
            (place, key_exponents, value_exponents, grad0, sibling_grad, later_grad),
            in_specs=[SMEM, SMEM, SMEM, VMEM, VMEM, VMEM],
        )
        arrived = [scaled]
        for steps in (1, 2, 3):
            pairs = [(at, (at + steps) % groups) for at in range(groups)]
            arrived.append(lax.ppermute(scaled, "head", pairs))
        gathered.append(arrived)
    fetched = lax.optimization_barrier((*fetched, gathered[0][0]))[:-1]
    swapped = [to_sibling(piece) for piece in fetched]
    input_grad = None
    for head in range(2):
        more = () if input_grad is None else (input_grad,)
        input_grad = vmem_call(
            functools.partial(project_kernel, head),
            shape_of(model_rows, BLOCK, jnp.bfloat16 if head else jnp.float32),
            (place, own, *fetched, *swapped, *gathered[head], *more),
            in_specs=[SMEM] + [VMEM] * (11 + len(more)),
            mebibytes=18,
        )
    return jnp.concatenate(query_grads, axis=1), input_grad


def solution(mesh):
    in_specs = (
        P("seq", "head"),
        P("seq", "head"),
        P("seq", "head"),
        P("seq", "head"),
        P("seq", "head"),
        P("seq", "head"),
        P(None, "head"),
        P(None, "head"),
    )
    out_specs = (P("seq", "head"), P("head", "seq"))
    return jax.shard_map(local, mesh=mesh, in_specs=in_specs, out_specs=out_specs, check_vma=False)
```

time: 200 us -> 117 us (0.58)
  waiting for transfers between devices: 89.8 us -> 48.8 us
  Pallas kernels: 0 us -> 32.2 us
  matrix products: 31.3 us -> 0 us
  other arithmetic: 23.4 us -> 1.62 us
  local copies, waits for them, and re-layouts: 23.4 us -> 2.11 us
    all_to_all x1 -> x0, waiting for transfers between devices: 62.3 us -> none  [sum_at_owner(): lax.all_to_all(tiles, axis, split_axis=0, concat_axis=0, tiled=True)]
    pallas_call x0 -> x11, Pallas kernels: none -> 32.2 us  [vmem_call(): pl.pallas_call(kernel, out_shape=out_shapes, in_specs=in_specs if in_spec...]
    ppermute x10 -> x21, waiting for transfers between devices: 27.5 us -> 48.8 us  [the longest x6 20.9 us: local(): arrived.append(lax.ppermute(scaled, 'head', pairs))]
    dot_general x13 -> x0, matrix products: 19 us -> none  [the longest x1 4.17 us: local(): jnp.dot(key_matrix, key_columns, preferred_element_type=jnp.float32)]
    sub x2 -> x0, matrix products: 12.4 us -> none  [one_head(): weights = jnp.exp(scores - highest)]
    convert_element_type x6 -> x0, other arithmetic: 9.4 us -> none  [the longest x2 7.51 us: one_head(): rounded = shares.astype(jnp.bfloat16)]
    convert_element_type x3 -> x0, local copies, waits for them, and re-layouts: 8.42 us -> none  [the longest x1 8.33 us: local(): input_grad = sum_at_owner((jnp.dot(key_matrix, key_columns, preferred_ele...]
    ppermute x10 -> x21, starting transfers between devices: 23.6 us -> 29.8 us  [the longest x6 15 us: onward(): return lax.ppermute(value, 'seq', shift_pairs(count, steps))]
  transfers between devices with their start and end apart: 11 -> 21, of which waited for: 9 -> 11; matrix products, arithmetic and copies ran while one was open for 7% -> 1% of each run, Pallas kernels for 0% -> 23%
where the time goes in v1:
time: 117 us; the launch traced here: 115 us
  waiting for transfers between devices  48.8 us (42%)
  Pallas kernels  32.2 us (28%)
  starting transfers between devices  29.8 us (25%)
  local copies, waits for them, and re-layouts  2.11 us (2%)
  other arithmetic  1.62 us (1%)
    pallas_call x11, Pallas kernels, vmem_call(): pl.pallas_call(kernel, out_shape=out_shapes, in_specs=in_specs if in_spec...  32.2 us
    ppermute x6, waiting for transfers between devices, local(): arrived.append(lax.ppermute(scaled, 'head', pairs))  20.9 us
    ppermute x6, waiting for transfers between devices, onward(): return lax.ppermute(value, 'seq', shift_pairs(count, steps))  20.1 us
    ppermute x6, starting transfers between devices, onward(): return lax.ppermute(value, 'seq', shift_pairs(count, steps))  15 us
    ppermute x6, starting transfers between devices, local(): arrived.append(lax.ppermute(scaled, 'head', pairs))  8.16 us
    ppermute x3, waiting for transfers between devices, local(): lax.ppermute(piece, 'head', [(at, (at + steps) % groups) for at in range(...  6.29 us
    ppermute x3, starting transfers between devices, local(): lax.ppermute(piece, 'head', [(at, (at + steps) % groups) for at in range(...  5.73 us
  transfers between devices with their start and end apart: 21, of which 11 were waited for; matrix products, arithmetic and copies ran while one was open for 1% of the time, Pallas kernels for 23%

profile of v1, /device:TPU:128, one launch (start us, length us, event | category | flops | bytes accessed | tf_op | source)
XLA Modules:
  0.0 115.4 jit_solution(146776734780169299)
XLA Ops:
  0.6 2.6 %shard_map.95 = (bf16[512,256]{1,0:T(8,128)(2,1)}, bf16[512,256]{1,0:T(8,128)(2,1)}, f32[8,256]{1,0:T(8,128)}) custom-call(s32[2,4]{1,0:T(2,128)} %bitcast.4, s32[2,4]{1,0:T(2,128)} %bitcast.7, bf16[512,256]{1,0:T(8,128)(2,1)} %keys.2, bf16[512,256]{1,0:T(8,128)(2,1)} %values.2), custom_call_target="tpu_custom_call" | custom-call | flops 1 | bytes 1 | tf_op jit(solution)/shard_map/pallas_call | solution.py:31
  3.2 3.5 %collective-permute-start = (bf16[512,256]{1,0:T(8,128)(2,1)}, bf16[512,256]{1,0:T(8,128)(2,1)S(1)}, u32[]{:S(2)}, u32[]{:S(2)}) collective-permute-start(bf16[512,256]{1,0:T(8,128)(2,1)} %get-tuple-element.25.ready.own), channel_id=1, source_target_pairs={{0,8},{4,12},{8,16},{12,20},{16,24},{20,28},{24,32},{28,36},{32,40... | collective-permute-start | bytes 786440 | tf_op jit(solution)/shard_map/ppermute | solution.py:257
  6.7 1.9 %collective-permute-start.1 = (f32[8,256]{1,0:T(8,128)}, f32[8,256]{1,0:T(8,128)S(1)}, u32[]{:S(2)}, u32[]{:S(2)}) collective-permute-start(f32[8,256]{1,0:T(8,128)} %get-tuple-element.30), channel_id=1, source_target_pairs={{0,4},{4,8},{8,12},{12,16},{16,20},{20,24},{24,28},{28,32},{32,36}... | collective-permute-start | bytes 24584 | tf_op jit(solution)/shard_map/ppermute | solution.py:257
  9.3 5.3 %shard_map.96 = (bf16[1344,256]{1,0:T(8,128)(2,1)}, bf16[1344,256]{1,0:T(8,128)(2,1)}, bf16[1344,256]{1,0:T(8,128)(2,1)}, bf16[2,1344,256]{2,1,0:T(8,128)(2,1)},...) custom-call(s32[2]{0:T(128)} %pad_add_fusion.place, bf16[5376,256]{1,0:T(8,128)(2,1)} %keys.3, ...), custom_call_target="tpu_custom_call" | custom-call | flops 1 | bytes 1 | tf_op jit(solution)/shard_map/pallas_call | solution.py:31
  15.7 2.4 %collective-permute-start.3 = (bf16[512,256]{1,0:T(8,128)(2,1)S(1)}, bf16[512,256]{1,0:T(8,128)(2,1)S(1)}, u32[]{:S(2)}, u32[]{:S(2)}) collective-permute-start(bf16[512,256]{1,0:T(8,128)(2,1)S(1)} %copy-done.1), channel_id=1, source_target_pairs={{0,8},{4,12},{8,16},{12,20},{16,24},{20,28},{24,32},{28,36},{32,40... | collective-permute-start | bytes 786440 | tf_op jit(solution)/shard_map/ppermute | solution.py:257
  19.1 3.2 %collective-permute-start.2 = (bf16[512,256]{1,0:T(8,128)(2,1)S(1)}, bf16[512,256]{1,0:T(8,128)(2,1)S(1)}, u32[]{:S(2)}, u32[]{:S(2)}) collective-permute-start(bf16[512,256]{1,0:T(8,128)(2,1)S(1)} %shard_map.97.keys0), channel_id=1, source_target_pairs={{0,8},{4,12},{8,16},{12,20},{16,24},{20,28},{24,32},{28,36},{32,40... | collective-permute-start | bytes 786440 | tf_op jit(solution)/shard_map/ppermute | solution.py:257
  22.3 7.7 %collective-permute-done.3.values2 = bf16[512,256]{1,0:T(8,128)(2,1)S(1)} collective-permute-done((bf16[512,256]{1,0:T(8,128)(2,1)S(1)}, bf16[512,256]{1,0:T(8,128)(2,1)S(1)}, u32[]{:S(2)}, u32[]{:S(2)}) %collective-permute-start.3) | collective-permute-done | bytes 262176 | tf_op jit(solution)/shard_map/ppermute | solution.py:257
  30.0 5.3 %collective-permute-done.2.keys2 = bf16[512,256]{1,0:T(8,128)(2,1)S(1)} collective-permute-done((bf16[512,256]{1,0:T(8,128)(2,1)S(1)}, bf16[512,256]{1,0:T(8,128)(2,1)S(1)}, u32[]{:S(2)}, u32[]{:S(2)}) %collective-permute-start.2) | collective-permute-done | bytes 262176 | tf_op jit(solution)/shard_map/ppermute | solution.py:257
  37.1 2.7 %collective-permute-start.7 = (bf16[1344,256]{1,0:T(8,128)(2,1)}, bf16[1344,256]{1,0:T(8,128)(2,1)S(1)}, u32[]{:S(2)}, u32[]{:S(2)}) collective-permute-start(bf16[1344,256]{1,0:T(8,128)(2,1)} %get-tuple-element.39), channel_id=1, source_target_pairs={{0,2},{1,3},{2,0},{3,1},{4,6},{5,7},{6,4},{7,5},{8,10},{9,11},{10,... | collective-permute-start | bytes 2064392 | tf_op jit(solution)/shard_map/ppermute | solution.py:286
  43.3 7.7 %shard_map.98 = (bf16[512,256]{1,0:T(8,128)(2,1)S(1)}, f32[512,256]{1,0:T(8,128)S(1)}, bf16[512,256]{1,0:T(8,128)(2,1)S(1)}, f32[512,256]{1,0:T(8,128)S(1)}) custom-call(s32[2]{0:T(128)S(1)} %copy-done.5, bf16[512,512]{1,0:T(8,128)(2,1)S(1)} %copy-done.2, bf16[512,512]{1,0:T(8,128)(2,1)S(1)} %copy-done.3, bf16[512,256]{1,0:T(8,128)(2,1)S(1)} %collective-permute-done.2.keys2, ...), custom_call_target="tpu_custom_call" | custom-call | flops 1 | bytes 1 | tf_op jit(solution)/shard_map/pallas_call | solution.py:31
  53.3 2.1 %collective-permute-start.9 = (bf16[512,256]{1,0:T(8,128)(2,1)S(1)}, bf16[512,256]{1,0:T(8,128)(2,1)S(1)}, u32[]{:S(2)}, u32[]{:S(2)}) collective-permute-start(bf16[512,256]{1,0:T(8,128)(2,1)S(1)} %shard_map.99), channel_id=1, source_target_pairs={{8,0},{12,4},{16,8},{20,12},{24,16},{28,20},{32,24},{36,28},{40,32... | collective-permute-start | bytes 786440 | tf_op jit(solution)/shard_map/ppermute | solution.py:257
  55.4 7.7 %shard_map.100 = (bf16[512,256]{1,0:T(8,128)(2,1)S(1)}, f32[512,256]{1,0:T(8,128)S(1)}, bf16[512,256]{1,0:T(8,128)(2,1)S(1)}, f32[512,256]{1,0:T(8,128)S(1)}) custom-call(s32[2]{0:T(128)S(1)} %copy-done.5, bf16[512,512]{1,0:T(8,128)(2,1)S(1)} %copy-done.2, bf16[512,512]{1,0:T(8,128)(2,1)S(1)} %copy-done.3, ...), custom_call_target="tpu_custom_call" | custom-call | flops 1 | bytes 1 | tf_op jit(solution)/shard_map/pallas_call | solution.py:31
  64.2 6.3 %collective-permute-done.7.rest_1_ = bf16[1344,256]{1,0:T(8,128)(2,1)S(1)} collective-permute-done((bf16[1344,256]{1,0:T(8,128)(2,1)}, bf16[1344,256]{1,0:T(8,128)(2,1)S(1)}, u32[]{:S(2)}, u32[]{:S(2)}) %collective-permute-start.7) | collective-permute-done | bytes 688160 | tf_op jit(solution)/shard_map/ppermute | solution.py:286
  71.1 1.9 %collective-permute-start.14 = (bf16[512,256]{1,0:T(8,128)(2,1)S(1)}, bf16[512,256]{1,0:T(8,128)(2,1)S(1)}, u32[]{:S(2)}, u32[]{:S(2)}) collective-permute-start(bf16[512,256]{1,0:T(8,128)(2,1)S(1)} %shard_map.102), channel_id=1, source_target_pairs={{8,0},{12,4},{16,8},{20,12},{24,16},{28,20},{32,24},{36,28},{40,32... | collective-permute-start | bytes 786440 | tf_op jit(solution)/shard_map/ppermute | solution.py:257
  73.1 2.4 %collective-permute-start.20 = (bf16[512,256]{1,0:T(8,128)(2,1)S(1)}, bf16[512,256]{1,0:T(8,128)(2,1)S(1)}, u32[]{:S(2)}, u32[]{:S(2)}) collective-permute-start(bf16[512,256]{1,0:T(8,128)(2,1)S(1)} %shard_map.101.rest_6_), channel_id=1, source_target_pairs={{0,3},{1,0},{2,1},{3,2},{4,7},{5,4},{6,5},{7,6},{8,11},{9,8},{10,9... | collective-permute-start | bytes 786440 | tf_op jit(solution)/shard_map/ppermute | solution.py:338
  75.9 5.8 %collective-permute-done.14.later = bf16[512,256]{1,0:T(8,128)(2,1)S(1)} collective-permute-done((bf16[512,256]{1,0:T(8,128)(2,1)S(1)}, bf16[512,256]{1,0:T(8,128)(2,1)S(1)}, u32[]{:S(2)}, u32[]{:S(2)}) %collective-permute-start.14) | collective-permute-done | bytes 262176 | tf_op jit(solution)/shard_map/ppermute | solution.py:257
  81.8 2.7 %collective-permute-start.19 = (bf16[512,256]{1,0:T(8,128)(2,1)S(1)}, bf16[512,256]{1,0:T(8,128)(2,1)S(1)}, u32[]{:S(2)}, u32[]{:S(2)}) collective-permute-start(bf16[512,256]{1,0:T(8,128)(2,1)S(1)} %shard_map.101.rest_6_), channel_id=1, source_target_pairs={{0,2},{1,3},{2,0},{3,1},{4,6},{5,7},{6,4},{7,5},{8,10},{9,11},{10,... | collective-permute-start | bytes 786440 | tf_op jit(solution)/shard_map/ppermute | solution.py:338
  85.6 6.9 %collective-permute-done.19.rest_8_ = bf16[512,256]{1,0:T(8,128)(2,1)S(1)} collective-permute-done((bf16[512,256]{1,0:T(8,128)(2,1)S(1)}, bf16[512,256]{1,0:T(8,128)(2,1)S(1)}, u32[]{:S(2)}, u32[]{:S(2)}) %collective-permute-start.19) | collective-permute-done | bytes 262176 | tf_op jit(solution)/shard_map/ppermute | solution.py:338
  93.4 3.4 %collective-permute-done.18.rest_7_ = bf16[512,256]{1,0:T(8,128)(2,1)S(1)} collective-permute-done((bf16[512,256]{1,0:T(8,128)(2,1)S(1)}, bf16[512,256]{1,0:T(8,128)(2,1)S(1)}, u32[]{:S(2)}, u32[]{:S(2)}) %collective-permute-start.18) | collective-permute-done | bytes 262176 | tf_op jit(solution)/shard_map/ppermute | solution.py:338
  96.8 1.8 %collective-permute-start.16 = (bf16[512,256]{1,0:T(8,128)(2,1)S(1)}, bf16[512,256]{1,0:T(8,128)(2,1)S(1)}, u32[]{:S(2)}, u32[]{:S(2)}) collective-permute-start(bf16[512,256]{1,0:T(8,128)(2,1)S(1)} %shard_map.103.rest_6_), channel_id=1, source_target_pairs={{0,2},{1,3},{2,0},{3,1},{4,6},{5,7},{6,4},{7,5},{8,10},{9,11},{10,... | collective-permute-start | bytes 786440 | tf_op jit(solution)/shard_map/ppermute | solution.py:338
  99.4 2.2 %shard_map.104.rest_10_ = f32[1344,512]{1,0:T(8,128)S(1)} custom-call(s32[2]{0:T(128)S(1)} %copy-done.5, bf16[2,1344,256]{2,1,0:T(8,128)(2,1)S(1)} %copy-done, bf16[1344,256]{1,0:T(8,128)(2,1)S(1)} %collective-permute-done.6.rest_0_, bf16[1344,256]{1,0:T(8,128)(2,1)S(1)} %collective-permute-done.7.rest_1_, ...), custom_call_target="tpu_custom_call" | custom-call | flops 1 | bytes 1 | tf_op jit(solution)/shard_map/pallas_call | solution.py:31
  101.6 5.9 %collective-permute-done.16.rest_8_ = bf16[512,256]{1,0:T(8,128)(2,1)S(1)} collective-permute-done((bf16[512,256]{1,0:T(8,128)(2,1)S(1)}, bf16[512,256]{1,0:T(8,128)(2,1)S(1)}, u32[]{:S(2)}, u32[]{:S(2)}) %collective-permute-start.16) | collective-permute-done | bytes 262176 | tf_op jit(solution)/shard_map/ppermute | solution.py:338
  107.5 4.6 %collective-permute-done.15.rest_7_ = bf16[512,256]{1,0:T(8,128)(2,1)S(1)} collective-permute-done((bf16[512,256]{1,0:T(8,128)(2,1)S(1)}, bf16[512,256]{1,0:T(8,128)(2,1)S(1)}, u32[]{:S(2)}, u32[]{:S(2)}) %collective-permute-start.15) | collective-permute-done | bytes 262176 | tf_op jit(solution)/shard_map/ppermute | solution.py:338
  112.2 3.2 %shard_map.105 = bf16[1344,512]{1,0:T(8,128)(2,1)} custom-call(s32[2]{0:T(128)S(1)} %copy-done.5, bf16[2,1344,256]{2,1,0:T(8,128)(2,1)S(1)} %copy-done, bf16[1344,256]{1,0:T(8,128)(2,1)S(1)} %collective-permute-done.6.rest_0_, bf16[1344,256]{1,0:T(8,128)(2,1)S(1)} %collective-permute-done.7.rest_1_, bf16[1344,256]{1,0:T(8,128)(2,1)S(1)} %collective-permute-done.8.rest_2_, ...), custom_call_target="tpu_custom_call" | custom-call | flops 1 | bytes 1 | tf_op jit(solution)/shard_map/pallas_call | solution.py:31
  (48 shorter events, 15.5 us)
Async XLA Ops:
  3.2 14.9 %collective-permute-start = (bf16[512,256]{1,0:T(8,128)(2,1)}, bf16[512,256]{1,0:T(8,128)(2,1)S(1)}, u32[]{:S(2)}, u32[]{:S(2)}) collective-permute-start(bf16[512,256]{1,0:T(8,128)(2,1)} %get-tuple-element.25.ready.own), channel_id=1, source_target_pairs={{0,8},{4,12},{8,16},{12,20},{16,24},{20,28},{24,32},{28,36},{32,40... | collective-permute-start | bytes 786440 | tf_op jit(solution)/shard_map/ppermute | solution.py:257
  6.7 9.0 %collective-permute-start.1 = (f32[8,256]{1,0:T(8,128)}, f32[8,256]{1,0:T(8,128)S(1)}, u32[]{:S(2)}, u32[]{:S(2)}) collective-permute-start(f32[8,256]{1,0:T(8,128)} %get-tuple-element.30), channel_id=1, source_target_pairs={{0,4},{4,8},{8,12},{12,16},{16,20},{20,24},{24,28},{28,32},{32,36}... | collective-permute-start | bytes 24584 | tf_op jit(solution)/shard_map/ppermute | solution.py:257
  15.7 14.3 %collective-permute-start.3 = (bf16[512,256]{1,0:T(8,128)(2,1)S(1)}, bf16[512,256]{1,0:T(8,128)(2,1)S(1)}, u32[]{:S(2)}, u32[]{:S(2)}) collective-permute-start(bf16[512,256]{1,0:T(8,128)(2,1)S(1)} %copy-done.1), channel_id=1, source_target_pairs={{0,8},{4,12},{8,16},{12,20},{16,24},{20,28},{24,32},{28,36},{32,40... | collective-permute-start | bytes 786440 | tf_op jit(solution)/shard_map/ppermute | solution.py:257
  19.1 16.2 %collective-permute-start.2 = (bf16[512,256]{1,0:T(8,128)(2,1)S(1)}, bf16[512,256]{1,0:T(8,128)(2,1)S(1)}, u32[]{:S(2)}, u32[]{:S(2)}) collective-permute-start(bf16[512,256]{1,0:T(8,128)(2,1)S(1)} %shard_map.97.keys0), channel_id=1, source_target_pairs={{0,8},{4,12},{8,16},{12,20},{16,24},{20,28},{24,32},{28,36},{32,40... | collective-permute-start | bytes 786440 | tf_op jit(solution)/shard_map/ppermute | solution.py:257
  35.4 5.8 %collective-permute-start.4 = (bf16[512,512]{1,0:T(8,128)(2,1)S(1)}, bf16[512,512]{1,0:T(8,128)(2,1)S(1)}, u32[]{:S(2)}, u32[]{:S(2)}) collective-permute-start(bf16[512,512]{1,0:T(8,128)(2,1)S(1)} %maximum_select_fusion), channel_id=1, source_target_pairs={{0,4},{4,0},{8,12},{12,8},{16,20},{20,16},{24,28},{28,24},{32,36},... | collective-permute-start | bytes 1572872 | tf_op jit(solution)/shard_map/ppermute | solution.py:254
  35.5 28.7 %collective-permute-start.6 = (bf16[1344,256]{1,0:T(8,128)(2,1)}, bf16[1344,256]{1,0:T(8,128)(2,1)S(1)}, u32[]{:S(2)}, u32[]{:S(2)}) collective-permute-start(bf16[1344,256]{1,0:T(8,128)(2,1)} %get-tuple-element.38), channel_id=1, source_target_pairs={{0,1},{1,2},{2,3},{3,0},{4,5},{5,6},{6,7},{7,4},{8,9},{9,10},{10,1... | collective-permute-start | bytes 2064392 | tf_op jit(solution)/shard_map/ppermute | solution.py:286
  37.1 33.4 %collective-permute-start.7 = (bf16[1344,256]{1,0:T(8,128)(2,1)}, bf16[1344,256]{1,0:T(8,128)(2,1)S(1)}, u32[]{:S(2)}, u32[]{:S(2)}) collective-permute-start(bf16[1344,256]{1,0:T(8,128)(2,1)} %get-tuple-element.39), channel_id=1, source_target_pairs={{0,2},{1,3},{2,0},{3,1},{4,6},{5,7},{6,4},{7,5},{8,10},{9,11},{10,... | collective-permute-start | bytes 2064392 | tf_op jit(solution)/shard_map/ppermute | solution.py:286
  39.8 30.7 %collective-permute-start.8 = (bf16[1344,256]{1,0:T(8,128)(2,1)}, bf16[1344,256]{1,0:T(8,128)(2,1)S(1)}, u32[]{:S(2)}, u32[]{:S(2)}) collective-permute-start(bf16[1344,256]{1,0:T(8,128)(2,1)} %get-tuple-element.40), channel_id=1, source_target_pairs={{0,3},{1,0},{2,1},{3,2},{4,7},{5,4},{6,5},{7,6},{8,11},{9,8},{10,9... | collective-permute-start | bytes 2064392 | tf_op jit(solution)/shard_map/ppermute | solution.py:286
  43.3 20.2 %copy-start.6 = (s32[4,2]{0,1:T(2,128)S(1)}, s32[4,2]{0,1:T(2,128)}, u32[]{:S(2)}) copy-start(s32[4,2]{0,1:T(2,128)} %param.12) | copy-start | bytes 100
  43.3 20.2 %copy-start.7 = (s32[4,2]{0,1:T(2,128)S(1)}, s32[4,2]{0,1:T(2,128)}, u32[]{:S(2)}) copy-start(s32[4,2]{0,1:T(2,128)} %param.13) | copy-start | bytes 100
  51.0 1.6 %collective-permute-start.5 = (bf16[512,256]{1,0:T(8,128)(2,1)S(1)}, bf16[512,256]{1,0:T(8,128)(2,1)S(1)}, u32[]{:S(2)}, u32[]{:S(2)}) collective-permute-start(bf16[512,256]{1,0:T(8,128)(2,1)S(1)} %get-tuple-element.35), channel_id=1, source_target_pairs={{0,4},{4,0},{8,12},{12,8},{16,20},{20,16},{24,28},{28,24},{32,36},... | collective-permute-start | bytes 786440 | tf_op jit(solution)/shard_map/ppermute | solution.py:254
  53.3 10.2 %collective-permute-start.9 = (bf16[512,256]{1,0:T(8,128)(2,1)S(1)}, bf16[512,256]{1,0:T(8,128)(2,1)S(1)}, u32[]{:S(2)}, u32[]{:S(2)}) collective-permute-start(bf16[512,256]{1,0:T(8,128)(2,1)S(1)} %shard_map.99), channel_id=1, source_target_pairs={{8,0},{12,4},{16,8},{20,12},{24,16},{28,20},{32,24},{36,28},{40,32... | collective-permute-start | bytes 786440 | tf_op jit(solution)/shard_map/ppermute | solution.py:257
  63.1 36.3 %copy-start = (bf16[2,1344,256]{2,1,0:T(8,128)(2,1)S(1)}, bf16[2,1344,256]{2,1,0:T(8,128)(2,1)}, u32[]{:S(2)}) copy-start(bf16[2,1344,256]{2,1,0:T(8,128)(2,1)} %get-tuple-element.28.own) | copy-start | bytes 4128772
  63.1 7.4 %collective-permute-start.13 = (bf16[512,256]{1,0:T(8,128)(2,1)S(1)}, bf16[512,256]{1,0:T(8,128)(2,1)S(1)}, u32[]{:S(2)}, u32[]{:S(2)}) collective-permute-start(bf16[512,256]{1,0:T(8,128)(2,1)S(1)} %get-tuple-element.46), channel_id=1, source_target_pairs={{0,4},{4,0},{8,12},{12,8},{16,20},{20,16},{24,28},{28,24},{32,36},... | collective-permute-start | bytes 786440 | tf_op jit(solution)/shard_map/ppermute | solution.py:254
  70.5 28.0 %collective-permute-start.10 = (bf16[1344,256]{1,0:T(8,128)(2,1)S(1)}, bf16[1344,256]{1,0:T(8,128)(2,1)S(1)}, u32[]{:S(2)}, u32[]{:S(2)}) collective-permute-start(bf16[1344,256]{1,0:T(8,128)(2,1)S(1)} %collective-permute-done.6.rest_0_), channel_id=1, source_target_pairs={{0,4},{4,0},{8,12},{12,8},{16,20},{20,16},{24,28},{28,24},{32,36},... | collective-permute-start | bytes 2064392 | tf_op jit(solution)/shard_map/ppermute | solution.py:254
  71.1 10.6 %collective-permute-start.14 = (bf16[512,256]{1,0:T(8,128)(2,1)S(1)}, bf16[512,256]{1,0:T(8,128)(2,1)S(1)}, u32[]{:S(2)}, u32[]{:S(2)}) collective-permute-start(bf16[512,256]{1,0:T(8,128)(2,1)S(1)} %shard_map.102), channel_id=1, source_target_pairs={{8,0},{12,4},{16,8},{20,12},{24,16},{28,20},{32,24},{36,28},{40,32... | collective-permute-start | bytes 786440 | tf_op jit(solution)/shard_map/ppermute | solution.py:257
  73.1 11.3 %collective-permute-start.20 = (bf16[512,256]{1,0:T(8,128)(2,1)S(1)}, bf16[512,256]{1,0:T(8,128)(2,1)S(1)}, u32[]{:S(2)}, u32[]{:S(2)}) collective-permute-start(bf16[512,256]{1,0:T(8,128)(2,1)S(1)} %shard_map.101.rest_6_), channel_id=1, source_target_pairs={{0,3},{1,0},{2,1},{3,2},{4,7},{5,4},{6,5},{7,6},{8,11},{9,8},{10,9... | collective-permute-start | bytes 786440 | tf_op jit(solution)/shard_map/ppermute | solution.py:338
  75.4 24.0 %collective-permute-start.11 = (bf16[1344,256]{1,0:T(8,128)(2,1)S(1)}, bf16[1344,256]{1,0:T(8,128)(2,1)S(1)}, u32[]{:S(2)}, u32[]{:S(2)}) collective-permute-start(bf16[1344,256]{1,0:T(8,128)(2,1)S(1)} %collective-permute-done.7.rest_1_), channel_id=1, source_target_pairs={{0,4},{4,0},{8,12},{12,8},{16,20},{20,16},{24,28},{28,24},{32,36},... | collective-permute-start | bytes 2064392 | tf_op jit(solution)/shard_map/ppermute | solution.py:254
  75.6 23.8 %collective-permute-start.12 = (bf16[1344,256]{1,0:T(8,128)(2,1)S(1)}, bf16[1344,256]{1,0:T(8,128)(2,1)S(1)}, u32[]{:S(2)}, u32[]{:S(2)}) collective-permute-start(bf16[1344,256]{1,0:T(8,128)(2,1)S(1)} %collective-permute-done.8.rest_2_), channel_id=1, source_target_pairs={{0,4},{4,0},{8,12},{12,8},{16,20},{20,16},{24,28},{28,24},{32,36},... | collective-permute-start | bytes 2064392 | tf_op jit(solution)/shard_map/ppermute | solution.py:254
  81.8 10.8 %collective-permute-start.19 = (bf16[512,256]{1,0:T(8,128)(2,1)S(1)}, bf16[512,256]{1,0:T(8,128)(2,1)S(1)}, u32[]{:S(2)}, u32[]{:S(2)}) collective-permute-start(bf16[512,256]{1,0:T(8,128)(2,1)S(1)} %shard_map.101.rest_6_), channel_id=1, source_target_pairs={{0,2},{1,3},{2,0},{3,1},{4,6},{5,7},{6,4},{7,5},{8,10},{9,11},{10,... | collective-permute-start | bytes 786440 | tf_op jit(solution)/shard_map/ppermute | solution.py:338
  84.4 12.4 %collective-permute-start.18 = (bf16[512,256]{1,0:T(8,128)(2,1)S(1)}, bf16[512,256]{1,0:T(8,128)(2,1)S(1)}, u32[]{:S(2)}, u32[]{:S(2)}) collective-permute-start(bf16[512,256]{1,0:T(8,128)(2,1)S(1)} %shard_map.101.rest_6_), channel_id=1, source_target_pairs={{0,1},{1,2},{2,3},{3,0},{4,5},{5,6},{6,7},{7,4},{8,9},{9,10},{10,1... | collective-permute-start | bytes 786440 | tf_op jit(solution)/shard_map/ppermute | solution.py:338
  92.5 9.1 %collective-permute-start.17 = (bf16[512,256]{1,0:T(8,128)(2,1)S(1)}, bf16[512,256]{1,0:T(8,128)(2,1)S(1)}, u32[]{:S(2)}, u32[]{:S(2)}) collective-permute-start(bf16[512,256]{1,0:T(8,128)(2,1)S(1)} %shard_map.103.rest_6_), channel_id=1, source_target_pairs={{0,3},{1,0},{2,1},{3,2},{4,7},{5,4},{6,5},{7,6},{8,11},{9,8},{10,9... | collective-permute-start | bytes 786440 | tf_op jit(solution)/shard_map/ppermute | solution.py:338
  96.8 10.7 %collective-permute-start.16 = (bf16[512,256]{1,0:T(8,128)(2,1)S(1)}, bf16[512,256]{1,0:T(8,128)(2,1)S(1)}, u32[]{:S(2)}, u32[]{:S(2)}) collective-permute-start(bf16[512,256]{1,0:T(8,128)(2,1)S(1)} %shard_map.103.rest_6_), channel_id=1, source_target_pairs={{0,2},{1,3},{2,0},{3,1},{4,6},{5,7},{6,4},{7,5},{8,10},{9,11},{10,... | collective-permute-start | bytes 786440 | tf_op jit(solution)/shard_map/ppermute | solution.py:338
  98.6 13.6 %collective-permute-start.15 = (bf16[512,256]{1,0:T(8,128)(2,1)S(1)}, bf16[512,256]{1,0:T(8,128)(2,1)S(1)}, u32[]{:S(2)}, u32[]{:S(2)}) collective-permute-start(bf16[512,256]{1,0:T(8,128)(2,1)S(1)} %shard_map.103.rest_6_), channel_id=1, source_target_pairs={{0,1},{1,2},{2,3},{3,0},{4,5},{5,6},{6,7},{7,4},{8,9},{9,10},{10,1... | collective-permute-start | bytes 786440 | tf_op jit(solution)/shard_map/ppermute | solution.py:338
  (5 other events, 26.2 us)

commit v2 on v1

--- a/solution.py
+++ b/solution.py
@@ -26,7 +26,7 @@
     return lax.dot_general(left, right, dims, preferred_element_type=jnp.float32)
 
 
-def vmem_call(kernel, out_shapes, inputs, in_specs=None, scratch=(), mebibytes=8):
+def vmem_call(kernel, out_shapes, inputs, in_specs=None, scratch=(), mebibytes=8, flops=1):
     whole = pl.BlockSpec(memory_space=pltpu.VMEM)
     return pl.pallas_call(
         kernel,
@@ -34,7 +34,7 @@
         in_specs=in_specs if in_specs is not None else [whole] * len(inputs),
         out_specs=jax.tree.map(lambda _: whole, out_shapes),
         scratch_shapes=list(scratch),
-        cost_estimate=pl.CostEstimate(flops=1, bytes_accessed=1, transcendentals=0),
+        cost_estimate=pl.CostEstimate(flops=flops, bytes_accessed=1, transcendentals=0),
         compiler_params=pltpu.CompilerParams(vmem_limit_bytes=mebibytes * MEBI),
     )(*inputs)
 
@@ -52,11 +52,35 @@
     return jnp.where(exponent > 0, 2.0, jnp.where(exponent < 0, 0.5, 1.0)).astype(jnp.float32)
 
 
-def dequantize_kernel(key_exps, value_exps, keys, values, key_out, value_out, total_out, key_in, value_in, arrivals):
+def identity():
+    row = lax.broadcasted_iota(jnp.int32, (HEAD_SIZE, HEAD_SIZE), 0)
+    column = lax.broadcasted_iota(jnp.int32, (HEAD_SIZE, HEAD_SIZE), 1)
+    return (row == column).astype(jnp.float32).astype(jnp.bfloat16)
+
+
+def front_kernel(
+    index, group, key_exps, value_exps, keys, values, key_matrix, value_matrix,
+    key_out, value_out, total_out, sent1, sent2, sent3,
+    key_in, value_in, rows, arrivals, departures,
+):
     fetch_keys = pltpu.make_async_copy(keys, key_in, arrivals.at[0])
     fetch_values = pltpu.make_async_copy(values, value_in, arrivals.at[1])
     fetch_keys.start()
     fetch_values.start()
+    half = HALF_ROWS
+    core = index[0] & 1
+    incoming, outgoing = [], []
+    for at, (steps, target) in enumerate(((1, sent1), (3, sent3), (2, sent2))):
+        begin = pl.multiple_of(((group[0] + steps) & 3) * (2 * half) + core * half, 16)
+        for part, matrix in enumerate((key_matrix, value_matrix)):
+            incoming.append(
+                pltpu.make_async_copy(
+                    matrix.at[pl.ds(begin, half), :], rows.at[at, pl.ds(part * half, half), :], arrivals.at[2 + 2 * at + part]
+                )
+            )
+        outgoing.append(pltpu.make_async_copy(rows.at[at], target, departures.at[at]))
+    for copy in incoming:
+        copy.start()
     for part, (fetch, source, exponents, target) in enumerate(
         ((fetch_keys, key_in, key_exps, key_out), (fetch_values, value_in, value_exps, value_out))
     ):
@@ -65,13 +89,19 @@
             lanes = slice(head * HEAD_SIZE, (head + 1) * HEAD_SIZE)
             total = jnp.zeros((1, HEAD_SIZE), jnp.float32)
             for block in range(BLOCK // SCALE_BLOCK):
-                rows = slice(block * SCALE_BLOCK, (block + 1) * SCALE_BLOCK)
-                scaled = source[rows, lanes].astype(jnp.float32) * factor_of(exponents[head, block])
-                target[rows, lanes] = scaled.astype(jnp.bfloat16)
+                rows_at = slice(block * SCALE_BLOCK, (block + 1) * SCALE_BLOCK)
+                scaled = source[rows_at, lanes].astype(jnp.float32) * factor_of(exponents[head, block])
+                target[rows_at, lanes] = scaled.astype(jnp.bfloat16)
                 if part == 0:
                     total = total + jnp.sum(scaled, axis=0, keepdims=True)
             if part == 0:
                 total_out[:, lanes] = jnp.broadcast_to(total, (8, HEAD_SIZE))
+    for at in range(3):
+        incoming[2 * at].wait()
+        incoming[2 * at + 1].wait()
+        outgoing[at].start()
+    for copy in outgoing:
+        copy.wait()
 
 
 def smooth_kernel(place, own, older, total, smooth_out):
@@ -87,7 +117,7 @@
 
 
 def attend_kernel(
-    head, place, queries, grads, keys2, last, keys0, values2, values0,
+    head, place, queries, grads, all_grad_cols, keys2, last, keys0, values2, values0,
     query_grad, grad2, grad1, grad0,
     key_rows, value_rows, key_cols, value_cols, weights, shares_out, score_out,
 ):
@@ -99,10 +129,7 @@
         key_rows[at * BLOCK : (at + 1) * BLOCK, :] = source[:, lanes]
     for at, source in enumerate((values2, last, values0)):
         value_rows[at * BLOCK : (at + 1) * BLOCK, :] = source[:, last_lanes if at == 1 else lanes]
-    eye = (
-        lax.broadcasted_iota(jnp.int32, (HEAD_SIZE, HEAD_SIZE), 0)
-        == lax.broadcasted_iota(jnp.int32, (HEAD_SIZE, HEAD_SIZE), 1)
-    ).astype(jnp.float32).astype(jnp.bfloat16)
+    eye = identity()
     key_cols[...] = product(eye, key_rows[...], NT).astype(jnp.bfloat16)
     value_cols[...] = product(eye, value_rows[...], NT).astype(jnp.bfloat16)
     key_at = lax.broadcasted_iota(jnp.int32, (TILE, TILE), 0)
@@ -115,7 +142,7 @@
             columns = slice((2 * head + member) * HEAD_SIZE, (2 * head + member + 1) * HEAD_SIZE)
             query = queries[rows, columns]
             grad = grads[rows, columns]
-            grad_cols = product(eye, grad, NT)
+            grad_cols = all_grad_cols[columns, rows]
             part = 2 * member + tile
             place_at = slice(part * TILE, (part + 1) * TILE)
             valid = [index >= 2, index >= 2, index >= 1, index >= 1, None, None]
@@ -200,40 +227,56 @@
             out[at] = (total * factor_of(exponents[head, block])).astype(jnp.bfloat16)
 
 
-def project_kernel(head, place, own, *rest):
-    mine, other, pieces, out = rest[:3], rest[3:6], rest[6:10], rest[-1]
-    core = place[0] & 1
+def remote_part(place, head, half_at, pieces, mine, other):
     half = HALF_ROWS
     lanes = slice(head * HEAD_SIZE, (head + 1) * HEAD_SIZE)
-    channels = jnp.concatenate([piece[...] for piece in pieces], axis=1)
-    for half_at, matrices in ((core, mine), (1 - core, other)):
-        rows = pl.ds(pl.multiple_of(half_at * half, 16), half)
-        parts = [own[0, rows, lanes], own[1, rows, lanes]]
-        for matrix in matrices:
-            parts += [matrix[0:half, lanes], matrix[half : 2 * half, lanes]]
-        total = product(jnp.concatenate(parts, axis=1), channels, NT)
-        if len(rest) == 12:
-            total = total + rest[10][rows, :]
-        out[rows, :] = total.astype(out.dtype)
-
-
-def fetch_kernel(place, keys, values, queries, grads, ready, sent1, sent2, sent3, own, query_out, grad_out, arrivals):
-    half = HALF_ROWS
+    parts = []
+    for matrix in mine if half_at == 0 else other:
+        parts += [matrix[0:half, lanes], matrix[half : 2 * half, lanes]]
+    return product(jnp.concatenate(parts, axis=1), jnp.concatenate([piece[...] for piece in pieces], axis=1), NT)
+
+
+def half_slice(place, half_at):
     core = place[0] & 1
-    copies = []
-    for steps, target in ((1, sent1), (2, sent2), (3, sent3)):
-        begin = pl.multiple_of(((place[1] + steps) & 3) * (2 * half) + core * half, 16)
-        for part, matrix in enumerate((keys, values)):
-            copies.append((matrix.at[pl.ds(begin, half), :], target.at[pl.ds(part * half, half), :]))
-    begin = pl.multiple_of(place[1] * (2 * half), 16)
-    for part, matrix in enumerate((keys, values)):
-        copies.append((matrix.at[pl.ds(begin, 2 * half), :], own.at[part]))
-    copies += [(queries, query_out), (grads, grad_out)]
-    started = [pltpu.make_async_copy(*pair, arrivals.at[at]) for at, pair in enumerate(copies)]
-    for copy in started:
+    at = core if half_at == 0 else 1 - core
+    return pl.ds(pl.multiple_of(at * HALF_ROWS, 16), HALF_ROWS)
+
+
+def early_kernel(place, group, keys, values, own0, own1, *rest):
+    pieces, mine, other, out, rows, arrivals = rest[:3], rest[3:6], rest[6:9], rest[9], rest[10], rest[11]
+    begin = pl.multiple_of(group[0] * (2 * HALF_ROWS), 16)
+    copies = [
+        pltpu.make_async_copy(matrix.at[pl.ds(begin, 2 * HALF_ROWS), :], rows.at[part], arrivals.at[part])
+        for part, matrix in enumerate((keys, values))
+    ]
+    for copy in copies:
         copy.start()
-    for copy in started:
+    for half_at in range(2):
+        out[half_slice(place, half_at), :] = remote_part(place, 0, half_at, pieces, mine, other)
+    for copy in copies:
         copy.wait()
+    channels = jnp.concatenate(
+        [own0[:, :HEAD_SIZE], own1[:, :HEAD_SIZE], own0[:, HEAD_SIZE:], own1[:, HEAD_SIZE:]], axis=1
+    )
+    for half_at in range(2):
+        at = slice(half_at * HALF_ROWS, (half_at + 1) * HALF_ROWS)
+        out[at, :] += product(jnp.concatenate([rows[0, at, :], rows[1, at, :]], axis=1), channels, NT)
+
+
+def late_kernel(place, early, *rest):
+    pieces, mine, other, out = rest[:3], rest[3:6], rest[6:9], rest[9]
+    for half_at in range(2):
+        rows = half_slice(place, half_at)
+        out[rows, :] = (early[rows, :] + remote_part(place, 1, half_at, pieces, mine, other)).astype(out.dtype)
+
+
+def prepare_kernel(queries, grads, ready, query_out, grad_out, grad_cols):
+    query_out[...] = queries[...]
+    grad_out[...] = grads[...]
+    eye = identity()
+    for head in range(4):
+        lanes = slice(head * HEAD_SIZE, (head + 1) * HEAD_SIZE)
+        grad_cols[lanes, :] = product(eye, grads[:, lanes], NT)
 
 
 def shift_pairs(count, steps):
@@ -246,7 +289,8 @@
     count = lax.axis_size("seq")
     groups = lax.axis_size("head")
     index = lax.axis_index("seq")
-    place = jnp.stack([index, lax.axis_index("head")]).astype(jnp.int32)
+    place = index.astype(jnp.int32).reshape(1)
+    group = lax.axis_index("head").astype(jnp.int32).reshape(1)
     core = index & 1
     siblings = [(at, at ^ 1) for at in range(count)]
 
@@ -257,43 +301,37 @@
         return lax.ppermute(value, "seq", shift_pairs(count, steps))
 
     key_exponents, value_exponents = key_exponents.T, value_exponents.T
-    exact_keys, exact_values, key_total = vmem_call(
-        dequantize_kernel,
-        (shape_of(BLOCK, 256), shape_of(BLOCK, 256), shape_of(8, 256, jnp.float32)),
-        (key_exponents, value_exponents, keys, values),
-        in_specs=[SMEM, SMEM, HBM, HBM],
-        mebibytes=60,
-        scratch=[
+    model_rows = key_matrix.shape[0] // groups
+    piece_shape = shape_of(model_rows, 256)
+    exact_keys, exact_values, key_total, *sent = pl.pallas_call(
+        front_kernel,
+        out_shape=(shape_of(BLOCK, 256), shape_of(BLOCK, 256), shape_of(8, 256, jnp.float32)) + (piece_shape,) * 3,
+        in_specs=[SMEM] * 4 + [HBM] * 4,
+        out_specs=(VMEM,) * 3 + (HBM,) * 3,
+        scratch_shapes=[
             pltpu.VMEM((BLOCK, 256), jnp.bfloat16),
             pltpu.VMEM((BLOCK, 256), jnp.bfloat16),
-            pltpu.SemaphoreType.DMA((2,)),
+            pltpu.VMEM((3, model_rows, 256), jnp.bfloat16),
+            pltpu.SemaphoreType.DMA((8,)),
+            pltpu.SemaphoreType.DMA((3,)),
         ],
-    )
+        cost_estimate=pl.CostEstimate(flops=1, bytes_accessed=1, transcendentals=0),
+        compiler_params=pltpu.CompilerParams(vmem_limit_bytes=59 * MEBI),
+    )(place, group, key_exponents, value_exponents, keys, values, key_matrix, value_matrix)
     older_keys = onward(exact_keys, 2)
     last_total = onward(key_total, 1)
 
-    model_rows = key_matrix.shape[0] // groups
-    piece_shape = shape_of(model_rows, 256)
-    *sent, own, queries, output_gradient = vmem_call(
-        fetch_kernel,
-        (piece_shape, piece_shape, piece_shape, jax.ShapeDtypeStruct((2, model_rows, 256), jnp.bfloat16), shape_of(BLOCK, 512), shape_of(BLOCK, 512)),
-        (place, key_matrix, value_matrix, queries, output_gradient, exact_keys),
-        in_specs=[SMEM] + [HBM] * 4 + [pl.BlockSpec(memory_space=pl.ANY)],
-        scratch=[pltpu.SemaphoreType.DMA((10,))],
-        mebibytes=57,
-    )
-    fetched = [
-        lax.ppermute(piece, "head", [(at, (at + steps) % groups) for at in range(groups)])
-        for steps, piece in zip(range(1, groups), sent)
-    ]
-
-    late_values, _ = lax.optimization_barrier((exact_values, last_total))
-    older_values = onward(late_values, 2)
-    older_keys, _ = lax.optimization_barrier((older_keys, own))
+    def along_head(value, steps):
+        return lax.ppermute(value, "head", [(at, (at + steps) % groups) for at in range(groups)])
+
+
+    older_values = onward(exact_values, 2)
     smooth = vmem_call(
         smooth_kernel, shape_of(BLOCK, 256), (place, exact_keys, older_keys, last_total), in_specs=[SMEM, VMEM, VMEM, VMEM]
     )
     older_smooth = onward(smooth, 2)
+    near, back_near, _ = lax.optimization_barrier((sent[0], sent[2], smooth))
+    fetched = [along_head(near, 1), None, along_head(back_near, 3)]
     last = to_sibling(
         jnp.where(
             core == 0,
@@ -302,15 +340,22 @@
         )
     )
 
+    queries, output_gradient, grad_cols = vmem_call(
+        prepare_kernel,
+        (shape_of(BLOCK, 512), shape_of(BLOCK, 512), shape_of(512, BLOCK, jnp.float32)),
+        (queries, output_gradient, smooth),
+        in_specs=[VMEM, VMEM, pl.BlockSpec(memory_space=pl.ANY)],
+    )
+
     query_grads, gathered = [], []
     for head in range(2):
         if head == 1:
-            queries, _ = lax.optimization_barrier((queries, back))
+            queries, _, swapped[0], swapped[2] = lax.optimization_barrier((queries, back, swapped[0], swapped[2]))
         query_part, grad2, grad1, grad0 = vmem_call(
             functools.partial(attend_kernel, head),
             (shape_of(BLOCK, 256), shape_of(BLOCK, 256, jnp.float32), shape_of(BLOCK, 256), shape_of(BLOCK, 256, jnp.float32)),
-            (place, queries, output_gradient, older_smooth, last, smooth, older_values, exact_values),
-            in_specs=[SMEM] + [VMEM] * 7,
+            (place, queries, output_gradient, grad_cols, older_smooth, last, smooth, older_values, exact_values),
+            in_specs=[SMEM] + [VMEM] * 8,
             scratch=[
                 pltpu.VMEM((WINDOW_ROWS, HEAD_SIZE), jnp.bfloat16),
                 pltpu.VMEM((WINDOW_ROWS, HEAD_SIZE), jnp.bfloat16),
@@ -323,7 +368,13 @@
             mebibytes=18,
         )
         query_grads.append(query_part)
+        if head == 0:
+            fetched[0], fetched[1], fetched[2], _ = lax.optimization_barrier((fetched[0], sent[1], fetched[2], grad1))
+            fetched[1] = along_head(fetched[1], 2)
+            swapped = [to_sibling(fetched[0]), None, to_sibling(fetched[2])]
         sibling_grad = to_sibling(grad1)
+        if head == 1:
+            grad2, _ = lax.optimization_barrier((grad2, gathered[0][0]))
         back = vmem_call(merge_kernel, shape_of(BLOCK, 256), (place, grad2, sibling_grad), in_specs=[SMEM, VMEM, VMEM])
         later_grad = onward(back, -2)
         scaled = vmem_call(
@@ -334,21 +385,25 @@
         )
         arrived = [scaled]
         for steps in (1, 2, 3):
-            pairs = [(at, (at + steps) % groups) for at in range(groups)]
-            arrived.append(lax.ppermute(scaled, "head", pairs))
+            arrived.append(along_head(scaled, steps))
         gathered.append(arrived)
-    fetched = lax.optimization_barrier((*fetched, gathered[0][0]))[:-1]
-    swapped = [to_sibling(piece) for piece in fetched]
-    input_grad = None
-    for head in range(2):
-        more = () if input_grad is None else (input_grad,)
-        input_grad = vmem_call(
-            functools.partial(project_kernel, head),
-            shape_of(model_rows, BLOCK, jnp.bfloat16 if head else jnp.float32),
-            (place, own, *fetched, *swapped, *gathered[head], *more),
-            in_specs=[SMEM] + [VMEM] * (11 + len(more)),
-            mebibytes=18,
-        )
+    fetched[1], _ = lax.optimization_barrier((fetched[1], back))
+    swapped[1] = to_sibling(fetched[1])
+    early = vmem_call(
+        early_kernel,
+        shape_of(model_rows, BLOCK, jnp.float32),
+        (place, group, key_matrix, value_matrix, gathered[0][0], gathered[1][0], *gathered[0][1:], *fetched, *swapped),
+        in_specs=[SMEM, SMEM, HBM, HBM] + [VMEM] * 11,
+        scratch=[pltpu.VMEM((2, model_rows, 256), jnp.bfloat16), pltpu.SemaphoreType.DMA((2,))],
+        mebibytes=18,
+    )
+    input_grad = vmem_call(
+        late_kernel,
+        shape_of(model_rows, BLOCK),
+        (place, early, *gathered[1][1:], *fetched, *swapped),
+        in_specs=[SMEM] + [VMEM] * 10,
+        mebibytes=18,
+    )
     return jnp.concatenate(query_grads, axis=1), input_grad
 
 

time: 117 us -> 96.5 us (0.82); the launches traced: 115 us -> 96.2 us
  waiting for transfers between devices: 48.8 us -> 31.8 us
  Pallas kernels: 32.2 us -> 25.6 us
  starting transfers between devices: 29.8 us -> 34.9 us
    ppermute x9, waiting for transfers between devices: 27.2 us -> 15.1 us  [along_head(): lax.ppermute(value, 'head', [(at, (at + steps) % groups) for at in range(...]
    pallas_call x11 -> x10, Pallas kernels: 32.2 us -> 21.4 us  [vmem_call(): pl.pallas_call(kernel, out_shape=out_shapes, in_specs=in_specs if in_spec...]
    ppermute x6, waiting for transfers between devices: 20.1 us -> 12.9 us  [onward(): return lax.ppermute(value, 'seq', shift_pairs(count, steps))]
    pallas_call x0 -> x1, Pallas kernels: none -> 4.27 us  [local(): pl.pallas_call(front_kernel, out_shape=(shape_of(BLOCK, 256), shape_of(BL...]
    ppermute x6, starting transfers between devices: 15 us -> 19.1 us  [onward(): return lax.ppermute(value, 'seq', shift_pairs(count, steps))]
    ppermute x6, waiting for transfers between devices: 1.54 us -> 3.84 us  [to_sibling(): return lax.ppermute(value, 'seq', siblings)]
  transfers between devices with their start and end apart: 21 -> 21, of which waited for: 11 -> 12; matrix products, arithmetic and copies ran while one was open for 1% -> 2% of each run, Pallas kernels for 23% -> 20%
where the time goes in v2:
time: 96.5 us; the launch traced here: 96.2 us
  starting transfers between devices  34.9 us (36%)
  waiting for transfers between devices  31.8 us (33%)
  Pallas kernels  25.6 us (27%)
  other arithmetic  1.91 us (2%)
  local copies, waits for them, and re-layouts  0.99 us (1%)
    pallas_call x10, Pallas kernels, vmem_call(): pl.pallas_call(kernel, out_shape=out_shapes, in_specs=in_specs if in_spec...  21.4 us
    ppermute x6, starting transfers between devices, onward(): return lax.ppermute(value, 'seq', shift_pairs(count, steps))  19.1 us
    ppermute x9, waiting for transfers between devices, along_head(): lax.ppermute(value, 'head', [(at, (at + steps) % groups) for at in range(...  15.1 us
    ppermute x9, starting transfers between devices, along_head(): lax.ppermute(value, 'head', [(at, (at + steps) % groups) for at in range(...  15 us
    ppermute x6, waiting for transfers between devices, onward(): return lax.ppermute(value, 'seq', shift_pairs(count, steps))  12.9 us
    pallas_call x1, Pallas kernels, local(): pl.pallas_call(front_kernel, out_shape=(shape_of(BLOCK, 256), shape_of(BL...  4.27 us
    ppermute x6, waiting for transfers between devices, to_sibling(): return lax.ppermute(value, 'seq', siblings)  3.84 us
  transfers between devices with their start and end apart: 21, of which 12 were waited for; matrix products, arithmetic and copies ran while one was open for 2% of the time, Pallas kernels for 20%

profile of v2, /device:TPU:128, one launch (start us, length us, event | category | flops | bytes accessed | tf_op | source)
XLA Modules:
  0.0 96.2 jit_solution(8470086799317288192)
XLA Ops:
  0.7 4.3 %shard_map.95 = (bf16[512,256]{1,0:T(8,128)(2,1)}, bf16[512,256]{1,0:T(8,128)(2,1)}, f32[8,256]{1,0:T(8,128)}, bf16[1344,256]{1,0:T(8,128)(2,1)}, bf16[1344,256]{1,0:T(8,128)(2,1)}, /*index=5*/bf16[1344,256]{1,0:T(8,128)(2,1)}) custom-call(s32[1]{0:T(128)} %bitcast.index.place, s32[1]{0:T(128)} %bitcast.1.group, s32[2,4]{1,0:T(2,128)} %bitcast.4, ...), custom_call_target="tpu_custom_call" | custom-call | flops 1 | bytes 1 | tf_op jit(solution)/shard_map/pallas_call | solution.py:306
  4.9 3.6 %collective-permute-start = (bf16[512,256]{1,0:T(8,128)(2,1)}, bf16[512,256]{1,0:T(8,128)(2,1)S(1)}, u32[]{:S(2)}, u32[]{:S(2)}) collective-permute-start(bf16[512,256]{1,0:T(8,128)(2,1)} %get-tuple-element.29.own), channel_id=1, source_target_pairs={{0,8},{4,12},{8,16},{12,20},{16,24},{20,28},{24,32},{28,36},{32,40... | collective-permute-start | bytes 786440 | tf_op jit(solution)/shard_map/ppermute | solution.py:301
  8.6 1.9 %collective-permute-start.1 = (f32[8,256]{1,0:T(8,128)}, f32[8,256]{1,0:T(8,128)S(1)}, u32[]{:S(2)}, u32[]{:S(2)}) collective-permute-start(f32[8,256]{1,0:T(8,128)} %get-tuple-element.30), channel_id=1, source_target_pairs={{0,4},{4,8},{8,12},{12,16},{16,20},{20,24},{24,28},{28,32},{32,36}... | collective-permute-start | bytes 24584 | tf_op jit(solution)/shard_map/ppermute | solution.py:301
  10.5 3.5 %collective-permute-start.3 = (bf16[512,256]{1,0:T(8,128)(2,1)}, bf16[512,256]{1,0:T(8,128)(2,1)S(1)}, u32[]{:S(2)}, u32[]{:S(2)}) collective-permute-start(bf16[512,256]{1,0:T(8,128)(2,1)} %get-tuple-element.34.values0), channel_id=1, source_target_pairs={{0,8},{4,12},{8,16},{12,20},{16,24},{20,28},{24,32},{28,36},{32,40... | collective-permute-start | bytes 786440 | tf_op jit(solution)/shard_map/ppermute | solution.py:301
  14.0 3.6 %collective-permute-done.1.total = f32[8,256]{1,0:T(8,128)S(1)} collective-permute-done((f32[8,256]{1,0:T(8,128)}, f32[8,256]{1,0:T(8,128)S(1)}, u32[]{:S(2)}, u32[]{:S(2)}) %collective-permute-start.1) | collective-permute-done | bytes 8224 | tf_op jit(solution)/shard_map/ppermute | solution.py:301
  20.0 1.9 %collective-permute-start.2 = (bf16[512,256]{1,0:T(8,128)(2,1)S(1)}, bf16[512,256]{1,0:T(8,128)(2,1)S(1)}, u32[]{:S(2)}, u32[]{:S(2)}) collective-permute-start(bf16[512,256]{1,0:T(8,128)(2,1)S(1)} %shard_map.96.ready.keys0), channel_id=1, source_target_pairs={{0,8},{4,12},{8,16},{12,20},{16,24},{20,28},{24,32},{28,36},{32,40... | collective-permute-start | bytes 786440 | tf_op jit(solution)/shard_map/ppermute | solution.py:301
  22.0 1.6 %collective-permute-start.6 = (bf16[1344,256]{1,0:T(8,128)(2,1)}, bf16[1344,256]{1,0:T(8,128)(2,1)S(1)}, u32[]{:S(2)}, u32[]{:S(2)}) collective-permute-start(bf16[1344,256]{1,0:T(8,128)(2,1)} %get-tuple-element.40), channel_id=1, source_target_pairs={{0,1},{1,2},{2,3},{3,0},{4,5},{5,6},{6,7},{7,4},{8,9},{9,10},{10,1... | collective-permute-start | bytes 2064392 | tf_op jit(solution)/shard_map/ppermute | solution.py:325
  23.5 1.7 %collective-permute-start.7 = (bf16[1344,256]{1,0:T(8,128)(2,1)}, bf16[1344,256]{1,0:T(8,128)(2,1)S(1)}, u32[]{:S(2)}, u32[]{:S(2)}) collective-permute-start(bf16[1344,256]{1,0:T(8,128)(2,1)} %get-tuple-element.42), channel_id=1, source_target_pairs={{0,3},{1,0},{2,1},{3,2},{4,7},{5,4},{6,5},{7,6},{8,11},{9,8},{10,9... | collective-permute-start | bytes 2064392 | tf_op jit(solution)/shard_map/ppermute | solution.py:325
  25.3 7.1 %collective-permute-done.2.keys2 = bf16[512,256]{1,0:T(8,128)(2,1)S(1)} collective-permute-done((bf16[512,256]{1,0:T(8,128)(2,1)S(1)}, bf16[512,256]{1,0:T(8,128)(2,1)S(1)}, u32[]{:S(2)}, u32[]{:S(2)}) %collective-permute-start.2) | collective-permute-done | bytes 262176 | tf_op jit(solution)/shard_map/ppermute | solution.py:301
  33.9 1.5 %collective-permute-done.4.last = bf16[512,512]{1,0:T(8,128)(2,1)S(1)} collective-permute-done((bf16[512,512]{1,0:T(8,128)(2,1)S(1)}, bf16[512,512]{1,0:T(8,128)(2,1)S(1)}, u32[]{:S(2)}, u32[]{:S(2)}) %collective-permute-start.4) | collective-permute-done | bytes 524320 | tf_op jit(solution)/shard_map/ppermute | solution.py:298
  35.4 7.0 %shard_map.98 = (bf16[512,256]{1,0:T(8,128)(2,1)S(1)}, f32[512,256]{1,0:T(8,128)S(1)}, bf16[512,256]{1,0:T(8,128)(2,1)S(1)}, f32[512,256]{1,0:T(8,128)S(1)}) custom-call(s32[1]{0:T(128)} %bitcast.index.place, bf16[512,512]{1,0:T(8,128)(2,1)S(1)} %get-tuple-element.45.queries, bf16[512,512]{1,0:T(8,128)(2,1)S(1)} %get-tuple-element.32.grads, ...), custom_call_target="tpu_custom_call" | custom-call | flops 1 | bytes 1 | tf_op jit(solution)/shard_map/pallas_call | solution.py:31
  43.0 3.0 %collective-permute-start.16 = (bf16[1344,256]{1,0:T(8,128)(2,1)S(1)}, bf16[1344,256]{1,0:T(8,128)(2,1)S(1)}, u32[]{:S(2)}, u32[]{:S(2)}) collective-permute-start(bf16[1344,256]{1,0:T(8,128)(2,1)S(1)} %copy-done.8), channel_id=1, source_target_pairs={{0,2},{1,3},{2,0},{3,1},{4,6},{5,7},{6,4},{7,5},{8,10},{9,11},{10,... | collective-permute-start | bytes 2064392 | tf_op jit(solution)/shard_map/ppermute | solution.py:325
  46.1 1.5 %collective-permute-done.5.arrived.sibling = bf16[512,256]{1,0:T(8,128)(2,1)S(1)} collective-permute-done((bf16[512,256]{1,0:T(8,128)(2,1)S(1)}, bf16[512,256]{1,0:T(8,128)(2,1)S(1)}, u32[]{:S(2)}, u32[]{:S(2)}) %collective-permute-start.5) | collective-permute-done | bytes 262176 | tf_op jit(solution)/shard_map/ppermute | solution.py:298
  47.7 4.0 %collective-permute-start.10 = (bf16[512,256]{1,0:T(8,128)(2,1)S(1)}, bf16[512,256]{1,0:T(8,128)(2,1)S(1)}, u32[]{:S(2)}, u32[]{:S(2)}) collective-permute-start(bf16[512,256]{1,0:T(8,128)(2,1)S(1)} %shard_map.99), channel_id=1, source_target_pairs={{8,0},{12,4},{16,8},{20,12},{24,16},{28,20},{32,24},{36,28},{40,32... | collective-permute-start | bytes 786440 | tf_op jit(solution)/shard_map/ppermute | solution.py:301
  51.7 7.0 %shard_map.100 = (bf16[512,256]{1,0:T(8,128)(2,1)S(1)}, f32[512,256]{1,0:T(8,128)S(1)}, bf16[512,256]{1,0:T(8,128)(2,1)S(1)}, f32[512,256]{1,0:T(8,128)S(1)}) custom-call(s32[1]{0:T(128)} %bitcast.index.place, bf16[512,512]{1,0:T(8,128)(2,1)S(1)} %get-tuple-element.45.queries, bf16[512,512]{1,0:T(8,128)(2,1)S(1)} %get-tuple-element.32.grads, ...), custom_call_target="tpu_custom_call" | custom-call | flops 1 | bytes 1 | tf_op jit(solution)/shard_map/pallas_call | solution.py:31
  60.4 1.6 %collective-permute-done.16.rest_4_ = bf16[1344,256]{1,0:T(8,128)(2,1)S(1)} collective-permute-done((bf16[1344,256]{1,0:T(8,128)(2,1)S(1)}, bf16[1344,256]{1,0:T(8,128)(2,1)S(1)}, u32[]{:S(2)}, u32[]{:S(2)}) %collective-permute-start.16) | collective-permute-done | bytes 688160 | tf_op jit(solution)/shard_map/ppermute | solution.py:325
  62.0 4.1 %collective-permute-start.12 = (bf16[512,256]{1,0:T(8,128)(2,1)S(1)}, bf16[512,256]{1,0:T(8,128)(2,1)S(1)}, u32[]{:S(2)}, u32[]{:S(2)}) collective-permute-start(bf16[512,256]{1,0:T(8,128)(2,1)S(1)} %shard_map.102), channel_id=1, source_target_pairs={{8,0},{12,4},{16,8},{20,12},{24,16},{28,20},{32,24},{36,28},{40,32... | collective-permute-start | bytes 786440 | tf_op jit(solution)/shard_map/ppermute | solution.py:301
  67.6 2.9 %collective-permute-start.14 = (bf16[512,256]{1,0:T(8,128)(2,1)S(1)}, bf16[512,256]{1,0:T(8,128)(2,1)S(1)}, u32[]{:S(2)}, u32[]{:S(2)}) collective-permute-start(bf16[512,256]{1,0:T(8,128)(2,1)S(1)} %shard_map.101.own0), channel_id=1, source_target_pairs={{0,2},{1,3},{2,0},{3,1},{4,6},{5,7},{6,4},{7,5},{8,10},{9,11},{10,... | collective-permute-start | bytes 786440 | tf_op jit(solution)/shard_map/ppermute | solution.py:325
  73.3 1.6 %collective-permute-start.18 = (bf16[512,256]{1,0:T(8,128)(2,1)S(1)}, bf16[512,256]{1,0:T(8,128)(2,1)S(1)}, u32[]{:S(2)}, u32[]{:S(2)}) collective-permute-start(bf16[512,256]{1,0:T(8,128)(2,1)S(1)} %shard_map.103.own1), channel_id=1, source_target_pairs={{0,1},{1,2},{2,3},{3,0},{4,5},{5,6},{6,7},{7,4},{8,9},{9,10},{10,1... | collective-permute-start | bytes 786440 | tf_op jit(solution)/shard_map/ppermute | solution.py:325
  75.9 1.8 %collective-permute-start.19 = (bf16[512,256]{1,0:T(8,128)(2,1)S(1)}, bf16[512,256]{1,0:T(8,128)(2,1)S(1)}, u32[]{:S(2)}, u32[]{:S(2)}) collective-permute-start(bf16[512,256]{1,0:T(8,128)(2,1)S(1)} %shard_map.103.own1), channel_id=1, source_target_pairs={{0,2},{1,3},{2,0},{3,1},{4,6},{5,7},{6,4},{7,5},{8,10},{9,11},{10,... | collective-permute-start | bytes 786440 | tf_op jit(solution)/shard_map/ppermute | solution.py:325
  77.7 5.6 %collective-permute-done.14.rest_1_ = bf16[512,256]{1,0:T(8,128)(2,1)S(1)} collective-permute-done((bf16[512,256]{1,0:T(8,128)(2,1)S(1)}, bf16[512,256]{1,0:T(8,128)(2,1)S(1)}, u32[]{:S(2)}, u32[]{:S(2)}) %collective-permute-start.14) | collective-permute-done | bytes 262176 | tf_op jit(solution)/shard_map/ppermute | solution.py:325
  84.1 2.7 %shard_map.104.early = f32[1344,512]{1,0:T(8,128)S(1)} custom-call(s32[1]{0:T(128)} %bitcast.index.place, s32[1]{0:T(128)} %bitcast.1.group, bf16[5376,256]{1,0:T(8,128)(2,1)S(1)} %copy-done, bf16[5376,256]{1,0:T(8,128)(2,1)S(1)} %copy-done.1, bf16[512,256]{1,0:T(8,128)(2,1)S(1)} %shard_map.101.own0, bf16[512,256]{1,0:T(8,128)(2,1)S(1)} %shard_map.103.own1, ...), custom_call_target="tpu_custom_call" | custom-call | flops 1 | bytes 1 | tf_op jit(solution)/shard_map/pallas_call | solution.py:31
  88.1 5.7 %collective-permute-done.19.rest_1_ = bf16[512,256]{1,0:T(8,128)(2,1)S(1)} collective-permute-done((bf16[512,256]{1,0:T(8,128)(2,1)S(1)}, bf16[512,256]{1,0:T(8,128)(2,1)S(1)}, u32[]{:S(2)}, u32[]{:S(2)}) %collective-permute-start.19) | collective-permute-done | bytes 262176 | tf_op jit(solution)/shard_map/ppermute | solution.py:325
  93.8 2.4 %shard_map.105 = bf16[1344,512]{1,0:T(8,128)(2,1)} custom-call(s32[1]{0:T(128)} %bitcast.index.place, f32[1344,512]{1,0:T(8,128)S(1)} %shard_map.104.early, bf16[512,256]{1,0:T(8,128)(2,1)S(1)} %collective-permute-done.18.rest_0_, bf16[512,256]{1,0:T(8,128)(2,1)S(1)} %collective-permute-done.19.rest_1_, ...), custom_call_target="tpu_custom_call" | custom-call | flops 1 | bytes 1 | tf_op jit(solution)/shard_map/pallas_call | solution.py:31
  (49 shorter events, 13.7 us)
Async XLA Ops:
  0.6 32.9 %copy-start.3 = (bf16[512,512]{1,0:T(8,128)(2,1)S(1)}, bf16[512,512]{1,0:T(8,128)(2,1)}, u32[]{:S(2)}) copy-start(bf16[512,512]{1,0:T(8,128)(2,1)} %queries.1) | copy-start | bytes 1572868
  0.6 32.9 %copy-start.4 = (bf16[512,512]{1,0:T(8,128)(2,1)S(1)}, bf16[512,512]{1,0:T(8,128)(2,1)}, u32[]{:S(2)}) copy-start(bf16[512,512]{1,0:T(8,128)(2,1)} %grads.1) | copy-start | bytes 1572868
  4.9 13.7 %collective-permute-start = (bf16[512,256]{1,0:T(8,128)(2,1)}, bf16[512,256]{1,0:T(8,128)(2,1)S(1)}, u32[]{:S(2)}, u32[]{:S(2)}) collective-permute-start(bf16[512,256]{1,0:T(8,128)(2,1)} %get-tuple-element.29.own), channel_id=1, source_target_pairs={{0,8},{4,12},{8,16},{12,20},{16,24},{20,28},{24,32},{28,36},{32,40... | collective-permute-start | bytes 786440 | tf_op jit(solution)/shard_map/ppermute | solution.py:301
  8.6 9.0 %collective-permute-start.1 = (f32[8,256]{1,0:T(8,128)}, f32[8,256]{1,0:T(8,128)S(1)}, u32[]{:S(2)}, u32[]{:S(2)}) collective-permute-start(f32[8,256]{1,0:T(8,128)} %get-tuple-element.30), channel_id=1, source_target_pairs={{0,4},{4,8},{8,12},{12,16},{16,20},{20,24},{24,28},{28,32},{32,36}... | collective-permute-start | bytes 24584 | tf_op jit(solution)/shard_map/ppermute | solution.py:301
  10.5 14.8 %collective-permute-start.3 = (bf16[512,256]{1,0:T(8,128)(2,1)}, bf16[512,256]{1,0:T(8,128)(2,1)S(1)}, u32[]{:S(2)}, u32[]{:S(2)}) collective-permute-start(bf16[512,256]{1,0:T(8,128)(2,1)} %get-tuple-element.34.values0), channel_id=1, source_target_pairs={{0,8},{4,12},{8,16},{12,20},{16,24},{20,28},{24,32},{28,36},{32,40... | collective-permute-start | bytes 786440 | tf_op jit(solution)/shard_map/ppermute | solution.py:301
  20.0 12.3 %collective-permute-start.2 = (bf16[512,256]{1,0:T(8,128)(2,1)S(1)}, bf16[512,256]{1,0:T(8,128)(2,1)S(1)}, u32[]{:S(2)}, u32[]{:S(2)}) collective-permute-start(bf16[512,256]{1,0:T(8,128)(2,1)S(1)} %shard_map.96.ready.keys0), channel_id=1, source_target_pairs={{0,8},{4,12},{8,16},{12,20},{16,24},{20,28},{24,32},{28,36},{32,40... | collective-permute-start | bytes 786440 | tf_op jit(solution)/shard_map/ppermute | solution.py:301
  22.0 20.5 %collective-permute-start.6 = (bf16[1344,256]{1,0:T(8,128)(2,1)}, bf16[1344,256]{1,0:T(8,128)(2,1)S(1)}, u32[]{:S(2)}, u32[]{:S(2)}) collective-permute-start(bf16[1344,256]{1,0:T(8,128)(2,1)} %get-tuple-element.40), channel_id=1, source_target_pairs={{0,1},{1,2},{2,3},{3,0},{4,5},{5,6},{6,7},{7,4},{8,9},{9,10},{10,1... | collective-permute-start | bytes 2064392 | tf_op jit(solution)/shard_map/ppermute | solution.py:325
  23.5 18.9 %collective-permute-start.7 = (bf16[1344,256]{1,0:T(8,128)(2,1)}, bf16[1344,256]{1,0:T(8,128)(2,1)S(1)}, u32[]{:S(2)}, u32[]{:S(2)}) collective-permute-start(bf16[1344,256]{1,0:T(8,128)(2,1)} %get-tuple-element.42), channel_id=1, source_target_pairs={{0,3},{1,0},{2,1},{3,2},{4,7},{5,4},{6,5},{7,6},{8,11},{9,8},{10,9... | collective-permute-start | bytes 2064392 | tf_op jit(solution)/shard_map/ppermute | solution.py:325
  33.4 2.0 %collective-permute-start.4 = (bf16[512,512]{1,0:T(8,128)(2,1)S(1)}, bf16[512,512]{1,0:T(8,128)(2,1)S(1)}, u32[]{:S(2)}, u32[]{:S(2)}) collective-permute-start(bf16[512,512]{1,0:T(8,128)(2,1)S(1)} %maximum_select_fusion), channel_id=1, source_target_pairs={{0,4},{4,0},{8,12},{12,8},{16,20},{20,16},{24,28},{28,24},{32,36},... | collective-permute-start | bytes 1572872 | tf_op jit(solution)/shard_map/ppermute | solution.py:298
  42.4 9.3 %collective-permute-start.8 = (bf16[1344,256]{1,0:T(8,128)(2,1)S(1)}, bf16[1344,256]{1,0:T(8,128)(2,1)S(1)}, u32[]{:S(2)}, u32[]{:S(2)}) collective-permute-start(bf16[1344,256]{1,0:T(8,128)(2,1)S(1)} %collective-permute-done.6.rest_3_), channel_id=1, source_target_pairs={{0,4},{4,0},{8,12},{12,8},{16,20},{20,16},{24,28},{28,24},{32,36},... | collective-permute-start | bytes 2064392 | tf_op jit(solution)/shard_map/ppermute | solution.py:298
  42.7 9.0 %collective-permute-start.9 = (bf16[1344,256]{1,0:T(8,128)(2,1)S(1)}, bf16[1344,256]{1,0:T(8,128)(2,1)S(1)}, u32[]{:S(2)}, u32[]{:S(2)}) collective-permute-start(bf16[1344,256]{1,0:T(8,128)(2,1)S(1)} %collective-permute-done.7.rest_5_), channel_id=1, source_target_pairs={{0,4},{4,0},{8,12},{12,8},{16,20},{20,16},{24,28},{28,24},{32,36},... | collective-permute-start | bytes 2064392 | tf_op jit(solution)/shard_map/ppermute | solution.py:298
  43.0 19.0 %collective-permute-start.16 = (bf16[1344,256]{1,0:T(8,128)(2,1)S(1)}, bf16[1344,256]{1,0:T(8,128)(2,1)S(1)}, u32[]{:S(2)}, u32[]{:S(2)}) collective-permute-start(bf16[1344,256]{1,0:T(8,128)(2,1)S(1)} %copy-done.8), channel_id=1, source_target_pairs={{0,2},{1,3},{2,0},{3,1},{4,6},{5,7},{6,4},{7,5},{8,10},{9,11},{10,... | collective-permute-start | bytes 2064392 | tf_op jit(solution)/shard_map/ppermute | solution.py:325
  46.1 1.5 %collective-permute-start.5 = (bf16[512,256]{1,0:T(8,128)(2,1)S(1)}, bf16[512,256]{1,0:T(8,128)(2,1)S(1)}, u32[]{:S(2)}, u32[]{:S(2)}) collective-permute-start(bf16[512,256]{1,0:T(8,128)(2,1)S(1)} %get-tuple-element.37), channel_id=1, source_target_pairs={{0,4},{4,0},{8,12},{12,8},{16,20},{20,16},{24,28},{28,24},{32,36},... | collective-permute-start | bytes 786440 | tf_op jit(solution)/shard_map/ppermute | solution.py:298
  47.7 11.1 %collective-permute-start.10 = (bf16[512,256]{1,0:T(8,128)(2,1)S(1)}, bf16[512,256]{1,0:T(8,128)(2,1)S(1)}, u32[]{:S(2)}, u32[]{:S(2)}) collective-permute-start(bf16[512,256]{1,0:T(8,128)(2,1)S(1)} %shard_map.99), channel_id=1, source_target_pairs={{8,0},{12,4},{16,8},{20,12},{24,16},{28,20},{32,24},{36,28},{40,32... | collective-permute-start | bytes 786440 | tf_op jit(solution)/shard_map/ppermute | solution.py:301
  51.7 32.4 %copy-start.1 = (bf16[5376,256]{1,0:T(8,128)(2,1)S(1)}, bf16[5376,256]{1,0:T(8,128)(2,1)}, u32[]{:S(2)}) copy-start(bf16[5376,256]{1,0:T(8,128)(2,1)} %values.3) | copy-start | bytes 8257540
  58.7 1.6 %collective-permute-start.11 = (bf16[512,256]{1,0:T(8,128)(2,1)S(1)}, bf16[512,256]{1,0:T(8,128)(2,1)S(1)}, u32[]{:S(2)}, u32[]{:S(2)}) collective-permute-start(bf16[512,256]{1,0:T(8,128)(2,1)S(1)} %get-tuple-element.49), channel_id=1, source_target_pairs={{0,4},{4,0},{8,12},{12,8},{16,20},{20,16},{24,28},{28,24},{32,36},... | collective-permute-start | bytes 786440 | tf_op jit(solution)/shard_map/ppermute | solution.py:298
  62.0 22.1 %collective-permute-start.17 = (bf16[1344,256]{1,0:T(8,128)(2,1)S(1)}, bf16[1344,256]{1,0:T(8,128)(2,1)S(1)}, u32[]{:S(2)}, u32[]{:S(2)}) collective-permute-start(bf16[1344,256]{1,0:T(8,128)(2,1)S(1)} %collective-permute-done.16.rest_4_), channel_id=1, source_target_pairs={{0,4},{4,0},{8,12},{12,8},{16,20},{20,16},{24,28},{28,24},{32,36},... | collective-permute-start | bytes 2064392 | tf_op jit(solution)/shard_map/ppermute | solution.py:298
  62.0 10.6 %collective-permute-start.12 = (bf16[512,256]{1,0:T(8,128)(2,1)S(1)}, bf16[512,256]{1,0:T(8,128)(2,1)S(1)}, u32[]{:S(2)}, u32[]{:S(2)}) collective-permute-start(bf16[512,256]{1,0:T(8,128)(2,1)S(1)} %shard_map.102), channel_id=1, source_target_pairs={{8,0},{12,4},{16,8},{20,12},{24,16},{28,20},{32,24},{36,28},{40,32... | collective-permute-start | bytes 786440 | tf_op jit(solution)/shard_map/ppermute | solution.py:301
  66.2 9.7 %collective-permute-start.13 = (bf16[512,256]{1,0:T(8,128)(2,1)S(1)}, bf16[512,256]{1,0:T(8,128)(2,1)S(1)}, u32[]{:S(2)}, u32[]{:S(2)}) collective-permute-start(bf16[512,256]{1,0:T(8,128)(2,1)S(1)} %shard_map.101.own0), channel_id=1, source_target_pairs={{0,1},{1,2},{2,3},{3,0},{4,5},{5,6},{6,7},{7,4},{8,9},{9,10},{10,1... | collective-permute-start | bytes 786440 | tf_op jit(solution)/shard_map/ppermute | solution.py:325
  67.6 15.7 %collective-permute-start.14 = (bf16[512,256]{1,0:T(8,128)(2,1)S(1)}, bf16[512,256]{1,0:T(8,128)(2,1)S(1)}, u32[]{:S(2)}, u32[]{:S(2)}) collective-permute-start(bf16[512,256]{1,0:T(8,128)(2,1)S(1)} %shard_map.101.own0), channel_id=1, source_target_pairs={{0,2},{1,3},{2,0},{3,1},{4,6},{5,7},{6,4},{7,5},{8,10},{9,11},{10,... | collective-permute-start | bytes 786440 | tf_op jit(solution)/shard_map/ppermute | solution.py:325
  70.5 13.6 %collective-permute-start.15 = (bf16[512,256]{1,0:T(8,128)(2,1)S(1)}, bf16[512,256]{1,0:T(8,128)(2,1)S(1)}, u32[]{:S(2)}, u32[]{:S(2)}) collective-permute-start(bf16[512,256]{1,0:T(8,128)(2,1)S(1)} %shard_map.101.own0), channel_id=1, source_target_pairs={{0,3},{1,0},{2,1},{3,2},{4,7},{5,4},{6,5},{7,6},{8,11},{9,8},{10,9... | collective-permute-start | bytes 786440 | tf_op jit(solution)/shard_map/ppermute | solution.py:325
  73.3 14.8 %collective-permute-start.18 = (bf16[512,256]{1,0:T(8,128)(2,1)S(1)}, bf16[512,256]{1,0:T(8,128)(2,1)S(1)}, u32[]{:S(2)}, u32[]{:S(2)}) collective-permute-start(bf16[512,256]{1,0:T(8,128)(2,1)S(1)} %shard_map.103.own1), channel_id=1, source_target_pairs={{0,1},{1,2},{2,3},{3,0},{4,5},{5,6},{6,7},{7,4},{8,9},{9,10},{10,1... | collective-permute-start | bytes 786440 | tf_op jit(solution)/shard_map/ppermute | solution.py:325
  75.9 17.9 %collective-permute-start.19 = (bf16[512,256]{1,0:T(8,128)(2,1)S(1)}, bf16[512,256]{1,0:T(8,128)(2,1)S(1)}, u32[]{:S(2)}, u32[]{:S(2)}) collective-permute-start(bf16[512,256]{1,0:T(8,128)(2,1)S(1)} %shard_map.103.own1), channel_id=1, source_target_pairs={{0,2},{1,3},{2,0},{3,1},{4,6},{5,7},{6,4},{7,5},{8,10},{9,11},{10,... | collective-permute-start | bytes 786440 | tf_op jit(solution)/shard_map/ppermute | solution.py:325
  83.3 10.5 %collective-permute-start.20 = (bf16[512,256]{1,0:T(8,128)(2,1)S(1)}, bf16[512,256]{1,0:T(8,128)(2,1)S(1)}, u32[]{:S(2)}, u32[]{:S(2)}) collective-permute-start(bf16[512,256]{1,0:T(8,128)(2,1)S(1)} %shard_map.103.own1), channel_id=1, source_target_pairs={{0,3},{1,0},{2,1},{3,2},{4,7},{5,4},{6,5},{7,6},{8,11},{9,8},{10,9... | collective-permute-start | bytes 786440 | tf_op jit(solution)/shard_map/ppermute | solution.py:325
  (6 other events, 99.4 us)

commit v3 on v2

--- a/solution.py
+++ b/solution.py
@@ -17,6 +17,7 @@
 HALF_ROWS = 672
 LOG2_E = 1.4426950408889634
 MEBI = 1024 * 1024
+CUT_LIMIT = 57
 
 NN = (((1,), (0,)), ((), ()))
 NT = (((1,), (1,)), ((), ()))
@@ -58,15 +59,22 @@
     return (row == column).astype(jnp.float32).astype(jnp.bfloat16)
 
 
-def front_kernel(
-    index, group, key_exps, value_exps, keys, values, key_matrix, value_matrix,
-    key_out, value_out, total_out, sent1, sent2, sent3,
-    key_in, value_in, rows, arrivals, departures,
-):
-    fetch_keys = pltpu.make_async_copy(keys, key_in, arrivals.at[0])
-    fetch_values = pltpu.make_async_copy(values, value_in, arrivals.at[1])
-    fetch_keys.start()
-    fetch_values.start()
+def dequantize_kernel(key_exps, value_exps, keys, values, key_out, value_out, total_out):
+    for part, (source, exponents, target) in enumerate(((keys, key_exps, key_out), (values, value_exps, value_out))):
+        for head in range(2):
+            lanes = slice(head * HEAD_SIZE, (head + 1) * HEAD_SIZE)
+            total = jnp.zeros((1, HEAD_SIZE), jnp.float32)
+            for block in range(BLOCK // SCALE_BLOCK):
+                rows = slice(block * SCALE_BLOCK, (block + 1) * SCALE_BLOCK)
+                scaled = source[rows, lanes].astype(jnp.float32) * factor_of(exponents[head, block])
+                target[rows, lanes] = scaled.astype(jnp.bfloat16)
+                if part == 0:
+                    total = total + jnp.sum(scaled, axis=0, keepdims=True)
+            if part == 0:
+                total_out[:, lanes] = jnp.broadcast_to(total, (8, HEAD_SIZE))
+
+
+def cut_kernel(index, group, key_matrix, value_matrix, ready, sent1, sent2, sent3, rows, arrivals, departures):
     half = HALF_ROWS
     core = index[0] & 1
     incoming, outgoing = [], []
@@ -75,27 +83,12 @@
         for part, matrix in enumerate((key_matrix, value_matrix)):
             incoming.append(
                 pltpu.make_async_copy(
-                    matrix.at[pl.ds(begin, half), :], rows.at[at, pl.ds(part * half, half), :], arrivals.at[2 + 2 * at + part]
+                    matrix.at[pl.ds(begin, half), :], rows.at[at, pl.ds(part * half, half), :], arrivals.at[2 * at + part]
                 )
             )
         outgoing.append(pltpu.make_async_copy(rows.at[at], target, departures.at[at]))
     for copy in incoming:
         copy.start()
-    for part, (fetch, source, exponents, target) in enumerate(
-        ((fetch_keys, key_in, key_exps, key_out), (fetch_values, value_in, value_exps, value_out))
-    ):
-        fetch.wait()
-        for head in range(2):
-            lanes = slice(head * HEAD_SIZE, (head + 1) * HEAD_SIZE)
-            total = jnp.zeros((1, HEAD_SIZE), jnp.float32)
-            for block in range(BLOCK // SCALE_BLOCK):
-                rows_at = slice(block * SCALE_BLOCK, (block + 1) * SCALE_BLOCK)
-                scaled = source[rows_at, lanes].astype(jnp.float32) * factor_of(exponents[head, block])
-                target[rows_at, lanes] = scaled.astype(jnp.bfloat16)
-                if part == 0:
-                    total = total + jnp.sum(scaled, axis=0, keepdims=True)
-            if part == 0:
-                total_out[:, lanes] = jnp.broadcast_to(total, (8, HEAD_SIZE))
     for at in range(3):
         incoming[2 * at].wait()
         incoming[2 * at + 1].wait()
@@ -136,80 +129,115 @@
     query_at = lax.broadcasted_iota(jnp.int32, (TILE, TILE), 1)
     lowest = -jnp.inf
 
-    for member in range(2):
-        for tile in range(BLOCK // TILE):
+    valid = [index >= 2, index >= 2, index >= 1, index >= 1, None, None]
+    factor = scale * LOG2_E
+    parts = []
+    for tile in range(BLOCK // TILE):
+        for member in range(2):
+            part = 2 * member + tile
             rows = slice(tile * TILE, (tile + 1) * TILE)
             columns = slice((2 * head + member) * HEAD_SIZE, (2 * head + member + 1) * HEAD_SIZE)
-            query = queries[rows, columns]
-            grad = grads[rows, columns]
-            grad_cols = all_grad_cols[columns, rows]
-            part = 2 * member + tile
-            place_at = slice(part * TILE, (part + 1) * TILE)
-            valid = [index >= 2, index >= 2, index >= 1, index >= 1, None, None]
-            highest = jnp.full((1, TILE), lowest, jnp.float32)
-            for step in range(5):
-                source = tile + step
-                at = slice(step * TILE, (step + 1) * TILE)
-                scores = product(key_rows[source * TILE : (source + 1) * TILE, :], query, NT)
-                if step == 0:
-                    scores = jnp.where(key_at > query_at, scores, lowest)
-                if step == 4:
-                    scores = jnp.where(key_at <= query_at, scores, lowest)
-                weights[part, at, :] = scores
-                peak = jnp.max(scores, axis=0, keepdims=True)
-                if valid[source] is not None:
-                    peak = jnp.where(valid[source], peak, lowest)
-                highest = jnp.maximum(highest, peak)
-            factor = scale * LOG2_E
-            shift = highest * factor
-            total = jnp.zeros((1, TILE), jnp.float32)
-            for step in range(5):
-                source = tile + step
-                at = slice(step * TILE, (step + 1) * TILE)
-                off = shift if valid[source] is None else jnp.where(valid[source], shift, jnp.inf)
-                weight = jnp.exp2(weights[part, at, :] * factor - off)
-                weights[part, at, :] = weight
-                total = total + jnp.sum(weight, axis=0, keepdims=True)
-            inverse = 1.0 / total
-            attended = jnp.zeros((HEAD_SIZE, TILE), jnp.float32)
-            for step in range(5):
-                source = tile + step
-                rounded = (weights[part, step * TILE : (step + 1) * TILE, :] * inverse).astype(jnp.bfloat16)
-                shares_out[source * TILE : (source + 1) * TILE, place_at] = rounded
-                attended = attended + product(value_cols[:, source * TILE : (source + 1) * TILE], rounded, NN)
-            row_dot = jnp.sum(attended * grad_cols, axis=0, keepdims=True)
-            query_part = jnp.zeros((HEAD_SIZE, TILE), jnp.float32)
-            for step in range(5):
-                source = tile + step
-                share_grad = product(value_rows[source * TILE : (source + 1) * TILE, :], grad, NT)
-                share = weights[part, step * TILE : (step + 1) * TILE, :] * inverse
-                score_grad = (share * (share_grad - row_dot)).astype(jnp.bfloat16)
-                score_out[source * TILE : (source + 1) * TILE, place_at] = score_grad
-                query_part = query_part + product(key_cols[:, source * TILE : (source + 1) * TILE], score_grad, NN)
-            query_grad[rows, member * HEAD_SIZE : (member + 1) * HEAD_SIZE] = (
-                (query_part * scale).T.astype(jnp.bfloat16)
+            parts.append(dict(
+                part=part, tile=tile, member=member, rows=rows, columns=columns,
+                highest=jnp.full((1, TILE), lowest, jnp.float32),
+                total=jnp.zeros((1, TILE), jnp.float32),
+                attended=jnp.zeros((HEAD_SIZE, TILE), jnp.float32),
+                query_part=jnp.zeros((HEAD_SIZE, TILE), jnp.float32),
+            ))
+
+    def take_scores(now, step):
+        source, part = now["tile"] + step, now["part"]
+        scores = product(key_rows[source * TILE : (source + 1) * TILE, :], queries[now["rows"], now["columns"]], NT)
+        if step == 0:
+            scores = jnp.where(key_at > query_at, scores, lowest)
+        if step == 4:
+            scores = jnp.where(key_at <= query_at, scores, lowest)
+        weights[part, step * TILE : (step + 1) * TILE, :] = scores
+        peak = jnp.max(scores, axis=0, keepdims=True)
+        if valid[source] is not None:
+            peak = jnp.where(valid[source], peak, lowest)
+        now["highest"] = jnp.maximum(now["highest"], peak)
+
+    def take_weights(now, step):
+        source, part = now["tile"] + step, now["part"]
+        at = slice(step * TILE, (step + 1) * TILE)
+        shift = now["highest"] * factor
+        off = shift if valid[source] is None else jnp.where(valid[source], shift, jnp.inf)
+        weight = jnp.exp2(weights[part, at, :] * factor - off)
+        weights[part, at, :] = weight
+        now["total"] = now["total"] + jnp.sum(weight, axis=0, keepdims=True)
+
+    def take_shares(now, step):
+        source, part = now["tile"] + step, now["part"]
+        if step == 0:
+            now["inverse"] = 1.0 / now["total"]
+        rounded = (weights[part, step * TILE : (step + 1) * TILE, :] * now["inverse"]).astype(jnp.bfloat16)
+        shares_out[source * TILE : (source + 1) * TILE, part * TILE : (part + 1) * TILE] = rounded
+        if step == 4:
+            span = slice(now["tile"] * TILE, (now["tile"] + 5) * TILE)
+            now["attended"] = product(value_cols[:, span], shares_out[span, part * TILE : (part + 1) * TILE], NN)
+
+    def take_grads(now, step):
+        source, part = now["tile"] + step, now["part"]
+        if step == 0:
+            now["row_dot"] = jnp.sum(now["attended"] * all_grad_cols[now["columns"], now["rows"]], axis=0, keepdims=True)
+        share_grad = product(value_rows[source * TILE : (source + 1) * TILE, :], grads[now["rows"], now["columns"]], NT)
+        share = weights[part, step * TILE : (step + 1) * TILE, :] * now["inverse"]
+        score_grad = (share * (share_grad - now["row_dot"])).astype(jnp.bfloat16)
+        score_out[source * TILE : (source + 1) * TILE, part * TILE : (part + 1) * TILE] = score_grad
+        if step == 4:
+            span = slice(now["tile"] * TILE, (now["tile"] + 5) * TILE)
+            now["query_part"] = product(key_cols[:, span], score_out[span, part * TILE : (part + 1) * TILE], NN)
+            query_grad[now["rows"], now["member"] * HEAD_SIZE : (now["member"] + 1) * HEAD_SIZE] = (
+                (now["query_part"] * scale).T.astype(jnp.bfloat16)
             )
+
+    stages = (take_grads, take_shares, take_weights, take_scores)
+    for turn in range(len(parts) + len(stages) - 1):
+        for step in range(5):
+            for stage, take in enumerate(stages):
+                at = turn - (len(stages) - 1 - stage)
+                if 0 <= at < len(parts):
+                    take(parts[at], step)
 
     for source in range(6):
         rows = slice(source * TILE, (source + 1) * TILE)
         out, first = ((grad2, 0), (grad1, 2), (grad0, 4))[source // 2]
         target = slice((source - first) * TILE, (source - first + 1) * TILE)
+        lanes_of = [slice((2 * head + member) * HEAD_SIZE, (2 * head + member + 1) * HEAD_SIZE) for member in range(2)]
         if 1 <= source <= 4:
-            parts = [(slice(member * BLOCK, (member + 1) * BLOCK), member, slice(0, BLOCK)) for member in range(2)]
+            query_rows = slice(0, BLOCK)
+            left = (score_out[rows, :], shares_out[rows, :])
         else:
             tile = 0 if source == 0 else 1
-            parts = [
-                (slice((2 * member + tile) * TILE, (2 * member + tile + 1) * TILE), member, slice(tile * TILE, (tile + 1) * TILE))
-                for member in range(2)
+            query_rows = slice(tile * TILE, (tile + 1) * TILE)
+            left = [
+                jnp.concatenate([kept[rows, (2 * member + tile) * TILE : (2 * member + tile + 1) * TILE] for member in range(2)], axis=1)
+                for kept in (score_out, shares_out)
             ]
-        key_part = jnp.zeros((TILE, HEAD_SIZE), jnp.float32)
-        value_part = jnp.zeros((TILE, HEAD_SIZE), jnp.float32)
-        for place_at, member, query_rows in parts:
-            columns = slice((2 * head + member) * HEAD_SIZE, (2 * head + member + 1) * HEAD_SIZE)
-            key_part = key_part + product(score_out[rows, place_at], queries[query_rows, columns], NN)
-            value_part = value_part + product(shares_out[rows, place_at], grads[query_rows, columns], NN)
+        key_part = product(left[0], jnp.concatenate([queries[query_rows, lanes] for lanes in lanes_of], axis=0), NN)
+        value_part = product(left[1], jnp.concatenate([grads[query_rows, lanes] for lanes in lanes_of], axis=0), NN)
         out[target, 0:HEAD_SIZE] = (key_part * scale).astype(out.dtype)
         out[target, HEAD_SIZE : 2 * HEAD_SIZE] = value_part.astype(out.dtype)
+
+
+def attend_call(head, *operands):
+    return vmem_call(
+        functools.partial(attend_kernel, head),
+        (shape_of(BLOCK, 256), shape_of(BLOCK, 256, jnp.float32), shape_of(BLOCK, 256), shape_of(BLOCK, 256, jnp.float32)),
+        operands,
+        in_specs=[SMEM] + [VMEM] * 8,
+        mebibytes=18,
+        scratch=[
+            pltpu.VMEM((WINDOW_ROWS, HEAD_SIZE), jnp.bfloat16),
+            pltpu.VMEM((WINDOW_ROWS, HEAD_SIZE), jnp.bfloat16),
+            pltpu.VMEM((HEAD_SIZE, WINDOW_ROWS), jnp.bfloat16),
+            pltpu.VMEM((HEAD_SIZE, WINDOW_ROWS), jnp.bfloat16),
+            pltpu.VMEM((4, 5 * TILE, TILE), jnp.float32),
+            pltpu.VMEM((WINDOW_ROWS, 4 * TILE), jnp.bfloat16),
+            pltpu.VMEM((WINDOW_ROWS, 4 * TILE), jnp.bfloat16),
+        ],
+    )
 
 
 def merge_kernel(place, older, arrived, out):
@@ -303,35 +331,38 @@
     key_exponents, value_exponents = key_exponents.T, value_exponents.T
     model_rows = key_matrix.shape[0] // groups
     piece_shape = shape_of(model_rows, 256)
-    exact_keys, exact_values, key_total, *sent = pl.pallas_call(
-        front_kernel,
-        out_shape=(shape_of(BLOCK, 256), shape_of(BLOCK, 256), shape_of(8, 256, jnp.float32)) + (piece_shape,) * 3,
-        in_specs=[SMEM] * 4 + [HBM] * 4,
-        out_specs=(VMEM,) * 3 + (HBM,) * 3,
+    exact_keys, exact_values, key_total = vmem_call(
+        dequantize_kernel,
+        (shape_of(BLOCK, 256), shape_of(BLOCK, 256), shape_of(8, 256, jnp.float32)),
+        (key_exponents, value_exponents, keys, values),
+        in_specs=[SMEM, SMEM, VMEM, VMEM],
+    )
+    older_keys = onward(exact_keys, 2)
+    last_total = onward(key_total, 1)
+
+    def along_head(value, steps):
+        return lax.ppermute(value, "head", [(at, (at + steps) % groups) for at in range(groups)])
+
+
+    older_values = onward(exact_values, 2)
+    smooth = vmem_call(
+        smooth_kernel, shape_of(BLOCK, 256), (place, exact_keys, older_keys, last_total), in_specs=[SMEM, VMEM, VMEM, VMEM]
+    )
+    older_smooth = onward(smooth, 2)
+    sent = pl.pallas_call(
+        cut_kernel,
+        out_shape=(piece_shape,) * 3,
+        in_specs=[SMEM, SMEM, HBM, HBM, pl.BlockSpec(memory_space=pl.ANY)],
+        out_specs=(HBM,) * 3,
         scratch_shapes=[
-            pltpu.VMEM((BLOCK, 256), jnp.bfloat16),
-            pltpu.VMEM((BLOCK, 256), jnp.bfloat16),
             pltpu.VMEM((3, model_rows, 256), jnp.bfloat16),
-            pltpu.SemaphoreType.DMA((8,)),
+            pltpu.SemaphoreType.DMA((6,)),
             pltpu.SemaphoreType.DMA((3,)),
         ],
         cost_estimate=pl.CostEstimate(flops=1, bytes_accessed=1, transcendentals=0),
-        compiler_params=pltpu.CompilerParams(vmem_limit_bytes=59 * MEBI),
-    )(place, group, key_exponents, value_exponents, keys, values, key_matrix, value_matrix)
-    older_keys = onward(exact_keys, 2)
-    last_total = onward(key_total, 1)
-
-    def along_head(value, steps):
-        return lax.ppermute(value, "head", [(at, (at + steps) % groups) for at in range(groups)])
-
-
-    older_values = onward(exact_values, 2)
-    smooth = vmem_call(
-        smooth_kernel, shape_of(BLOCK, 256), (place, exact_keys, older_keys, last_total), in_specs=[SMEM, VMEM, VMEM, VMEM]
-    )
-    older_smooth = onward(smooth, 2)
-    near, back_near, _ = lax.optimization_barrier((sent[0], sent[2], smooth))
-    fetched = [along_head(near, 1), None, along_head(back_near, 3)]
+        compiler_params=pltpu.CompilerParams(vmem_limit_bytes=CUT_LIMIT * MEBI),
+    )(place, group, key_matrix, value_matrix, smooth)
+    fetched = [along_head(piece, steps) for steps, piece in zip((1, 2, 3), sent)]
     last = to_sibling(
         jnp.where(
             core == 0,
@@ -351,26 +382,12 @@
     for head in range(2):
         if head == 1:
             queries, _, swapped[0], swapped[2] = lax.optimization_barrier((queries, back, swapped[0], swapped[2]))
-        query_part, grad2, grad1, grad0 = vmem_call(
-            functools.partial(attend_kernel, head),
-            (shape_of(BLOCK, 256), shape_of(BLOCK, 256, jnp.float32), shape_of(BLOCK, 256), shape_of(BLOCK, 256, jnp.float32)),
-            (place, queries, output_gradient, grad_cols, older_smooth, last, smooth, older_values, exact_values),
-            in_specs=[SMEM] + [VMEM] * 8,
-            scratch=[
-                pltpu.VMEM((WINDOW_ROWS, HEAD_SIZE), jnp.bfloat16),
-                pltpu.VMEM((WINDOW_ROWS, HEAD_SIZE), jnp.bfloat16),
-                pltpu.VMEM((HEAD_SIZE, WINDOW_ROWS), jnp.bfloat16),
-                pltpu.VMEM((HEAD_SIZE, WINDOW_ROWS), jnp.bfloat16),
-                pltpu.VMEM((4, 5 * TILE, TILE), jnp.float32),
-                pltpu.VMEM((WINDOW_ROWS, 4 * TILE), jnp.bfloat16),
-                pltpu.VMEM((WINDOW_ROWS, 4 * TILE), jnp.bfloat16),
-            ],
-            mebibytes=18,
+        query_part, grad2, grad1, grad0 = attend_call(
+            head, place, queries, output_gradient, grad_cols, older_smooth, last, smooth, older_values, exact_values
         )
         query_grads.append(query_part)
         if head == 0:
-            fetched[0], fetched[1], fetched[2], _ = lax.optimization_barrier((fetched[0], sent[1], fetched[2], grad1))
-            fetched[1] = along_head(fetched[1], 2)
+            fetched[0], fetched[2], _ = lax.optimization_barrier((fetched[0], fetched[2], grad1))
             swapped = [to_sibling(fetched[0]), None, to_sibling(fetched[2])]
         sibling_grad = to_sibling(grad1)
         if head == 1:

time: 96.5 us -> 98.3 us (1.019)
  starting transfers between devices: 34.9 us -> 40.3 us
  waiting for transfers between devices: 31.8 us -> 28.4 us
  Pallas kernels: 25.6 us -> 22.9 us
  local copies, waits for them, and re-layouts: 0.99 us -> 3.29 us
    ppermute x6, starting transfers between devices: 19.1 us -> 24.4 us  [onward(): return lax.ppermute(value, 'seq', shift_pairs(count, steps))]
    ppermute x6, waiting for transfers between devices: 12.9 us -> 9.87 us  [onward(): return lax.ppermute(value, 'seq', shift_pairs(count, steps))]
    unnamed x18 -> x22, local copies, waits for them, and re-layouts: 0.99 us -> 3.29 us
    pallas_call x1, Pallas kernels: 4.27 us -> 2.57 us  [local(): pl.pallas_call(cut_kernel, out_shape=(piece_shape,) * 3, in_specs=[SMEM,...]
    pallas_call x10 -> x11, Pallas kernels: 21.4 us -> 20.4 us  [vmem_call(): pl.pallas_call(kernel, out_shape=out_shapes, in_specs=in_specs if in_spec...]
where the time goes in v3:
time: 98.3 us; the launch traced here: 97.8 us
  starting transfers between devices  40.3 us (41%)
  waiting for transfers between devices  28.4 us (29%)
  Pallas kernels  22.9 us (23%)
  local copies, waits for them, and re-layouts  3.29 us (3%)
  other arithmetic  1.91 us (2%)
    ppermute x6, starting transfers between devices, onward(): return lax.ppermute(value, 'seq', shift_pairs(count, steps))  24.4 us
    pallas_call x11, Pallas kernels, vmem_call(): pl.pallas_call(kernel, out_shape=out_shapes, in_specs=in_specs if in_spec...  20.4 us
    ppermute x9, starting transfers between devices, along_head(): lax.ppermute(value, 'head', [(at, (at + steps) % groups) for at in range(...  15 us
    ppermute x9, waiting for transfers between devices, along_head(): lax.ppermute(value, 'head', [(at, (at + steps) % groups) for at in range(...  14.7 us
    ppermute x6, waiting for transfers between devices, onward(): return lax.ppermute(value, 'seq', shift_pairs(count, steps))  9.87 us
    ppermute x6, waiting for transfers between devices, to_sibling(): return lax.ppermute(value, 'seq', siblings)  3.85 us
    unnamed x22, local copies, waits for them, and re-layouts  3.29 us
    pallas_call x1, Pallas kernels, local(): pl.pallas_call(cut_kernel, out_shape=(piece_shape,) * 3, in_specs=[SMEM,...  2.57 us
  transfers between devices with their start and end apart: 21, of which 12 were waited for; matrix products, arithmetic and copies ran while one was open for 2% of the time, Pallas kernels for 20%

profile of v3, /device:TPU:128, one launch (start us, length us, event | category | flops | bytes accessed | tf_op | source)
XLA Modules:
  0.0 97.8 jit_solution(4852374346149182365)
XLA Ops:
  4.6 3.5 %collective-permute-start = (bf16[512,256]{1,0:T(8,128)(2,1)S(1)}, bf16[512,256]{1,0:T(8,128)(2,1)S(1)}, u32[]{:S(2)}, u32[]{:S(2)}) collective-permute-start(bf16[512,256]{1,0:T(8,128)(2,1)S(1)} %get-tuple-element.26.own), channel_id=1, source_target_pairs={{0,8},{4,12},{8,16},{12,20},{16,24},{20,28},{24,32},{28,36},{32,40... | collective-permute-start | bytes 786440 | tf_op jit(solution)/shard_map/ppermute | solution.py:329
  8.1 1.9 %collective-permute-start.1 = (f32[8,256]{1,0:T(8,128)S(1)}, f32[8,256]{1,0:T(8,128)S(1)}, u32[]{:S(2)}, u32[]{:S(2)}) collective-permute-start(f32[8,256]{1,0:T(8,128)S(1)} %get-tuple-element.27), channel_id=1, source_target_pairs={{0,4},{4,8},{8,12},{12,16},{16,20},{20,24},{24,28},{28,32},{32,36}... | collective-permute-start | bytes 24584 | tf_op jit(solution)/shard_map/ppermute | solution.py:329
  10.0 3.5 %collective-permute-start.3 = (bf16[512,256]{1,0:T(8,128)(2,1)S(1)}, bf16[512,256]{1,0:T(8,128)(2,1)S(1)}, u32[]{:S(2)}, u32[]{:S(2)}) collective-permute-start(bf16[512,256]{1,0:T(8,128)(2,1)S(1)} %get-tuple-element.31.values0), channel_id=1, source_target_pairs={{0,8},{4,12},{8,16},{12,20},{16,24},{20,28},{24,32},{28,36},{32,40... | collective-permute-start | bytes 786440 | tf_op jit(solution)/shard_map/ppermute | solution.py:329
  13.5 3.4 %collective-permute-done.1.total = f32[8,256]{1,0:T(8,128)S(1)} collective-permute-done((f32[8,256]{1,0:T(8,128)S(1)}, f32[8,256]{1,0:T(8,128)S(1)}, u32[]{:S(2)}, u32[]{:S(2)}) %collective-permute-start.1) | collective-permute-done | bytes 8224 | tf_op jit(solution)/shard_map/ppermute | solution.py:329
  19.1 1.9 %collective-permute-start.2 = (bf16[512,256]{1,0:T(8,128)(2,1)}, bf16[512,256]{1,0:T(8,128)(2,1)S(1)}, u32[]{:S(2)}, u32[]{:S(2)}) collective-permute-start(bf16[512,256]{1,0:T(8,128)(2,1)} %shard_map.96.ready.keys0), channel_id=1, source_target_pairs={{0,8},{4,12},{8,16},{12,20},{16,24},{20,28},{24,32},{28,36},{32,40... | collective-permute-start | bytes 786440 | tf_op jit(solution)/shard_map/ppermute | solution.py:329
  21.0 2.6 %shard_map.100 = (bf16[1344,256]{1,0:T(8,128)(2,1)}, bf16[1344,256]{1,0:T(8,128)(2,1)}, bf16[1344,256]{1,0:T(8,128)(2,1)}) custom-call(s32[1]{0:T(128)} %bitcast.place.index, s32[1]{0:T(128)} %bitcast.3.group, bf16[5376,256]{1,0:T(8,128)(2,1)} %keys.3, bf16[5376,256]{1,0:T(8,128)(2,1)} %values.3, bf16[512,256]{1,0:T(8,128)(2,1)} %shard_map.96.ready.keys0), custom_call_target="tpu_custom_call" | custom-call | flops 1 | bytes 1 | tf_op jit(solution)/shard_map/pallas_call | solution.py:352
  23.6 1.6 %collective-permute-start.6 = (bf16[1344,256]{1,0:T(8,128)(2,1)}, bf16[1344,256]{1,0:T(8,128)(2,1)S(1)}, u32[]{:S(2)}, u32[]{:S(2)}) collective-permute-start(bf16[1344,256]{1,0:T(8,128)(2,1)} %get-tuple-element.35), channel_id=1, source_target_pairs={{0,1},{1,2},{2,3},{3,0},{4,5},{5,6},{6,7},{7,4},{8,9},{9,10},{10,1... | collective-permute-start | bytes 2064392 | tf_op jit(solution)/shard_map/ppermute | solution.py:344
  25.2 1.7 %collective-permute-start.7 = (bf16[1344,256]{1,0:T(8,128)(2,1)}, bf16[1344,256]{1,0:T(8,128)(2,1)S(1)}, u32[]{:S(2)}, u32[]{:S(2)}) collective-permute-start(bf16[1344,256]{1,0:T(8,128)(2,1)} %get-tuple-element.36), channel_id=1, source_target_pairs={{0,3},{1,0},{2,1},{3,2},{4,7},{5,4},{6,5},{7,6},{8,11},{9,8},{10,9... | collective-permute-start | bytes 2064392 | tf_op jit(solution)/shard_map/ppermute | solution.py:344
  26.9 4.7 %collective-permute-done.2.keys2 = bf16[512,256]{1,0:T(8,128)(2,1)S(1)} collective-permute-done((bf16[512,256]{1,0:T(8,128)(2,1)}, bf16[512,256]{1,0:T(8,128)(2,1)S(1)}, u32[]{:S(2)}, u32[]{:S(2)}) %collective-permute-start.2) | collective-permute-done | bytes 262176 | tf_op jit(solution)/shard_map/ppermute | solution.py:329
  33.2 1.5 %collective-permute-done.4.last = bf16[512,512]{1,0:T(8,128)(2,1)S(1)} collective-permute-done((bf16[512,512]{1,0:T(8,128)(2,1)S(1)}, bf16[512,512]{1,0:T(8,128)(2,1)S(1)}, u32[]{:S(2)}, u32[]{:S(2)}) %collective-permute-start.4) | collective-permute-done | bytes 524320 | tf_op jit(solution)/shard_map/ppermute | solution.py:326
  34.7 5.7 %shard_map.98 = (bf16[512,256]{1,0:T(8,128)(2,1)S(1)}, f32[512,256]{1,0:T(8,128)S(1)}, bf16[512,256]{1,0:T(8,128)(2,1)S(1)}, f32[512,256]{1,0:T(8,128)S(1)}) custom-call(s32[1]{0:T(128)} %bitcast.place.index, bf16[512,512]{1,0:T(8,128)(2,1)S(1)} %get-tuple-element.39.queries, bf16[512,512]{1,0:T(8,128)(2,1)S(1)} %get-tuple-element.29.grads, ...), custom_call_target="tpu_custom_call" | custom-call | flops 1 | bytes 1 | tf_op jit(solution)/shard_map/pallas_call | solution.py:32
  41.8 2.7 %collective-permute-start.16 = (bf16[1344,256]{1,0:T(8,128)(2,1)S(1)}, bf16[1344,256]{1,0:T(8,128)(2,1)S(1)}, u32[]{:S(2)}, u32[]{:S(2)}) collective-permute-start(bf16[1344,256]{1,0:T(8,128)(2,1)S(1)} %copy-done.10), channel_id=1, source_target_pairs={{0,2},{1,3},{2,0},{3,1},{4,6},{5,7},{6,4},{7,5},{8,10},{9,11},{10,... | collective-permute-start | bytes 2064392 | tf_op jit(solution)/shard_map/ppermute | solution.py:344
  44.6 1.5 %collective-permute-done.5.arrived.sibling = bf16[512,256]{1,0:T(8,128)(2,1)S(1)} collective-permute-done((bf16[512,256]{1,0:T(8,128)(2,1)S(1)}, bf16[512,256]{1,0:T(8,128)(2,1)S(1)}, u32[]{:S(2)}, u32[]{:S(2)}) %collective-permute-start.5) | collective-permute-done | bytes 262176 | tf_op jit(solution)/shard_map/ppermute | solution.py:326
  46.2 7.1 %collective-permute-start.10 = (bf16[512,256]{1,0:T(8,128)(2,1)S(1)}, bf16[512,256]{1,0:T(8,128)(2,1)S(1)}, u32[]{:S(2)}, u32[]{:S(2)}) collective-permute-start(bf16[512,256]{1,0:T(8,128)(2,1)S(1)} %shard_map.99), channel_id=1, source_target_pairs={{8,0},{12,4},{16,8},{20,12},{24,16},{28,20},{32,24},{36,28},{40,32... | collective-permute-start | bytes 786440 | tf_op jit(solution)/shard_map/ppermute | solution.py:329
  53.3 5.9 %shard_map.101 = (bf16[512,256]{1,0:T(8,128)(2,1)S(1)}, f32[512,256]{1,0:T(8,128)S(1)}, bf16[512,256]{1,0:T(8,128)(2,1)S(1)}, f32[512,256]{1,0:T(8,128)S(1)}) custom-call(s32[1]{0:T(128)} %bitcast.place.index, bf16[512,512]{1,0:T(8,128)(2,1)S(1)} %get-tuple-element.39.queries, bf16[512,512]{1,0:T(8,128)(2,1)S(1)} %get-tuple-element.29.grads, ...), custom_call_target="tpu_custom_call" | custom-call | flops 1 | bytes 1 | tf_op jit(solution)/shard_map/pallas_call | solution.py:32
  61.1 6.5 %collective-permute-start.12 = (bf16[512,256]{1,0:T(8,128)(2,1)S(1)}, bf16[512,256]{1,0:T(8,128)(2,1)S(1)}, u32[]{:S(2)}, u32[]{:S(2)}) collective-permute-start(bf16[512,256]{1,0:T(8,128)(2,1)S(1)} %shard_map.103), channel_id=1, source_target_pairs={{8,0},{12,4},{16,8},{20,12},{24,16},{28,20},{32,24},{36,28},{40,32... | collective-permute-start | bytes 786440 | tf_op jit(solution)/shard_map/ppermute | solution.py:329
  67.6 1.6 %collective-permute-start.13 = (bf16[512,256]{1,0:T(8,128)(2,1)S(1)}, bf16[512,256]{1,0:T(8,128)(2,1)S(1)}, u32[]{:S(2)}, u32[]{:S(2)}) collective-permute-start(bf16[512,256]{1,0:T(8,128)(2,1)S(1)} %shard_map.102.own0), channel_id=1, source_target_pairs={{0,1},{1,2},{2,3},{3,0},{4,5},{5,6},{6,7},{7,4},{8,9},{9,10},{10,1... | collective-permute-start | bytes 786440 | tf_op jit(solution)/shard_map/ppermute | solution.py:344
  69.2 2.9 %collective-permute-start.14 = (bf16[512,256]{1,0:T(8,128)(2,1)S(1)}, bf16[512,256]{1,0:T(8,128)(2,1)S(1)}, u32[]{:S(2)}, u32[]{:S(2)}) collective-permute-start(bf16[512,256]{1,0:T(8,128)(2,1)S(1)} %shard_map.102.own0), channel_id=1, source_target_pairs={{0,2},{1,3},{2,0},{3,1},{4,6},{5,7},{6,4},{7,5},{8,10},{9,11},{10,... | collective-permute-start | bytes 786440 | tf_op jit(solution)/shard_map/ppermute | solution.py:344
  74.6 1.6 %collective-permute-start.18 = (bf16[512,256]{1,0:T(8,128)(2,1)S(1)}, bf16[512,256]{1,0:T(8,128)(2,1)S(1)}, u32[]{:S(2)}, u32[]{:S(2)}) collective-permute-start(bf16[512,256]{1,0:T(8,128)(2,1)S(1)} %shard_map.104.own1), channel_id=1, source_target_pairs={{0,1},{1,2},{2,3},{3,0},{4,5},{5,6},{6,7},{7,4},{8,9},{9,10},{10,1... | collective-permute-start | bytes 786440 | tf_op jit(solution)/shard_map/ppermute | solution.py:344
  77.4 1.9 %collective-permute-start.19 = (bf16[512,256]{1,0:T(8,128)(2,1)S(1)}, bf16[512,256]{1,0:T(8,128)(2,1)S(1)}, u32[]{:S(2)}, u32[]{:S(2)}) collective-permute-start(bf16[512,256]{1,0:T(8,128)(2,1)S(1)} %shard_map.104.own1), channel_id=1, source_target_pairs={{0,2},{1,3},{2,0},{3,1},{4,6},{5,7},{6,4},{7,5},{8,10},{9,11},{10,... | collective-permute-start | bytes 786440 | tf_op jit(solution)/shard_map/ppermute | solution.py:344
  79.3 5.6 %collective-permute-done.14.rest_1_ = bf16[512,256]{1,0:T(8,128)(2,1)S(1)} collective-permute-done((bf16[512,256]{1,0:T(8,128)(2,1)S(1)}, bf16[512,256]{1,0:T(8,128)(2,1)S(1)}, u32[]{:S(2)}, u32[]{:S(2)}) %collective-permute-start.14) | collective-permute-done | bytes 262176 | tf_op jit(solution)/shard_map/ppermute | solution.py:344
  85.8 2.7 %shard_map.105.early = f32[1344,512]{1,0:T(8,128)S(1)} custom-call(s32[1]{0:T(128)} %bitcast.place.index, s32[1]{0:T(128)} %bitcast.3.group, bf16[5376,256]{1,0:T(8,128)(2,1)S(1)} %copy-done, bf16[5376,256]{1,0:T(8,128)(2,1)S(1)} %copy-done.1, bf16[512,256]{1,0:T(8,128)(2,1)S(1)} %shard_map.102.own0, bf16[512,256]{1,0:T(8,128)(2,1)S(1)} %shard_map.104.own1, ...), custom_call_target="tpu_custom_call" | custom-call | flops 1 | bytes 1 | tf_op jit(solution)/shard_map/pallas_call | solution.py:32
  89.3 6.1 %collective-permute-done.19.rest_1_ = bf16[512,256]{1,0:T(8,128)(2,1)S(1)} collective-permute-done((bf16[512,256]{1,0:T(8,128)(2,1)S(1)}, bf16[512,256]{1,0:T(8,128)(2,1)S(1)}, u32[]{:S(2)}, u32[]{:S(2)}) %collective-permute-start.19) | collective-permute-done | bytes 262176 | tf_op jit(solution)/shard_map/ppermute | solution.py:344
  95.5 2.4 %shard_map.106 = bf16[1344,512]{1,0:T(8,128)(2,1)} custom-call(s32[1]{0:T(128)} %bitcast.place.index, f32[1344,512]{1,0:T(8,128)S(1)} %shard_map.105.early, bf16[512,256]{1,0:T(8,128)(2,1)S(1)} %collective-permute-done.18.rest_0_, bf16[512,256]{1,0:T(8,128)(2,1)S(1)} %collective-permute-done.19.rest_1_, ...), custom_call_target="tpu_custom_call" | custom-call | flops 1 | bytes 1 | tf_op jit(solution)/shard_map/pallas_call | solution.py:32
  (54 shorter events, 16.4 us)
Async XLA Ops:
  4.6 13.3 %collective-permute-start = (bf16[512,256]{1,0:T(8,128)(2,1)S(1)}, bf16[512,256]{1,0:T(8,128)(2,1)S(1)}, u32[]{:S(2)}, u32[]{:S(2)}) collective-permute-start(bf16[512,256]{1,0:T(8,128)(2,1)S(1)} %get-tuple-element.26.own), channel_id=1, source_target_pairs={{0,8},{4,12},{8,16},{12,20},{16,24},{20,28},{24,32},{28,36},{32,40... | collective-permute-start | bytes 786440 | tf_op jit(solution)/shard_map/ppermute | solution.py:329
  8.1 8.8 %collective-permute-start.1 = (f32[8,256]{1,0:T(8,128)S(1)}, f32[8,256]{1,0:T(8,128)S(1)}, u32[]{:S(2)}, u32[]{:S(2)}) collective-permute-start(f32[8,256]{1,0:T(8,128)S(1)} %get-tuple-element.27), channel_id=1, source_target_pairs={{0,4},{4,8},{8,12},{12,16},{16,20},{20,24},{24,28},{28,32},{32,36}... | collective-permute-start | bytes 24584 | tf_op jit(solution)/shard_map/ppermute | solution.py:329
  10.0 16.9 %collective-permute-start.3 = (bf16[512,256]{1,0:T(8,128)(2,1)S(1)}, bf16[512,256]{1,0:T(8,128)(2,1)S(1)}, u32[]{:S(2)}, u32[]{:S(2)}) collective-permute-start(bf16[512,256]{1,0:T(8,128)(2,1)S(1)} %get-tuple-element.31.values0), channel_id=1, source_target_pairs={{0,8},{4,12},{8,16},{12,20},{16,24},{20,28},{24,32},{28,36},{32,40... | collective-permute-start | bytes 786440 | tf_op jit(solution)/shard_map/ppermute | solution.py:329
  19.1 12.5 %collective-permute-start.2 = (bf16[512,256]{1,0:T(8,128)(2,1)}, bf16[512,256]{1,0:T(8,128)(2,1)S(1)}, u32[]{:S(2)}, u32[]{:S(2)}) collective-permute-start(bf16[512,256]{1,0:T(8,128)(2,1)} %shard_map.96.ready.keys0), channel_id=1, source_target_pairs={{0,8},{4,12},{8,16},{12,20},{16,24},{20,28},{24,32},{28,36},{32,40... | collective-permute-start | bytes 786440 | tf_op jit(solution)/shard_map/ppermute | solution.py:329
  23.6 17.7 %collective-permute-start.6 = (bf16[1344,256]{1,0:T(8,128)(2,1)}, bf16[1344,256]{1,0:T(8,128)(2,1)S(1)}, u32[]{:S(2)}, u32[]{:S(2)}) collective-permute-start(bf16[1344,256]{1,0:T(8,128)(2,1)} %get-tuple-element.35), channel_id=1, source_target_pairs={{0,1},{1,2},{2,3},{3,0},{4,5},{5,6},{6,7},{7,4},{8,9},{9,10},{10,1... | collective-permute-start | bytes 2064392 | tf_op jit(solution)/shard_map/ppermute | solution.py:344
  25.2 16.1 %collective-permute-start.7 = (bf16[1344,256]{1,0:T(8,128)(2,1)}, bf16[1344,256]{1,0:T(8,128)(2,1)S(1)}, u32[]{:S(2)}, u32[]{:S(2)}) collective-permute-start(bf16[1344,256]{1,0:T(8,128)(2,1)} %get-tuple-element.36), channel_id=1, source_target_pairs={{0,3},{1,0},{2,1},{3,2},{4,7},{5,4},{6,5},{7,6},{8,11},{9,8},{10,9... | collective-permute-start | bytes 2064392 | tf_op jit(solution)/shard_map/ppermute | solution.py:344
  32.7 2.0 %collective-permute-start.4 = (bf16[512,512]{1,0:T(8,128)(2,1)S(1)}, bf16[512,512]{1,0:T(8,128)(2,1)S(1)}, u32[]{:S(2)}, u32[]{:S(2)}) collective-permute-start(bf16[512,512]{1,0:T(8,128)(2,1)S(1)} %maximum_select_fusion), channel_id=1, source_target_pairs={{0,4},{4,0},{8,12},{12,8},{16,20},{20,16},{24,28},{28,24},{32,36},... | collective-permute-start | bytes 1572872 | tf_op jit(solution)/shard_map/ppermute | solution.py:326
  40.4 19.0 %copy-start.7 = (s32[4,2]{0,1:T(2,128)S(1)}, s32[4,2]{0,1:T(2,128)}, u32[]{:S(2)}) copy-start(s32[4,2]{0,1:T(2,128)} %param.12) | copy-start | bytes 100
  41.3 12.0 %collective-permute-start.8 = (bf16[1344,256]{1,0:T(8,128)(2,1)S(1)}, bf16[1344,256]{1,0:T(8,128)(2,1)S(1)}, u32[]{:S(2)}, u32[]{:S(2)}) collective-permute-start(bf16[1344,256]{1,0:T(8,128)(2,1)S(1)} %collective-permute-done.6.rest_3_), channel_id=1, source_target_pairs={{0,4},{4,0},{8,12},{12,8},{16,20},{20,16},{24,28},{28,24},{32,36},... | collective-permute-start | bytes 2064392 | tf_op jit(solution)/shard_map/ppermute | solution.py:326
  41.3 12.0 %collective-permute-start.9 = (bf16[1344,256]{1,0:T(8,128)(2,1)S(1)}, bf16[1344,256]{1,0:T(8,128)(2,1)S(1)}, u32[]{:S(2)}, u32[]{:S(2)}) collective-permute-start(bf16[1344,256]{1,0:T(8,128)(2,1)S(1)} %collective-permute-done.7.rest_5_), channel_id=1, source_target_pairs={{0,4},{4,0},{8,12},{12,8},{16,20},{20,16},{24,28},{28,24},{32,36},... | collective-permute-start | bytes 2064392 | tf_op jit(solution)/shard_map/ppermute | solution.py:326
  41.8 19.1 %collective-permute-start.16 = (bf16[1344,256]{1,0:T(8,128)(2,1)S(1)}, bf16[1344,256]{1,0:T(8,128)(2,1)S(1)}, u32[]{:S(2)}, u32[]{:S(2)}) collective-permute-start(bf16[1344,256]{1,0:T(8,128)(2,1)S(1)} %copy-done.10), channel_id=1, source_target_pairs={{0,2},{1,3},{2,0},{3,1},{4,6},{5,7},{6,4},{7,5},{8,10},{9,11},{10,... | collective-permute-start | bytes 2064392 | tf_op jit(solution)/shard_map/ppermute | solution.py:344
  44.6 1.5 %collective-permute-start.5 = (bf16[512,256]{1,0:T(8,128)(2,1)S(1)}, bf16[512,256]{1,0:T(8,128)(2,1)S(1)}, u32[]{:S(2)}, u32[]{:S(2)}) collective-permute-start(bf16[512,256]{1,0:T(8,128)(2,1)S(1)} %get-tuple-element.34), channel_id=1, source_target_pairs={{0,4},{4,0},{8,12},{12,8},{16,20},{20,16},{24,28},{28,24},{32,36},... | collective-permute-start | bytes 786440 | tf_op jit(solution)/shard_map/ppermute | solution.py:326
  46.2 13.2 %collective-permute-start.10 = (bf16[512,256]{1,0:T(8,128)(2,1)S(1)}, bf16[512,256]{1,0:T(8,128)(2,1)S(1)}, u32[]{:S(2)}, u32[]{:S(2)}) collective-permute-start(bf16[512,256]{1,0:T(8,128)(2,1)S(1)} %shard_map.99), channel_id=1, source_target_pairs={{8,0},{12,4},{16,8},{20,12},{24,16},{28,20},{32,24},{36,28},{40,32... | collective-permute-start | bytes 786440 | tf_op jit(solution)/shard_map/ppermute | solution.py:329
  53.3 32.4 %copy-start.1 = (bf16[5376,256]{1,0:T(8,128)(2,1)S(1)}, bf16[5376,256]{1,0:T(8,128)(2,1)}, u32[]{:S(2)}) copy-start(bf16[5376,256]{1,0:T(8,128)(2,1)} %values.3) | copy-start | bytes 8257540
  59.2 26.6 %copy-start = (bf16[5376,256]{1,0:T(8,128)(2,1)S(1)}, bf16[5376,256]{1,0:T(8,128)(2,1)}, u32[]{:S(2)}) copy-start(bf16[5376,256]{1,0:T(8,128)(2,1)} %keys.3) | copy-start | bytes 8257540
  59.2 1.6 %collective-permute-start.11 = (bf16[512,256]{1,0:T(8,128)(2,1)S(1)}, bf16[512,256]{1,0:T(8,128)(2,1)S(1)}, u32[]{:S(2)}, u32[]{:S(2)}) collective-permute-start(bf16[512,256]{1,0:T(8,128)(2,1)S(1)} %get-tuple-element.43), channel_id=1, source_target_pairs={{0,4},{4,0},{8,12},{12,8},{16,20},{20,16},{24,28},{28,24},{32,36},... | collective-permute-start | bytes 786440 | tf_op jit(solution)/shard_map/ppermute | solution.py:326
  60.9 24.8 %collective-permute-start.17 = (bf16[1344,256]{1,0:T(8,128)(2,1)S(1)}, bf16[1344,256]{1,0:T(8,128)(2,1)S(1)}, u32[]{:S(2)}, u32[]{:S(2)}) collective-permute-start(bf16[1344,256]{1,0:T(8,128)(2,1)S(1)} %collective-permute-done.16.rest_4_), channel_id=1, source_target_pairs={{0,4},{4,0},{8,12},{12,8},{16,20},{20,16},{24,28},{28,24},{32,36},... | collective-permute-start | bytes 2064392 | tf_op jit(solution)/shard_map/ppermute | solution.py:326
  61.1 12.7 %collective-permute-start.12 = (bf16[512,256]{1,0:T(8,128)(2,1)S(1)}, bf16[512,256]{1,0:T(8,128)(2,1)S(1)}, u32[]{:S(2)}, u32[]{:S(2)}) collective-permute-start(bf16[512,256]{1,0:T(8,128)(2,1)S(1)} %shard_map.103), channel_id=1, source_target_pairs={{8,0},{12,4},{16,8},{20,12},{24,16},{28,20},{32,24},{36,28},{40,32... | collective-permute-start | bytes 786440 | tf_op jit(solution)/shard_map/ppermute | solution.py:329
  67.6 9.7 %collective-permute-start.13 = (bf16[512,256]{1,0:T(8,128)(2,1)S(1)}, bf16[512,256]{1,0:T(8,128)(2,1)S(1)}, u32[]{:S(2)}, u32[]{:S(2)}) collective-permute-start(bf16[512,256]{1,0:T(8,128)(2,1)S(1)} %shard_map.102.own0), channel_id=1, source_target_pairs={{0,1},{1,2},{2,3},{3,0},{4,5},{5,6},{6,7},{7,4},{8,9},{9,10},{10,1... | collective-permute-start | bytes 786440 | tf_op jit(solution)/shard_map/ppermute | solution.py:344
  69.2 15.7 %collective-permute-start.14 = (bf16[512,256]{1,0:T(8,128)(2,1)S(1)}, bf16[512,256]{1,0:T(8,128)(2,1)S(1)}, u32[]{:S(2)}, u32[]{:S(2)}) collective-permute-start(bf16[512,256]{1,0:T(8,128)(2,1)S(1)} %shard_map.102.own0), channel_id=1, source_target_pairs={{0,2},{1,3},{2,0},{3,1},{4,6},{5,7},{6,4},{7,5},{8,10},{9,11},{10,... | collective-permute-start | bytes 786440 | tf_op jit(solution)/shard_map/ppermute | solution.py:344
  72.1 13.6 %collective-permute-start.15 = (bf16[512,256]{1,0:T(8,128)(2,1)S(1)}, bf16[512,256]{1,0:T(8,128)(2,1)S(1)}, u32[]{:S(2)}, u32[]{:S(2)}) collective-permute-start(bf16[512,256]{1,0:T(8,128)(2,1)S(1)} %shard_map.102.own0), channel_id=1, source_target_pairs={{0,3},{1,0},{2,1},{3,2},{4,7},{5,4},{6,5},{7,6},{8,11},{9,8},{10,9... | collective-permute-start | bytes 786440 | tf_op jit(solution)/shard_map/ppermute | solution.py:344
  74.6 14.8 %collective-permute-start.18 = (bf16[512,256]{1,0:T(8,128)(2,1)S(1)}, bf16[512,256]{1,0:T(8,128)(2,1)S(1)}, u32[]{:S(2)}, u32[]{:S(2)}) collective-permute-start(bf16[512,256]{1,0:T(8,128)(2,1)S(1)} %shard_map.104.own1), channel_id=1, source_target_pairs={{0,1},{1,2},{2,3},{3,0},{4,5},{5,6},{6,7},{7,4},{8,9},{9,10},{10,1... | collective-permute-start | bytes 786440 | tf_op jit(solution)/shard_map/ppermute | solution.py:344
  77.4 18.1 %collective-permute-start.19 = (bf16[512,256]{1,0:T(8,128)(2,1)S(1)}, bf16[512,256]{1,0:T(8,128)(2,1)S(1)}, u32[]{:S(2)}, u32[]{:S(2)}) collective-permute-start(bf16[512,256]{1,0:T(8,128)(2,1)S(1)} %shard_map.104.own1), channel_id=1, source_target_pairs={{0,2},{1,3},{2,0},{3,1},{4,6},{5,7},{6,4},{7,5},{8,10},{9,11},{10,... | collective-permute-start | bytes 786440 | tf_op jit(solution)/shard_map/ppermute | solution.py:344
  84.9 10.5 %collective-permute-start.20 = (bf16[512,256]{1,0:T(8,128)(2,1)S(1)}, bf16[512,256]{1,0:T(8,128)(2,1)S(1)}, u32[]{:S(2)}, u32[]{:S(2)}) collective-permute-start(bf16[512,256]{1,0:T(8,128)(2,1)S(1)} %shard_map.104.own1), channel_id=1, source_target_pairs={{0,3},{1,0},{2,1},{3,2},{4,7},{5,4},{6,5},{7,6},{8,11},{9,8},{10,9... | collective-permute-start | bytes 786440 | tf_op jit(solution)/shard_map/ppermute | solution.py:344
  (8 other events, 54.9 us)

commit v4 on v3

--- a/solution.py
+++ b/solution.py
@@ -74,22 +74,27 @@
                 total_out[:, lanes] = jnp.broadcast_to(total, (8, HEAD_SIZE))
 
 
-def cut_kernel(index, group, key_matrix, value_matrix, ready, sent1, sent2, sent3, rows, arrivals, departures):
+def cut_kernel(index, group, key_matrix, value_matrix, ready, near, far, near_rows, far_rows, arrivals, departures):
     half = HALF_ROWS
     core = index[0] & 1
+    begins = (
+        pl.multiple_of(((group[0] + 1 + 2 * core) & 3) * (2 * half), 16),
+        pl.multiple_of(((group[0] + 2) & 3) * (2 * half) + core * half, 16),
+    )
     incoming, outgoing = [], []
-    for at, (steps, target) in enumerate(((1, sent1), (3, sent3), (2, sent2))):
-        begin = pl.multiple_of(((group[0] + steps) & 3) * (2 * half) + core * half, 16)
+    for at, (begin, count, kept, target) in enumerate(
+        ((begins[0], 2 * half, near_rows, near), (begins[1], half, far_rows, far))
+    ):
         for part, matrix in enumerate((key_matrix, value_matrix)):
             incoming.append(
                 pltpu.make_async_copy(
-                    matrix.at[pl.ds(begin, half), :], rows.at[at, pl.ds(part * half, half), :], arrivals.at[2 * at + part]
+                    matrix.at[pl.ds(begin, count), :], kept.at[pl.ds(part * count, count), :], arrivals.at[2 * at + part]
                 )
             )
-        outgoing.append(pltpu.make_async_copy(rows.at[at], target, departures.at[at]))
+        outgoing.append(pltpu.make_async_copy(kept, target, departures.at[at]))
     for copy in incoming:
         copy.start()
-    for at in range(3):
+    for at in range(2):
         incoming[2 * at].wait()
         incoming[2 * at + 1].wait()
         outgoing[at].start()
@@ -255,23 +260,34 @@
             out[at] = (total * factor_of(exponents[head, block])).astype(jnp.bfloat16)
 
 
-def remote_part(place, head, half_at, pieces, mine, other):
+def remote_parts(place, head, pieces, matrices):
+    before, opposite, after = pieces
+    near, other_near, far, other_far = matrices
     half = HALF_ROWS
+    core = place[0] & 1
+    even = jnp.broadcast_to(core == 0, before.shape)
     lanes = slice(head * HEAD_SIZE, (head + 1) * HEAD_SIZE)
-    parts = []
-    for matrix in mine if half_at == 0 else other:
-        parts += [matrix[0:half, lanes], matrix[half : 2 * half, lanes]]
-    return product(jnp.concatenate(parts, axis=1), jnp.concatenate([piece[...] for piece in pieces], axis=1), NT)
-
-
-def half_slice(place, half_at):
-    core = place[0] & 1
-    at = core if half_at == 0 else 1 - core
-    return pl.ds(pl.multiple_of(at * HALF_ROWS, 16), HALF_ROWS)
+    first, second = before[...].astype(jnp.float32), after[...].astype(jnp.float32)
+    channels = jnp.concatenate(
+        [
+            jnp.where(even, first, second).astype(jnp.bfloat16),
+            jnp.where(even, second, first).astype(jnp.bfloat16),
+            opposite[...],
+        ],
+        axis=1,
+    )
+    for at, opposite_rows in ((core, far), (1 - core, other_far)):
+        begin = pl.multiple_of(at * half, 16)
+        parts = []
+        for matrix in (near, other_near):
+            for part in range(2):
+                parts.append(matrix[pl.ds(pl.multiple_of(part * 2 * half + begin, 16), half), lanes])
+        parts += [opposite_rows[0:half, lanes], opposite_rows[half : 2 * half, lanes]]
+        yield pl.ds(begin, half), product(jnp.concatenate(parts, axis=1), channels, NT)
 
 
 def early_kernel(place, group, keys, values, own0, own1, *rest):
-    pieces, mine, other, out, rows, arrivals = rest[:3], rest[3:6], rest[6:9], rest[9], rest[10], rest[11]
+    pieces, matrices, out, rows, arrivals = rest[:3], rest[3:7], rest[7], rest[8], rest[9]
     begin = pl.multiple_of(group[0] * (2 * HALF_ROWS), 16)
     copies = [
         pltpu.make_async_copy(matrix.at[pl.ds(begin, 2 * HALF_ROWS), :], rows.at[part], arrivals.at[part])
@@ -279,8 +295,8 @@
     ]
     for copy in copies:
         copy.start()
-    for half_at in range(2):
-        out[half_slice(place, half_at), :] = remote_part(place, 0, half_at, pieces, mine, other)
+    for at, part in remote_parts(place, 0, pieces, matrices):
+        out[at, :] = part
     for copy in copies:
         copy.wait()
     channels = jnp.concatenate(
@@ -292,10 +308,9 @@
 
 
 def late_kernel(place, early, *rest):
-    pieces, mine, other, out = rest[:3], rest[3:6], rest[6:9], rest[9]
-    for half_at in range(2):
-        rows = half_slice(place, half_at)
-        out[rows, :] = (early[rows, :] + remote_part(place, 1, half_at, pieces, mine, other)).astype(out.dtype)
+    pieces, matrices, out = rest[:3], rest[3:7], rest[7]
+    for at, part in remote_parts(place, 1, pieces, matrices):
+        out[at, :] = (early[at, :] + part).astype(out.dtype)
 
 
 def prepare_kernel(queries, grads, ready, query_out, grad_out, grad_cols):
@@ -328,9 +343,11 @@
     def onward(value, steps):
         return lax.ppermute(value, "seq", shift_pairs(count, steps))
 
+    def along_head(value, steps):
+        return lax.ppermute(value, "head", [(at, (at + steps) % groups) for at in range(groups)])
+
     key_exponents, value_exponents = key_exponents.T, value_exponents.T
     model_rows = key_matrix.shape[0] // groups
-    piece_shape = shape_of(model_rows, 256)
     exact_keys, exact_values, key_total = vmem_call(
         dequantize_kernel,
         (shape_of(BLOCK, 256), shape_of(BLOCK, 256), shape_of(8, 256, jnp.float32)),
@@ -340,29 +357,34 @@
     older_keys = onward(exact_keys, 2)
     last_total = onward(key_total, 1)
 
-    def along_head(value, steps):
-        return lax.ppermute(value, "head", [(at, (at + steps) % groups) for at in range(groups)])
-
-
+
+    near_sent, far_sent = pl.pallas_call(
+        cut_kernel,
+        out_shape=(shape_of(2 * model_rows, 256), shape_of(model_rows, 256)),
+        in_specs=[SMEM, SMEM, HBM, HBM, pl.BlockSpec(memory_space=pl.ANY)],
+        out_specs=(HBM,) * 2,
+        scratch_shapes=[
+            pltpu.VMEM((2 * model_rows, 256), jnp.bfloat16),
+            pltpu.VMEM((model_rows, 256), jnp.bfloat16),
+            pltpu.SemaphoreType.DMA((4,)),
+            pltpu.SemaphoreType.DMA((2,)),
+        ],
+        cost_estimate=pl.CostEstimate(flops=1, bytes_accessed=1, transcendentals=0),
+        compiler_params=pltpu.CompilerParams(vmem_limit_bytes=CUT_LIMIT * MEBI),
+    )(place, group, key_matrix, value_matrix, keys)
+    near_pairs = [
+        (at * groups + there, at * groups + (there + (1 if at % 2 == 0 else groups - 1)) % groups)
+        for at in range(count)
+        for there in range(groups)
+    ]
     older_values = onward(exact_values, 2)
     smooth = vmem_call(
         smooth_kernel, shape_of(BLOCK, 256), (place, exact_keys, older_keys, last_total), in_specs=[SMEM, VMEM, VMEM, VMEM]
     )
     older_smooth = onward(smooth, 2)
-    sent = pl.pallas_call(
-        cut_kernel,
-        out_shape=(piece_shape,) * 3,
-        in_specs=[SMEM, SMEM, HBM, HBM, pl.BlockSpec(memory_space=pl.ANY)],
-        out_specs=(HBM,) * 3,
-        scratch_shapes=[
-            pltpu.VMEM((3, model_rows, 256), jnp.bfloat16),
-            pltpu.SemaphoreType.DMA((6,)),
-            pltpu.SemaphoreType.DMA((3,)),
-        ],
-        cost_estimate=pl.CostEstimate(flops=1, bytes_accessed=1, transcendentals=0),
-        compiler_params=pltpu.CompilerParams(vmem_limit_bytes=CUT_LIMIT * MEBI),
-    )(place, group, key_matrix, value_matrix, smooth)
-    fetched = [along_head(piece, steps) for steps, piece in zip((1, 2, 3), sent)]
+    near = lax.ppermute(near_sent, ("seq", "head"), near_pairs)
+    far = along_head(far_sent, 2)
+
     last = to_sibling(
         jnp.where(
             core == 0,
@@ -381,14 +403,14 @@
     query_grads, gathered = [], []
     for head in range(2):
         if head == 1:
-            queries, _, swapped[0], swapped[2] = lax.optimization_barrier((queries, back, swapped[0], swapped[2]))
+            queries, _, other_near = lax.optimization_barrier((queries, back, other_near))
         query_part, grad2, grad1, grad0 = attend_call(
             head, place, queries, output_gradient, grad_cols, older_smooth, last, smooth, older_values, exact_values
         )
         query_grads.append(query_part)
         if head == 0:
-            fetched[0], fetched[2], _ = lax.optimization_barrier((fetched[0], fetched[2], grad1))
-            swapped = [to_sibling(fetched[0]), None, to_sibling(fetched[2])]
+            near_now, far, _ = lax.optimization_barrier((near, far, grad1))
+            other_near, other_far = to_sibling(near_now), to_sibling(far)
         sibling_grad = to_sibling(grad1)
         if head == 1:
             grad2, _ = lax.optimization_barrier((grad2, gathered[0][0]))
@@ -404,21 +426,20 @@
         for steps in (1, 2, 3):
             arrived.append(along_head(scaled, steps))
         gathered.append(arrived)
-    fetched[1], _ = lax.optimization_barrier((fetched[1], back))
-    swapped[1] = to_sibling(fetched[1])
+    fetched = (near, other_near, far, other_far)
     early = vmem_call(
         early_kernel,
         shape_of(model_rows, BLOCK, jnp.float32),
-        (place, group, key_matrix, value_matrix, gathered[0][0], gathered[1][0], *gathered[0][1:], *fetched, *swapped),
-        in_specs=[SMEM, SMEM, HBM, HBM] + [VMEM] * 11,
+        (place, group, key_matrix, value_matrix, gathered[0][0], gathered[1][0], *gathered[0][1:], *fetched),
+        in_specs=[SMEM, SMEM, HBM, HBM] + [VMEM] * 9,
         scratch=[pltpu.VMEM((2, model_rows, 256), jnp.bfloat16), pltpu.SemaphoreType.DMA((2,))],
         mebibytes=18,
     )
     input_grad = vmem_call(
         late_kernel,
         shape_of(model_rows, BLOCK),
-        (place, early, *gathered[1][1:], *fetched, *swapped),
-        in_specs=[SMEM] + [VMEM] * 10,
+        (place, early, *gathered[1][1:], *fetched),
+        in_specs=[SMEM] + [VMEM] * 8,
         mebibytes=18,
     )
     return jnp.concatenate(query_grads, axis=1), input_grad

time: 98.3 us -> 95.1 us (0.967)
  waiting for transfers between devices: 28.4 us -> 39.2 us
  starting transfers between devices: 40.3 us -> 33.4 us
  local copies, waits for them, and re-layouts: 3.29 us -> 0.03 us
  Pallas kernels: 22.9 us -> 20.4 us
    ppermute x9 -> x7, starting transfers between devices: 15 us -> 4.29 us  [along_head(): lax.ppermute(value, 'head', [(at, (at + steps) % groups) for at in range(...]
    ppermute x6, waiting for transfers between devices: 9.87 us -> 17.4 us  [onward(): return lax.ppermute(value, 'seq', shift_pairs(count, steps))]
    unnamed x22 -> x16, local copies, waits for them, and re-layouts: 3.29 us -> 0.03 us
    pallas_call x11, Pallas kernels: 20.4 us -> 17.7 us  [vmem_call(): pl.pallas_call(kernel, out_shape=out_shapes, in_specs=in_specs if in_spec...]
    ppermute x9 -> x7, waiting for transfers between devices: 14.7 us -> 17.3 us  [along_head(): lax.ppermute(value, 'head', [(at, (at + steps) % groups) for at in range(...]
    ppermute x6, starting transfers between devices: 24.4 us -> 26.3 us  [onward(): return lax.ppermute(value, 'seq', shift_pairs(count, steps))]
    ppermute x0 -> x1, starting transfers between devices: none -> 1.57 us  [local(): near = lax.ppermute(near_sent, ('seq', 'head'), near_pairs)]
    ppermute x6 -> x5, waiting for transfers between devices: 3.85 us -> 4.55 us  [to_sibling(): return lax.ppermute(value, 'seq', siblings)]
  transfers between devices with their start and end apart: 21 -> 19, of which waited for: 12 -> 12; matrix products, arithmetic and copies ran while one was open for 2% -> 1% of each run, Pallas kernels for 20% -> 16%
where the time goes in v4:
time: 95.1 us; the launch traced here: 94.9 us
  waiting for transfers between devices  39.2 us (41%)
  starting transfers between devices  33.4 us (35%)
  Pallas kernels  20.4 us (21%)
    ppermute x6, starting transfers between devices, onward(): return lax.ppermute(value, 'seq', shift_pairs(count, steps))  26.3 us
    pallas_call x11, Pallas kernels, vmem_call(): pl.pallas_call(kernel, out_shape=out_shapes, in_specs=in_specs if in_spec...  17.7 us
    ppermute x6, waiting for transfers between devices, onward(): return lax.ppermute(value, 'seq', shift_pairs(count, steps))  17.4 us
    ppermute x7, waiting for transfers between devices, along_head(): lax.ppermute(value, 'head', [(at, (at + steps) % groups) for at in range(...  17.3 us
    ppermute x5, waiting for transfers between devices, to_sibling(): return lax.ppermute(value, 'seq', siblings)  4.55 us
    ppermute x7, starting transfers between devices, along_head(): lax.ppermute(value, 'head', [(at, (at + steps) % groups) for at in range(...  4.29 us
    pallas_call x1, Pallas kernels, local(): pl.pallas_call(cut_kernel, out_shape=(shape_of(2 * model_rows, 256), shap...  2.71 us
  transfers between devices with their start and end apart: 19, of which 12 were waited for; matrix products, arithmetic and copies ran while one was open for 1% of the time, Pallas kernels for 16%

profile of v4, /device:TPU:128, one launch (start us, length us, event | category | flops | bytes accessed | tf_op | source)
XLA Modules:
  0.0 94.9 jit_solution(10949278606120645542)
XLA Ops:
  0.7 2.7 %shard_map.100 = (bf16[2688,256]{1,0:T(8,128)(2,1)}, bf16[1344,256]{1,0:T(8,128)(2,1)}) custom-call(s32[1]{0:T(128)} %bitcast.place.index, s32[1]{0:T(128)} %bitcast.3.group, bf16[5376,256]{1,0:T(8,128)(2,1)} %keys.3, bf16[5376,256]{1,0:T(8,128)(2,1)} %values.3, bf16[512,256]{1,0:T(8,128)(2,1)} %ready.1), custom_call_target="tpu_custom_call" | custom-call | flops 1 | bytes 1 | tf_op jit(solution)/shard_map/pallas_call | solution.py:361
  3.4 1.6 %collective-permute-start.6 = (bf16[2688,256]{1,0:T(8,128)(2,1)}, bf16[2688,256]{1,0:T(8,128)(2,1)S(1)}, u32[]{:S(2)}, u32[]{:S(2)}) collective-permute-start(bf16[2688,256]{1,0:T(8,128)(2,1)} %get-tuple-element.32), channel_id=1, source_target_pairs={{0,1},{1,2},{2,3},{3,0},{4,7},{5,4},{6,5},{7,6},{8,9},{9,10},{10,1... | collective-permute-start | bytes 4128776 | tf_op jit(solution)/shard_map/ppermute | solution.py:385
  5.7 3.5 %collective-permute-start = (bf16[512,256]{1,0:T(8,128)(2,1)S(1)}, bf16[512,256]{1,0:T(8,128)(2,1)S(1)}, u32[]{:S(2)}, u32[]{:S(2)}) collective-permute-start(bf16[512,256]{1,0:T(8,128)(2,1)S(1)} %get-tuple-element.23.own), channel_id=1, source_target_pairs={{0,8},{4,12},{8,16},{12,20},{16,24},{20,28},{24,32},{28,36},{32,40... | collective-permute-start | bytes 786440 | tf_op jit(solution)/shard_map/ppermute | solution.py:344
  9.2 2.5 %collective-permute-start.1 = (f32[8,256]{1,0:T(8,128)S(1)}, f32[8,256]{1,0:T(8,128)S(1)}, u32[]{:S(2)}, u32[]{:S(2)}) collective-permute-start(f32[8,256]{1,0:T(8,128)S(1)} %get-tuple-element.24), channel_id=1, source_target_pairs={{0,4},{4,8},{8,12},{12,16},{16,20},{20,24},{24,28},{28,32},{32,36}... | collective-permute-start | bytes 24584 | tf_op jit(solution)/shard_map/ppermute | solution.py:344
  11.6 3.5 %collective-permute-start.3 = (bf16[512,256]{1,0:T(8,128)(2,1)S(1)}, bf16[512,256]{1,0:T(8,128)(2,1)S(1)}, u32[]{:S(2)}, u32[]{:S(2)}) collective-permute-start(bf16[512,256]{1,0:T(8,128)(2,1)S(1)} %get-tuple-element.28.values0), channel_id=1, source_target_pairs={{0,8},{4,12},{8,16},{12,20},{16,24},{20,28},{24,32},{28,36},{32,40... | collective-permute-start | bytes 786440 | tf_op jit(solution)/shard_map/ppermute | solution.py:344
  15.1 4.8 %collective-permute-done.1.total = f32[8,256]{1,0:T(8,128)S(1)} collective-permute-done((f32[8,256]{1,0:T(8,128)S(1)}, f32[8,256]{1,0:T(8,128)S(1)}, u32[]{:S(2)}, u32[]{:S(2)}) %collective-permute-start.1) | collective-permute-done | bytes 8224 | tf_op jit(solution)/shard_map/ppermute | solution.py:344
  20.5 1.9 %collective-permute-start.2 = (bf16[512,256]{1,0:T(8,128)(2,1)S(1)}, bf16[512,256]{1,0:T(8,128)(2,1)S(1)}, u32[]{:S(2)}, u32[]{:S(2)}) collective-permute-start(bf16[512,256]{1,0:T(8,128)(2,1)S(1)} %shard_map.96.ready.keys0), channel_id=1, source_target_pairs={{0,8},{4,12},{8,16},{12,20},{16,24},{20,28},{24,32},{28,36},{32,40... | collective-permute-start | bytes 786440 | tf_op jit(solution)/shard_map/ppermute | solution.py:344
  22.4 0.9 collective-permute-start.7
  23.3 2.6 %collective-permute-done.3.values2 = bf16[512,256]{1,0:T(8,128)(2,1)S(1)} collective-permute-done((bf16[512,256]{1,0:T(8,128)(2,1)S(1)}, bf16[512,256]{1,0:T(8,128)(2,1)S(1)}, u32[]{:S(2)}, u32[]{:S(2)}) %collective-permute-start.3) | collective-permute-done | bytes 262176 | tf_op jit(solution)/shard_map/ppermute | solution.py:344
  25.8 7.9 %collective-permute-done.2.keys2 = bf16[512,256]{1,0:T(8,128)(2,1)S(1)} collective-permute-done((bf16[512,256]{1,0:T(8,128)(2,1)S(1)}, bf16[512,256]{1,0:T(8,128)(2,1)S(1)}, u32[]{:S(2)}, u32[]{:S(2)}) %collective-permute-start.2) | collective-permute-done | bytes 262176 | tf_op jit(solution)/shard_map/ppermute | solution.py:344
  34.4 1.5 %collective-permute-done.4.last = bf16[512,512]{1,0:T(8,128)(2,1)S(1)} collective-permute-done((bf16[512,512]{1,0:T(8,128)(2,1)S(1)}, bf16[512,512]{1,0:T(8,128)(2,1)S(1)}, u32[]{:S(2)}, u32[]{:S(2)}) %collective-permute-start.4) | collective-permute-done | bytes 524320 | tf_op jit(solution)/shard_map/ppermute | solution.py:341
  35.9 4.7 %shard_map.98 = (bf16[512,256]{1,0:T(8,128)(2,1)S(1)}, f32[512,256]{1,0:T(8,128)S(1)}, bf16[512,256]{1,0:T(8,128)(2,1)S(1)}, f32[512,256]{1,0:T(8,128)S(1)}) custom-call(s32[1]{0:T(128)} %bitcast.place.index, bf16[512,512]{1,0:T(8,128)(2,1)S(1)} %get-tuple-element.35.queries, bf16[512,512]{1,0:T(8,128)(2,1)S(1)} %get-tuple-element.26.grads, ...), custom_call_target="tpu_custom_call" | custom-call | flops 1 | bytes 1 | tf_op jit(solution)/shard_map/pallas_call | solution.py:32
  41.9 3.0 %collective-permute-done.5.arrived.sibling = bf16[512,256]{1,0:T(8,128)(2,1)S(1)} collective-permute-done((bf16[512,256]{1,0:T(8,128)(2,1)S(1)}, bf16[512,256]{1,0:T(8,128)(2,1)S(1)}, u32[]{:S(2)}, u32[]{:S(2)}) %collective-permute-start.5) | collective-permute-done | bytes 262176 | tf_op jit(solution)/shard_map/ppermute | solution.py:341
  45.0 7.1 %collective-permute-start.9 = (bf16[512,256]{1,0:T(8,128)(2,1)S(1)}, bf16[512,256]{1,0:T(8,128)(2,1)S(1)}, u32[]{:S(2)}, u32[]{:S(2)}) collective-permute-start(bf16[512,256]{1,0:T(8,128)(2,1)S(1)} %shard_map.99), channel_id=1, source_target_pairs={{8,0},{12,4},{16,8},{20,12},{24,16},{28,20},{32,24},{36,28},{40,32... | collective-permute-start | bytes 786440 | tf_op jit(solution)/shard_map/ppermute | solution.py:344
  52.2 4.8 %shard_map.101 = (bf16[512,256]{1,0:T(8,128)(2,1)S(1)}, f32[512,256]{1,0:T(8,128)S(1)}, bf16[512,256]{1,0:T(8,128)(2,1)S(1)}, f32[512,256]{1,0:T(8,128)S(1)}) custom-call(s32[1]{0:T(128)} %bitcast.place.index, bf16[512,512]{1,0:T(8,128)(2,1)S(1)} %get-tuple-element.35.queries, bf16[512,512]{1,0:T(8,128)(2,1)S(1)} %get-tuple-element.26.grads, ...), custom_call_target="tpu_custom_call" | custom-call | flops 1 | bytes 1 | tf_op jit(solution)/shard_map/pallas_call | solution.py:32
  58.6 7.8 %collective-permute-start.11 = (bf16[512,256]{1,0:T(8,128)(2,1)S(1)}, bf16[512,256]{1,0:T(8,128)(2,1)S(1)}, u32[]{:S(2)}, u32[]{:S(2)}) collective-permute-start(bf16[512,256]{1,0:T(8,128)(2,1)S(1)} %shard_map.103), channel_id=1, source_target_pairs={{8,0},{12,4},{16,8},{20,12},{24,16},{28,20},{32,24},{36,28},{40,32... | collective-permute-start | bytes 786440 | tf_op jit(solution)/shard_map/ppermute | solution.py:344
  66.5 1.4 %collective-permute-start.13 = (bf16[512,256]{1,0:T(8,128)(2,1)S(1)}, bf16[512,256]{1,0:T(8,128)(2,1)S(1)}, u32[]{:S(2)}, u32[]{:S(2)}) collective-permute-start(bf16[512,256]{1,0:T(8,128)(2,1)S(1)} %shard_map.102.own0), channel_id=1, source_target_pairs={{0,2},{1,3},{2,0},{3,1},{4,6},{5,7},{6,4},{7,5},{8,10},{9,11},{10,... | collective-permute-start | bytes 786440 | tf_op jit(solution)/shard_map/ppermute | solution.py:347
  67.9 1.9 %collective-permute-start.14 = (bf16[512,256]{1,0:T(8,128)(2,1)S(1)}, bf16[512,256]{1,0:T(8,128)(2,1)S(1)}, u32[]{:S(2)}, u32[]{:S(2)}) collective-permute-start(bf16[512,256]{1,0:T(8,128)(2,1)S(1)} %shard_map.102.own0), channel_id=1, source_target_pairs={{0,3},{1,0},{2,1},{3,2},{4,7},{5,4},{6,5},{7,6},{8,11},{9,8},{10,9... | collective-permute-start | bytes 786440 | tf_op jit(solution)/shard_map/ppermute | solution.py:347
  69.8 1.7 %collective-permute-done.11.later = bf16[512,256]{1,0:T(8,128)(2,1)S(1)} collective-permute-done((bf16[512,256]{1,0:T(8,128)(2,1)S(1)}, bf16[512,256]{1,0:T(8,128)(2,1)S(1)}, u32[]{:S(2)}, u32[]{:S(2)}) %collective-permute-start.11) | collective-permute-done | bytes 262176 | tf_op jit(solution)/shard_map/ppermute | solution.py:344
  72.2 10.4 %collective-permute-done.12.rest_0_ = bf16[512,256]{1,0:T(8,128)(2,1)S(1)} collective-permute-done((bf16[512,256]{1,0:T(8,128)(2,1)S(1)}, bf16[512,256]{1,0:T(8,128)(2,1)S(1)}, u32[]{:S(2)}, u32[]{:S(2)}) %collective-permute-start.12) | collective-permute-done | bytes 262176 | tf_op jit(solution)/shard_map/ppermute | solution.py:347
  82.6 0.8 pad_maximum_fusion
  83.5 2.8 %shard_map.105.early = f32[1344,512]{1,0:T(8,128)S(1)} custom-call(s32[1]{0:T(128)} %bitcast.place.index, s32[1]{0:T(128)} %bitcast.3.group, bf16[5376,256]{1,0:T(8,128)(2,1)S(1)} %copy-done, bf16[5376,256]{1,0:T(8,128)(2,1)S(1)} %copy-done.1, bf16[512,256]{1,0:T(8,128)(2,1)S(1)} %shard_map.102.own0, bf16[512,256]{1,0:T(8,128)(2,1)S(1)} %shard_map.104.own1, ...), custom_call_target="tpu_custom_call" | custom-call | flops 1 | bytes 1 | tf_op jit(solution)/shard_map/pallas_call | solution.py:32
  86.3 5.6 %collective-permute-done.16.rest_0_ = bf16[512,256]{1,0:T(8,128)(2,1)S(1)} collective-permute-done((bf16[512,256]{1,0:T(8,128)(2,1)S(1)}, bf16[512,256]{1,0:T(8,128)(2,1)S(1)}, u32[]{:S(2)}, u32[]{:S(2)}) %collective-permute-start.16) | collective-permute-done | bytes 262176 | tf_op jit(solution)/shard_map/ppermute | solution.py:347
  92.5 2.4 %shard_map.106 = bf16[1344,512]{1,0:T(8,128)(2,1)} custom-call(s32[1]{0:T(128)} %bitcast.place.index, f32[1344,512]{1,0:T(8,128)S(1)} %shard_map.105.early, bf16[512,256]{1,0:T(8,128)(2,1)S(1)} %collective-permute-done.16.rest_0_, bf16[512,256]{1,0:T(8,128)(2,1)S(1)} %collective-permute-done.17.rest_1_, ...), custom_call_target="tpu_custom_call" | custom-call | flops 1 | bytes 1 | tf_op jit(solution)/shard_map/pallas_call | solution.py:32
  (44 shorter events, 6.3 us)
Async XLA Ops:
  0.6 4.3 %copy-start.2 = (bf16[512,256]{1,0:T(8,128)(2,1)S(1)}, bf16[512,256]{1,0:T(8,128)(2,1)}, u32[]{:S(2)}) copy-start(bf16[512,256]{1,0:T(8,128)(2,1)} %ready.1) | copy-start | bytes 786436
  3.4 38.0 %collective-permute-start.6 = (bf16[2688,256]{1,0:T(8,128)(2,1)}, bf16[2688,256]{1,0:T(8,128)(2,1)S(1)}, u32[]{:S(2)}, u32[]{:S(2)}) collective-permute-start(bf16[2688,256]{1,0:T(8,128)(2,1)} %get-tuple-element.32), channel_id=1, source_target_pairs={{0,1},{1,2},{2,3},{3,0},{4,7},{5,4},{6,5},{7,6},{8,9},{9,10},{10,1... | collective-permute-start | bytes 4128776 | tf_op jit(solution)/shard_map/ppermute | solution.py:385
  5.7 14.3 %collective-permute-start = (bf16[512,256]{1,0:T(8,128)(2,1)S(1)}, bf16[512,256]{1,0:T(8,128)(2,1)S(1)}, u32[]{:S(2)}, u32[]{:S(2)}) collective-permute-start(bf16[512,256]{1,0:T(8,128)(2,1)S(1)} %get-tuple-element.23.own), channel_id=1, source_target_pairs={{0,8},{4,12},{8,16},{12,20},{16,24},{20,28},{24,32},{28,36},{32,40... | collective-permute-start | bytes 786440 | tf_op jit(solution)/shard_map/ppermute | solution.py:344
  9.2 10.8 %collective-permute-start.1 = (f32[8,256]{1,0:T(8,128)S(1)}, f32[8,256]{1,0:T(8,128)S(1)}, u32[]{:S(2)}, u32[]{:S(2)}) collective-permute-start(f32[8,256]{1,0:T(8,128)S(1)} %get-tuple-element.24), channel_id=1, source_target_pairs={{0,4},{4,8},{8,12},{12,16},{16,20},{20,24},{24,28},{28,32},{32,36}... | collective-permute-start | bytes 24584 | tf_op jit(solution)/shard_map/ppermute | solution.py:344
  11.6 14.2 %collective-permute-start.3 = (bf16[512,256]{1,0:T(8,128)(2,1)S(1)}, bf16[512,256]{1,0:T(8,128)(2,1)S(1)}, u32[]{:S(2)}, u32[]{:S(2)}) collective-permute-start(bf16[512,256]{1,0:T(8,128)(2,1)S(1)} %get-tuple-element.28.values0), channel_id=1, source_target_pairs={{0,8},{4,12},{8,16},{12,20},{16,24},{20,28},{24,32},{28,36},{32,40... | collective-permute-start | bytes 786440 | tf_op jit(solution)/shard_map/ppermute | solution.py:344
  20.5 13.3 %collective-permute-start.2 = (bf16[512,256]{1,0:T(8,128)(2,1)S(1)}, bf16[512,256]{1,0:T(8,128)(2,1)S(1)}, u32[]{:S(2)}, u32[]{:S(2)}) collective-permute-start(bf16[512,256]{1,0:T(8,128)(2,1)S(1)} %shard_map.96.ready.keys0), channel_id=1, source_target_pairs={{0,8},{4,12},{8,16},{12,20},{16,24},{20,28},{24,32},{28,36},{32,40... | collective-permute-start | bytes 786440 | tf_op jit(solution)/shard_map/ppermute | solution.py:344
  22.4 19.0 %collective-permute-start.7 = (bf16[1344,256]{1,0:T(8,128)(2,1)}, bf16[1344,256]{1,0:T(8,128)(2,1)S(1)}, u32[]{:S(2)}, u32[]{:S(2)}) collective-permute-start(bf16[1344,256]{1,0:T(8,128)(2,1)} %get-tuple-element.33), channel_id=1, source_target_pairs={{0,2},{1,3},{2,0},{3,1},{4,6},{5,7},{6,4},{7,5},{8,10},{9,11},{10,... | collective-permute-start | bytes 2064392 | tf_op jit(solution)/shard_map/ppermute | solution.py:347
  23.3 10.7 %copy-start.3 = (bf16[512,512]{1,0:T(8,128)(2,1)S(1)}, bf16[512,512]{1,0:T(8,128)(2,1)}, u32[]{:S(2)}) copy-start(bf16[512,512]{1,0:T(8,128)(2,1)} %queries.1) | copy-start | bytes 1572868
  23.3 10.7 %copy-start.4 = (bf16[512,512]{1,0:T(8,128)(2,1)S(1)}, bf16[512,512]{1,0:T(8,128)(2,1)}, u32[]{:S(2)}) copy-start(bf16[512,512]{1,0:T(8,128)(2,1)} %grads.1) | copy-start | bytes 1572868
  33.9 2.0 %collective-permute-start.4 = (bf16[512,512]{1,0:T(8,128)(2,1)S(1)}, bf16[512,512]{1,0:T(8,128)(2,1)S(1)}, u32[]{:S(2)}, u32[]{:S(2)}) collective-permute-start(bf16[512,512]{1,0:T(8,128)(2,1)S(1)} %maximum_select_fusion), channel_id=1, source_target_pairs={{0,4},{4,0},{8,12},{12,8},{16,20},{20,16},{24,28},{28,24},{32,36},... | collective-permute-start | bytes 1572872 | tf_op jit(solution)/shard_map/ppermute | solution.py:341
  41.4 10.7 %collective-permute-start.8 = (bf16[2688,256]{1,0:T(8,128)(2,1)S(1)}, bf16[2688,256]{1,0:T(8,128)(2,1)S(1)}, u32[]{:S(2)}, u32[]{:S(2)}) collective-permute-start(bf16[2688,256]{1,0:T(8,128)(2,1)S(1)} %collective-permute-done.6.rest_3_), channel_id=1, source_target_pairs={{0,4},{4,0},{8,12},{12,8},{16,20},{20,16},{24,28},{28,24},{32,36},... | collective-permute-start | bytes 4128776 | tf_op jit(solution)/shard_map/ppermute | solution.py:341
  41.4 3.5 %collective-permute-start.5 = (bf16[512,256]{1,0:T(8,128)(2,1)S(1)}, bf16[512,256]{1,0:T(8,128)(2,1)S(1)}, u32[]{:S(2)}, u32[]{:S(2)}) collective-permute-start(bf16[512,256]{1,0:T(8,128)(2,1)S(1)} %get-tuple-element.31), channel_id=1, source_target_pairs={{0,4},{4,0},{8,12},{12,8},{16,20},{20,16},{24,28},{28,24},{32,36},... | collective-permute-start | bytes 786440 | tf_op jit(solution)/shard_map/ppermute | solution.py:341
  45.0 12.8 %collective-permute-start.9 = (bf16[512,256]{1,0:T(8,128)(2,1)S(1)}, bf16[512,256]{1,0:T(8,128)(2,1)S(1)}, u32[]{:S(2)}, u32[]{:S(2)}) collective-permute-start(bf16[512,256]{1,0:T(8,128)(2,1)S(1)} %shard_map.99), channel_id=1, source_target_pairs={{8,0},{12,4},{16,8},{20,12},{24,16},{28,20},{32,24},{36,28},{40,32... | collective-permute-start | bytes 786440 | tf_op jit(solution)/shard_map/ppermute | solution.py:344
  52.2 31.3 %copy-start.1 = (bf16[5376,256]{1,0:T(8,128)(2,1)S(1)}, bf16[5376,256]{1,0:T(8,128)(2,1)}, u32[]{:S(2)}) copy-start(bf16[5376,256]{1,0:T(8,128)(2,1)} %values.3) | copy-start | bytes 8257540
  56.9 1.6 %collective-permute-start.10 = (bf16[512,256]{1,0:T(8,128)(2,1)S(1)}, bf16[512,256]{1,0:T(8,128)(2,1)S(1)}, u32[]{:S(2)}, u32[]{:S(2)}) collective-permute-start(bf16[512,256]{1,0:T(8,128)(2,1)S(1)} %get-tuple-element.39), channel_id=1, source_target_pairs={{0,4},{4,0},{8,12},{12,8},{16,20},{20,16},{24,28},{28,24},{32,36},... | collective-permute-start | bytes 786440 | tf_op jit(solution)/shard_map/ppermute | solution.py:341
  57.0 26.5 %collective-permute-start.15 = (bf16[1344,256]{1,0:T(8,128)(2,1)S(1)}, bf16[1344,256]{1,0:T(8,128)(2,1)S(1)}, u32[]{:S(2)}, u32[]{:S(2)}) collective-permute-start(bf16[1344,256]{1,0:T(8,128)(2,1)S(1)} %collective-permute-done.7.rest_5_), channel_id=1, source_target_pairs={{0,4},{4,0},{8,12},{12,8},{16,20},{20,16},{24,28},{28,24},{32,36},... | collective-permute-start | bytes 2064392 | tf_op jit(solution)/shard_map/ppermute | solution.py:341
  58.5 24.9 %copy-start = (bf16[5376,256]{1,0:T(8,128)(2,1)S(1)}, bf16[5376,256]{1,0:T(8,128)(2,1)}, u32[]{:S(2)}) copy-start(bf16[5376,256]{1,0:T(8,128)(2,1)} %keys.3) | copy-start | bytes 8257540
  58.6 12.9 %collective-permute-start.11 = (bf16[512,256]{1,0:T(8,128)(2,1)S(1)}, bf16[512,256]{1,0:T(8,128)(2,1)S(1)}, u32[]{:S(2)}, u32[]{:S(2)}) collective-permute-start(bf16[512,256]{1,0:T(8,128)(2,1)S(1)} %shard_map.103), channel_id=1, source_target_pairs={{8,0},{12,4},{16,8},{20,12},{24,16},{28,20},{32,24},{36,28},{40,32... | collective-permute-start | bytes 786440 | tf_op jit(solution)/shard_map/ppermute | solution.py:344
  66.5 16.2 %collective-permute-start.12 = (bf16[512,256]{1,0:T(8,128)(2,1)S(1)}, bf16[512,256]{1,0:T(8,128)(2,1)S(1)}, u32[]{:S(2)}, u32[]{:S(2)}) collective-permute-start(bf16[512,256]{1,0:T(8,128)(2,1)S(1)} %shard_map.102.own0), channel_id=1, source_target_pairs={{0,1},{1,2},{2,3},{3,0},{4,5},{5,6},{6,7},{7,4},{8,9},{9,10},{10,1... | collective-permute-start | bytes 786440 | tf_op jit(solution)/shard_map/ppermute | solution.py:347
  66.5 16.1 %collective-permute-start.13 = (bf16[512,256]{1,0:T(8,128)(2,1)S(1)}, bf16[512,256]{1,0:T(8,128)(2,1)S(1)}, u32[]{:S(2)}, u32[]{:S(2)}) collective-permute-start(bf16[512,256]{1,0:T(8,128)(2,1)S(1)} %shard_map.102.own0), channel_id=1, source_target_pairs={{0,2},{1,3},{2,0},{3,1},{4,6},{5,7},{6,4},{7,5},{8,10},{9,11},{10,... | collective-permute-start | bytes 786440 | tf_op jit(solution)/shard_map/ppermute | solution.py:347
  67.9 15.6 %collective-permute-start.14 = (bf16[512,256]{1,0:T(8,128)(2,1)S(1)}, bf16[512,256]{1,0:T(8,128)(2,1)S(1)}, u32[]{:S(2)}, u32[]{:S(2)}) collective-permute-start(bf16[512,256]{1,0:T(8,128)(2,1)S(1)} %shard_map.102.own0), channel_id=1, source_target_pairs={{0,3},{1,0},{2,1},{3,2},{4,7},{5,4},{6,5},{7,6},{8,11},{9,8},{10,9... | collective-permute-start | bytes 786440 | tf_op jit(solution)/shard_map/ppermute | solution.py:347
  72.2 19.7 %collective-permute-start.16 = (bf16[512,256]{1,0:T(8,128)(2,1)S(1)}, bf16[512,256]{1,0:T(8,128)(2,1)S(1)}, u32[]{:S(2)}, u32[]{:S(2)}) collective-permute-start(bf16[512,256]{1,0:T(8,128)(2,1)S(1)} %shard_map.104.own1), channel_id=1, source_target_pairs={{0,1},{1,2},{2,3},{3,0},{4,5},{5,6},{6,7},{7,4},{8,9},{9,10},{10,1... | collective-permute-start | bytes 786440 | tf_op jit(solution)/shard_map/ppermute | solution.py:347
  82.6 9.2 %collective-permute-start.17 = (bf16[512,256]{1,0:T(8,128)(2,1)S(1)}, bf16[512,256]{1,0:T(8,128)(2,1)S(1)}, u32[]{:S(2)}, u32[]{:S(2)}) collective-permute-start(bf16[512,256]{1,0:T(8,128)(2,1)S(1)} %shard_map.104.own1), channel_id=1, source_target_pairs={{0,2},{1,3},{2,0},{3,1},{4,6},{5,7},{6,4},{7,5},{8,10},{9,11},{10,... | collective-permute-start | bytes 786440 | tf_op jit(solution)/shard_map/ppermute | solution.py:347
  82.6 9.8 %collective-permute-start.18 = (bf16[512,256]{1,0:T(8,128)(2,1)S(1)}, bf16[512,256]{1,0:T(8,128)(2,1)S(1)}, u32[]{:S(2)}, u32[]{:S(2)}) collective-permute-start(bf16[512,256]{1,0:T(8,128)(2,1)S(1)} %shard_map.104.own1), channel_id=1, source_target_pairs={{0,3},{1,0},{2,1},{3,2},{4,7},{5,4},{6,5},{7,6},{8,11},{9,8},{10,9... | collective-permute-start | bytes 786440 | tf_op jit(solution)/shard_map/ppermute | solution.py:347
  (3 other events, 13.0 us)

commit v5 on v4

--- a/solution.py
+++ b/solution.py
@@ -383,7 +383,6 @@
     )
     older_smooth = onward(smooth, 2)
     near = lax.ppermute(near_sent, ("seq", "head"), near_pairs)
-    far = along_head(far_sent, 2)
 
     last = to_sibling(
         jnp.where(
@@ -400,6 +399,7 @@
         in_specs=[VMEM, VMEM, pl.BlockSpec(memory_space=pl.ANY)],
     )
 
+    queries, near, _ = lax.optimization_barrier((queries, near, smooth))
     query_grads, gathered = [], []
     for head in range(2):
         if head == 1:
@@ -409,12 +409,14 @@
         )
         query_grads.append(query_part)
         if head == 0:
-            near_now, far, _ = lax.optimization_barrier((near, far, grad1))
-            other_near, other_far = to_sibling(near_now), to_sibling(far)
+            far = along_head(lax.optimization_barrier((far_sent, grad1))[0], 2)
         sibling_grad = to_sibling(grad1)
         if head == 1:
             grad2, _ = lax.optimization_barrier((grad2, gathered[0][0]))
         back = vmem_call(merge_kernel, shape_of(BLOCK, 256), (place, grad2, sibling_grad), in_specs=[SMEM, VMEM, VMEM])
+        if head == 0:
+            back, near_now = lax.optimization_barrier((back, near))
+            other_near = to_sibling(near_now)
         later_grad = onward(back, -2)
         scaled = vmem_call(
             functools.partial(finish_kernel, head),
@@ -426,7 +428,8 @@
         for steps in (1, 2, 3):
             arrived.append(along_head(scaled, steps))
         gathered.append(arrived)
-    fetched = (near, other_near, far, other_far)
+    far, _ = lax.optimization_barrier((far, back))
+    fetched = (near, other_near, far, to_sibling(far))
     early = vmem_call(
         early_kernel,
         shape_of(model_rows, BLOCK, jnp.float32),

time: 95.1 us -> 94.1 us (0.989)
  starting transfers between devices: 33.4 us -> 21.3 us
  waiting for transfers between devices: 39.2 us -> 50.1 us
    ppermute x6, starting transfers between devices: 26.3 us -> 15.4 us  [onward(): return lax.ppermute(value, 'seq', shift_pairs(count, steps))]
    ppermute x6, waiting for transfers between devices: 17.4 us -> 24.1 us  [onward(): return lax.ppermute(value, 'seq', shift_pairs(count, steps))]
    ppermute x7, waiting for transfers between devices: 17.3 us -> 22.4 us  [along_head(): lax.ppermute(value, 'head', [(at, (at + steps) % groups) for at in range(...]
  transfers between devices with their start and end apart: 19 -> 19, of which waited for: 12 -> 13; matrix products, arithmetic and copies ran while one was open for 1% -> 1% of each run, Pallas kernels for 16% -> 11%
where the time goes in v5:
time: 94.1 us; the launch traced here: 93.7 us
  waiting for transfers between devices  50.1 us (53%)
  starting transfers between devices  21.3 us (23%)
  Pallas kernels  20.4 us (22%)
  other arithmetic  0.95 us (1%)
    ppermute x6, waiting for transfers between devices, onward(): return lax.ppermute(value, 'seq', shift_pairs(count, steps))  24.1 us
    ppermute x7, waiting for transfers between devices, along_head(): lax.ppermute(value, 'head', [(at, (at + steps) % groups) for at in range(...  22.4 us
    pallas_call x11, Pallas kernels, vmem_call(): pl.pallas_call(kernel, out_shape=out_shapes, in_specs=in_specs if in_spec...  17.7 us
    ppermute x6, starting transfers between devices, onward(): return lax.ppermute(value, 'seq', shift_pairs(count, steps))  15.4 us
    ppermute x5, waiting for transfers between devices, to_sibling(): return lax.ppermute(value, 'seq', siblings)  3.61 us
    ppermute x7, starting transfers between devices, along_head(): lax.ppermute(value, 'head', [(at, (at + steps) % groups) for at in range(...  3.49 us
    pallas_call x1, Pallas kernels, local(): pl.pallas_call(cut_kernel, out_shape=(shape_of(2 * model_rows, 256), shap...  2.71 us
  transfers between devices with their start and end apart: 19, of which 13 were waited for; matrix products, arithmetic and copies ran while one was open for 1% of the time, Pallas kernels for 11%

profile of v5, /device:TPU:128, one launch (start us, length us, event | category | flops | bytes accessed | tf_op | source)
XLA Modules:
  0.0 93.7 jit_solution(886016321701794731)
XLA Ops:
  0.7 2.7 %shard_map.98 = (bf16[2688,256]{1,0:T(8,128)(2,1)}, bf16[1344,256]{1,0:T(8,128)(2,1)}) custom-call(s32[1]{0:T(128)} %bitcast.place.index, s32[1]{0:T(128)} %bitcast.3.group, bf16[5376,256]{1,0:T(8,128)(2,1)} %keys.3, bf16[5376,256]{1,0:T(8,128)(2,1)} %values.3, bf16[512,256]{1,0:T(8,128)(2,1)} %ready.1), custom_call_target="tpu_custom_call" | custom-call | flops 1 | bytes 1 | tf_op jit(solution)/shard_map/pallas_call | solution.py:361
  3.4 1.6 %collective-permute-start.2 = (bf16[2688,256]{1,0:T(8,128)(2,1)}, bf16[2688,256]{1,0:T(8,128)(2,1)S(1)}, u32[]{:S(2)}, u32[]{:S(2)}) collective-permute-start(bf16[2688,256]{1,0:T(8,128)(2,1)} %get-tuple-element.30), channel_id=1, source_target_pairs={{0,1},{1,2},{2,3},{3,0},{4,7},{5,4},{6,5},{7,6},{8,9},{9,10},{10,1... | collective-permute-start | bytes 4128776 | tf_op jit(solution)/shard_map/ppermute | solution.py:385
  5.7 3.5 %collective-permute-start = (bf16[512,256]{1,0:T(8,128)(2,1)S(1)}, bf16[512,256]{1,0:T(8,128)(2,1)S(1)}, u32[]{:S(2)}, u32[]{:S(2)}) collective-permute-start(bf16[512,256]{1,0:T(8,128)(2,1)S(1)} %get-tuple-element.27.own), channel_id=1, source_target_pairs={{0,8},{4,12},{8,16},{12,20},{16,24},{20,28},{24,32},{28,36},{32,40... | collective-permute-start | bytes 786440 | tf_op jit(solution)/shard_map/ppermute | solution.py:344
  9.2 2.5 %collective-permute-start.1 = (f32[8,256]{1,0:T(8,128)S(1)}, f32[8,256]{1,0:T(8,128)S(1)}, u32[]{:S(2)}, u32[]{:S(2)}) collective-permute-start(f32[8,256]{1,0:T(8,128)S(1)} %get-tuple-element.28), channel_id=1, source_target_pairs={{0,4},{4,8},{8,12},{12,16},{16,20},{20,24},{24,28},{28,32},{32,36}... | collective-permute-start | bytes 24584 | tf_op jit(solution)/shard_map/ppermute | solution.py:344
  11.7 3.5 %collective-permute-start.4 = (bf16[512,256]{1,0:T(8,128)(2,1)S(1)}, bf16[512,256]{1,0:T(8,128)(2,1)S(1)}, u32[]{:S(2)}, u32[]{:S(2)}) collective-permute-start(bf16[512,256]{1,0:T(8,128)(2,1)S(1)} %get-tuple-element.34.values0), channel_id=1, source_target_pairs={{0,8},{4,12},{8,16},{12,20},{16,24},{20,28},{24,32},{28,36},{32,40... | collective-permute-start | bytes 786440 | tf_op jit(solution)/shard_map/ppermute | solution.py:344
  15.1 4.8 %collective-permute-done.1.total = f32[8,256]{1,0:T(8,128)S(1)} collective-permute-done((f32[8,256]{1,0:T(8,128)S(1)}, f32[8,256]{1,0:T(8,128)S(1)}, u32[]{:S(2)}, u32[]{:S(2)}) %collective-permute-start.1) | collective-permute-done | bytes 8224 | tf_op jit(solution)/shard_map/ppermute | solution.py:344
  20.5 1.9 %collective-permute-start.3 = (bf16[512,256]{1,0:T(8,128)(2,1)S(1)}, bf16[512,256]{1,0:T(8,128)(2,1)S(1)}, u32[]{:S(2)}, u32[]{:S(2)}) collective-permute-start(bf16[512,256]{1,0:T(8,128)(2,1)S(1)} %shard_map.96.ready.keys0), channel_id=1, source_target_pairs={{0,8},{4,12},{8,16},{12,20},{16,24},{20,28},{24,32},{28,36},{32,40... | collective-permute-start | bytes 786440 | tf_op jit(solution)/shard_map/ppermute | solution.py:344
  22.4 3.4 %collective-permute-done.4.values2 = bf16[512,256]{1,0:T(8,128)(2,1)S(1)} collective-permute-done((bf16[512,256]{1,0:T(8,128)(2,1)S(1)}, bf16[512,256]{1,0:T(8,128)(2,1)S(1)}, u32[]{:S(2)}, u32[]{:S(2)}) %collective-permute-start.4) | collective-permute-done | bytes 262176 | tf_op jit(solution)/shard_map/ppermute | solution.py:344
  25.9 7.9 %collective-permute-done.3.keys2 = bf16[512,256]{1,0:T(8,128)(2,1)S(1)} collective-permute-done((bf16[512,256]{1,0:T(8,128)(2,1)S(1)}, bf16[512,256]{1,0:T(8,128)(2,1)S(1)}, u32[]{:S(2)}, u32[]{:S(2)}) %collective-permute-start.3) | collective-permute-done | bytes 262176 | tf_op jit(solution)/shard_map/ppermute | solution.py:344
  34.4 1.5 %collective-permute-done.5.last = bf16[512,512]{1,0:T(8,128)(2,1)S(1)} collective-permute-done((bf16[512,512]{1,0:T(8,128)(2,1)S(1)}, bf16[512,512]{1,0:T(8,128)(2,1)S(1)}, u32[]{:S(2)}, u32[]{:S(2)}) %collective-permute-start.5) | collective-permute-done | bytes 524320 | tf_op jit(solution)/shard_map/ppermute | solution.py:341
  35.9 4.8 %shard_map.99 = (bf16[512,256]{1,0:T(8,128)(2,1)S(1)}, f32[512,256]{1,0:T(8,128)S(1)}, bf16[512,256]{1,0:T(8,128)(2,1)S(1)}, f32[512,256]{1,0:T(8,128)S(1)}) custom-call(s32[1]{0:T(128)} %bitcast.place.index, bf16[512,512]{1,0:T(8,128)(2,1)S(1)} %get-tuple-element.41.queries, bf16[512,512]{1,0:T(8,128)(2,1)S(1)} %get-tuple-element.32.grads, ...), custom_call_target="tpu_custom_call" | custom-call | flops 1 | bytes 1 | tf_op jit(solution)/shard_map/pallas_call | solution.py:32
  40.9 1.4 %collective-permute-done.6.arrived.sibling = bf16[512,256]{1,0:T(8,128)(2,1)S(1)} collective-permute-done((bf16[512,256]{1,0:T(8,128)(2,1)S(1)}, bf16[512,256]{1,0:T(8,128)(2,1)S(1)}, u32[]{:S(2)}, u32[]{:S(2)}) %collective-permute-start.6) | collective-permute-done | bytes 262176 | tf_op jit(solution)/shard_map/ppermute | solution.py:341
  42.7 2.2 %collective-permute-start.8 = (bf16[512,256]{1,0:T(8,128)(2,1)S(1)}, bf16[512,256]{1,0:T(8,128)(2,1)S(1)}, u32[]{:S(2)}, u32[]{:S(2)}) collective-permute-start(bf16[512,256]{1,0:T(8,128)(2,1)S(1)} %shard_map.100), channel_id=1, source_target_pairs={{8,0},{12,4},{16,8},{20,12},{24,16},{28,20},{32,24},{36,28},{40,32... | collective-permute-start | bytes 786440 | tf_op jit(solution)/shard_map/ppermute | solution.py:344
  45.6 4.7 %shard_map.101 = (bf16[512,256]{1,0:T(8,128)(2,1)S(1)}, f32[512,256]{1,0:T(8,128)S(1)}, bf16[512,256]{1,0:T(8,128)(2,1)S(1)}, f32[512,256]{1,0:T(8,128)S(1)}) custom-call(s32[1]{0:T(128)} %bitcast.place.index, bf16[512,512]{1,0:T(8,128)(2,1)S(1)} %get-tuple-element.41.queries, bf16[512,512]{1,0:T(8,128)(2,1)S(1)} %get-tuple-element.32.grads, ...), custom_call_target="tpu_custom_call" | custom-call | flops 1 | bytes 1 | tf_op jit(solution)/shard_map/pallas_call | solution.py:32
  50.6 2.5 %collective-permute-done.8.later = bf16[512,256]{1,0:T(8,128)(2,1)S(1)} collective-permute-done((bf16[512,256]{1,0:T(8,128)(2,1)S(1)}, bf16[512,256]{1,0:T(8,128)(2,1)S(1)}, u32[]{:S(2)}, u32[]{:S(2)}) %collective-permute-start.8) | collective-permute-done | bytes 262176 | tf_op jit(solution)/shard_map/ppermute | solution.py:344
  53.9 8.0 %collective-permute-done.14.rest_5_ = bf16[1344,256]{1,0:T(8,128)(2,1)S(1)} collective-permute-done((bf16[1344,256]{1,0:T(8,128)(2,1)S(1)}, bf16[1344,256]{1,0:T(8,128)(2,1)S(1)}, u32[]{:S(2)}, u32[]{:S(2)}) %collective-permute-start.14) | collective-permute-done | bytes 688160 | tf_op jit(solution)/shard_map/ppermute | solution.py:347
  61.8 1.9 %collective-permute-start.10 = (bf16[512,256]{1,0:T(8,128)(2,1)S(1)}, bf16[512,256]{1,0:T(8,128)(2,1)S(1)}, u32[]{:S(2)}, u32[]{:S(2)}) collective-permute-start(bf16[512,256]{1,0:T(8,128)(2,1)S(1)} %shard_map.103), channel_id=1, source_target_pairs={{8,0},{12,4},{16,8},{20,12},{24,16},{28,20},{32,24},{36,28},{40,32... | collective-permute-start | bytes 786440 | tf_op jit(solution)/shard_map/ppermute | solution.py:344
  63.8 1.3 %collective-permute-start.12 = (bf16[512,256]{1,0:T(8,128)(2,1)S(1)}, bf16[512,256]{1,0:T(8,128)(2,1)S(1)}, u32[]{:S(2)}, u32[]{:S(2)}) collective-permute-start(bf16[512,256]{1,0:T(8,128)(2,1)S(1)} %shard_map.102.own0), channel_id=1, source_target_pairs={{0,2},{1,3},{2,0},{3,1},{4,6},{5,7},{6,4},{7,5},{8,10},{9,11},{10,... | collective-permute-start | bytes 786440 | tf_op jit(solution)/shard_map/ppermute | solution.py:347
  65.2 1.9 %collective-permute-start.13 = (bf16[512,256]{1,0:T(8,128)(2,1)S(1)}, bf16[512,256]{1,0:T(8,128)(2,1)S(1)}, u32[]{:S(2)}, u32[]{:S(2)}) collective-permute-start(bf16[512,256]{1,0:T(8,128)(2,1)S(1)} %shard_map.102.own0), channel_id=1, source_target_pairs={{0,3},{1,0},{2,1},{3,2},{4,7},{5,4},{6,5},{7,6},{8,11},{9,8},{10,9... | collective-permute-start | bytes 786440 | tf_op jit(solution)/shard_map/ppermute | solution.py:347
  67.1 5.4 %collective-permute-done.10.later = bf16[512,256]{1,0:T(8,128)(2,1)S(1)} collective-permute-done((bf16[512,256]{1,0:T(8,128)(2,1)S(1)}, bf16[512,256]{1,0:T(8,128)(2,1)S(1)}, u32[]{:S(2)}, u32[]{:S(2)}) %collective-permute-start.10) | collective-permute-done | bytes 262176 | tf_op jit(solution)/shard_map/ppermute | solution.py:344
  73.2 6.5 %collective-permute-done.11.rest_0_ = bf16[512,256]{1,0:T(8,128)(2,1)S(1)} collective-permute-done((bf16[512,256]{1,0:T(8,128)(2,1)S(1)}, bf16[512,256]{1,0:T(8,128)(2,1)S(1)}, u32[]{:S(2)}, u32[]{:S(2)}) %collective-permute-start.11) | collective-permute-done | bytes 262176 | tf_op jit(solution)/shard_map/ppermute | solution.py:347
  80.6 2.8 %shard_map.105.early = f32[1344,512]{1,0:T(8,128)S(1)} custom-call(s32[1]{0:T(128)} %bitcast.place.index, s32[1]{0:T(128)} %bitcast.3.group, bf16[5376,256]{1,0:T(8,128)(2,1)S(1)} %copy-done, bf16[5376,256]{1,0:T(8,128)(2,1)S(1)} %copy-done.1, bf16[512,256]{1,0:T(8,128)(2,1)S(1)} %shard_map.102.own0, bf16[512,256]{1,0:T(8,128)(2,1)S(1)} %shard_map.104.own1, ...), custom_call_target="tpu_custom_call" | custom-call | flops 1 | bytes 1 | tf_op jit(solution)/shard_map/pallas_call | solution.py:32
  83.4 7.2 %collective-permute-done.16.rest_0_ = bf16[512,256]{1,0:T(8,128)(2,1)S(1)} collective-permute-done((bf16[512,256]{1,0:T(8,128)(2,1)S(1)}, bf16[512,256]{1,0:T(8,128)(2,1)S(1)}, u32[]{:S(2)}, u32[]{:S(2)}) %collective-permute-start.16) | collective-permute-done | bytes 262176 | tf_op jit(solution)/shard_map/ppermute | solution.py:347
  91.3 2.4 %shard_map.106 = bf16[1344,512]{1,0:T(8,128)(2,1)} custom-call(s32[1]{0:T(128)} %bitcast.place.index, f32[1344,512]{1,0:T(8,128)S(1)} %shard_map.105.early, bf16[512,256]{1,0:T(8,128)(2,1)S(1)} %collective-permute-done.16.rest_0_, bf16[512,256]{1,0:T(8,128)(2,1)S(1)} %collective-permute-done.17.rest_1_, ...), custom_call_target="tpu_custom_call" | custom-call | flops 1 | bytes 1 | tf_op jit(solution)/shard_map/pallas_call | solution.py:32
  (46 shorter events, 6.5 us)
Async XLA Ops:
  3.4 31.0 %collective-permute-start.2 = (bf16[2688,256]{1,0:T(8,128)(2,1)}, bf16[2688,256]{1,0:T(8,128)(2,1)S(1)}, u32[]{:S(2)}, u32[]{:S(2)}) collective-permute-start(bf16[2688,256]{1,0:T(8,128)(2,1)} %get-tuple-element.30), channel_id=1, source_target_pairs={{0,1},{1,2},{2,3},{3,0},{4,7},{5,4},{6,5},{7,6},{8,9},{9,10},{10,1... | collective-permute-start | bytes 4128776 | tf_op jit(solution)/shard_map/ppermute | solution.py:385
  5.0 29.0 %copy-start.3 = (bf16[512,512]{1,0:T(8,128)(2,1)S(1)}, bf16[512,512]{1,0:T(8,128)(2,1)}, u32[]{:S(2)}) copy-start(bf16[512,512]{1,0:T(8,128)(2,1)} %queries.1) | copy-start | bytes 1572868
  5.0 29.0 %copy-start.4 = (bf16[512,512]{1,0:T(8,128)(2,1)S(1)}, bf16[512,512]{1,0:T(8,128)(2,1)}, u32[]{:S(2)}) copy-start(bf16[512,512]{1,0:T(8,128)(2,1)} %grads.1) | copy-start | bytes 1572868
  5.7 14.3 %collective-permute-start = (bf16[512,256]{1,0:T(8,128)(2,1)S(1)}, bf16[512,256]{1,0:T(8,128)(2,1)S(1)}, u32[]{:S(2)}, u32[]{:S(2)}) collective-permute-start(bf16[512,256]{1,0:T(8,128)(2,1)S(1)} %get-tuple-element.27.own), channel_id=1, source_target_pairs={{0,8},{4,12},{8,16},{12,20},{16,24},{20,28},{24,32},{28,36},{32,40... | collective-permute-start | bytes 786440 | tf_op jit(solution)/shard_map/ppermute | solution.py:344
  9.2 10.8 %collective-permute-start.1 = (f32[8,256]{1,0:T(8,128)S(1)}, f32[8,256]{1,0:T(8,128)S(1)}, u32[]{:S(2)}, u32[]{:S(2)}) collective-permute-start(f32[8,256]{1,0:T(8,128)S(1)} %get-tuple-element.28), channel_id=1, source_target_pairs={{0,4},{4,8},{8,12},{12,16},{16,20},{20,24},{24,28},{28,32},{32,36}... | collective-permute-start | bytes 24584 | tf_op jit(solution)/shard_map/ppermute | solution.py:344
  11.7 14.2 %collective-permute-start.4 = (bf16[512,256]{1,0:T(8,128)(2,1)S(1)}, bf16[512,256]{1,0:T(8,128)(2,1)S(1)}, u32[]{:S(2)}, u32[]{:S(2)}) collective-permute-start(bf16[512,256]{1,0:T(8,128)(2,1)S(1)} %get-tuple-element.34.values0), channel_id=1, source_target_pairs={{0,8},{4,12},{8,16},{12,20},{16,24},{20,28},{24,32},{28,36},{32,40... | collective-permute-start | bytes 786440 | tf_op jit(solution)/shard_map/ppermute | solution.py:344
  20.5 13.3 %collective-permute-start.3 = (bf16[512,256]{1,0:T(8,128)(2,1)S(1)}, bf16[512,256]{1,0:T(8,128)(2,1)S(1)}, u32[]{:S(2)}, u32[]{:S(2)}) collective-permute-start(bf16[512,256]{1,0:T(8,128)(2,1)S(1)} %shard_map.96.ready.keys0), channel_id=1, source_target_pairs={{0,8},{4,12},{8,16},{12,20},{16,24},{20,28},{24,32},{28,36},{32,40... | collective-permute-start | bytes 786440 | tf_op jit(solution)/shard_map/ppermute | solution.py:344
  33.9 2.0 %collective-permute-start.5 = (bf16[512,512]{1,0:T(8,128)(2,1)S(1)}, bf16[512,512]{1,0:T(8,128)(2,1)S(1)}, u32[]{:S(2)}, u32[]{:S(2)}) collective-permute-start(bf16[512,512]{1,0:T(8,128)(2,1)S(1)} %maximum_select_fusion), channel_id=1, source_target_pairs={{0,4},{4,0},{8,12},{12,8},{16,20},{20,16},{24,28},{28,24},{32,36},... | collective-permute-start | bytes 1572872 | tf_op jit(solution)/shard_map/ppermute | solution.py:341
  35.9 6.7 %copy-start.8 = (bf16[1344,256]{1,0:T(8,128)(2,1)S(1)}, bf16[1344,256]{1,0:T(8,128)(2,1)}, u32[]{:S(2)}) copy-start(bf16[1344,256]{1,0:T(8,128)(2,1)} %get-tuple-element.50) | copy-start | bytes 2064388
  40.7 1.6 %collective-permute-start.6 = (bf16[512,256]{1,0:T(8,128)(2,1)S(1)}, bf16[512,256]{1,0:T(8,128)(2,1)S(1)}, u32[]{:S(2)}, u32[]{:S(2)}) collective-permute-start(bf16[512,256]{1,0:T(8,128)(2,1)S(1)} %get-tuple-element.37), channel_id=1, source_target_pairs={{0,4},{4,0},{8,12},{12,8},{16,20},{20,16},{24,28},{28,24},{32,36},... | collective-permute-start | bytes 786440 | tf_op jit(solution)/shard_map/ppermute | solution.py:341
  42.4 3.2 %collective-permute-start.7 = (bf16[2688,256]{1,0:T(8,128)(2,1)S(1)}, bf16[2688,256]{1,0:T(8,128)(2,1)S(1)}, u32[]{:S(2)}, u32[]{:S(2)}) collective-permute-start(bf16[2688,256]{1,0:T(8,128)(2,1)S(1)} %collective-permute-done.2.rest_3_), channel_id=1, source_target_pairs={{0,4},{4,0},{8,12},{12,8},{16,20},{20,16},{24,28},{28,24},{32,36},... | collective-permute-start | bytes 4128776 | tf_op jit(solution)/shard_map/ppermute | solution.py:341
  42.6 19.2 %collective-permute-start.14 = (bf16[1344,256]{1,0:T(8,128)(2,1)S(1)}, bf16[1344,256]{1,0:T(8,128)(2,1)S(1)}, u32[]{:S(2)}, u32[]{:S(2)}) collective-permute-start(bf16[1344,256]{1,0:T(8,128)(2,1)S(1)} %copy-done.8), channel_id=1, source_target_pairs={{0,2},{1,3},{2,0},{3,1},{4,6},{5,7},{6,4},{7,5},{8,10},{9,11},{10,... | collective-permute-start | bytes 2064392 | tf_op jit(solution)/shard_map/ppermute | solution.py:347
  42.7 10.4 %collective-permute-start.8 = (bf16[512,256]{1,0:T(8,128)(2,1)S(1)}, bf16[512,256]{1,0:T(8,128)(2,1)S(1)}, u32[]{:S(2)}, u32[]{:S(2)}) collective-permute-start(bf16[512,256]{1,0:T(8,128)(2,1)S(1)} %shard_map.100), channel_id=1, source_target_pairs={{8,0},{12,4},{16,8},{20,12},{24,16},{28,20},{32,24},{36,28},{40,32... | collective-permute-start | bytes 786440 | tf_op jit(solution)/shard_map/ppermute | solution.py:344
  45.6 35.0 %copy-start.1 = (bf16[5376,256]{1,0:T(8,128)(2,1)S(1)}, bf16[5376,256]{1,0:T(8,128)(2,1)}, u32[]{:S(2)}) copy-start(bf16[5376,256]{1,0:T(8,128)(2,1)} %values.3) | copy-start | bytes 8257540
  50.3 3.4 %collective-permute-start.9 = (bf16[512,256]{1,0:T(8,128)(2,1)S(1)}, bf16[512,256]{1,0:T(8,128)(2,1)S(1)}, u32[]{:S(2)}, u32[]{:S(2)}) collective-permute-start(bf16[512,256]{1,0:T(8,128)(2,1)S(1)} %get-tuple-element.45), channel_id=1, source_target_pairs={{0,4},{4,0},{8,12},{12,8},{16,20},{20,16},{24,28},{28,24},{32,36},... | collective-permute-start | bytes 786440 | tf_op jit(solution)/shard_map/ppermute | solution.py:341
  53.8 26.8 %copy-start = (bf16[5376,256]{1,0:T(8,128)(2,1)S(1)}, bf16[5376,256]{1,0:T(8,128)(2,1)}, u32[]{:S(2)}) copy-start(bf16[5376,256]{1,0:T(8,128)(2,1)} %keys.3) | copy-start | bytes 8257540
  61.8 18.8 %collective-permute-start.15 = (bf16[1344,256]{1,0:T(8,128)(2,1)S(1)}, bf16[1344,256]{1,0:T(8,128)(2,1)S(1)}, u32[]{:S(2)}, u32[]{:S(2)}) collective-permute-start(bf16[1344,256]{1,0:T(8,128)(2,1)S(1)} %collective-permute-done.14.rest_5_), channel_id=1, source_target_pairs={{0,4},{4,0},{8,12},{12,8},{16,20},{20,16},{24,28},{28,24},{32,36},... | collective-permute-start | bytes 2064392 | tf_op jit(solution)/shard_map/ppermute | solution.py:341
  61.8 10.6 %collective-permute-start.10 = (bf16[512,256]{1,0:T(8,128)(2,1)S(1)}, bf16[512,256]{1,0:T(8,128)(2,1)S(1)}, u32[]{:S(2)}, u32[]{:S(2)}) collective-permute-start(bf16[512,256]{1,0:T(8,128)(2,1)S(1)} %shard_map.103), channel_id=1, source_target_pairs={{8,0},{12,4},{16,8},{20,12},{24,16},{28,20},{32,24},{36,28},{40,32... | collective-permute-start | bytes 786440 | tf_op jit(solution)/shard_map/ppermute | solution.py:344
  63.7 16.0 %collective-permute-start.11 = (bf16[512,256]{1,0:T(8,128)(2,1)S(1)}, bf16[512,256]{1,0:T(8,128)(2,1)S(1)}, u32[]{:S(2)}, u32[]{:S(2)}) collective-permute-start(bf16[512,256]{1,0:T(8,128)(2,1)S(1)} %shard_map.102.own0), channel_id=1, source_target_pairs={{0,1},{1,2},{2,3},{3,0},{4,5},{5,6},{6,7},{7,4},{8,9},{9,10},{10,1... | collective-permute-start | bytes 786440 | tf_op jit(solution)/shard_map/ppermute | solution.py:347
  63.8 15.9 %collective-permute-start.12 = (bf16[512,256]{1,0:T(8,128)(2,1)S(1)}, bf16[512,256]{1,0:T(8,128)(2,1)S(1)}, u32[]{:S(2)}, u32[]{:S(2)}) collective-permute-start(bf16[512,256]{1,0:T(8,128)(2,1)S(1)} %shard_map.102.own0), channel_id=1, source_target_pairs={{0,2},{1,3},{2,0},{3,1},{4,6},{5,7},{6,4},{7,5},{8,10},{9,11},{10,... | collective-permute-start | bytes 786440 | tf_op jit(solution)/shard_map/ppermute | solution.py:347
  65.2 15.4 %collective-permute-start.13 = (bf16[512,256]{1,0:T(8,128)(2,1)S(1)}, bf16[512,256]{1,0:T(8,128)(2,1)S(1)}, u32[]{:S(2)}, u32[]{:S(2)}) collective-permute-start(bf16[512,256]{1,0:T(8,128)(2,1)S(1)} %shard_map.102.own0), channel_id=1, source_target_pairs={{0,3},{1,0},{2,1},{3,2},{4,7},{5,4},{6,5},{7,6},{8,11},{9,8},{10,9... | collective-permute-start | bytes 786440 | tf_op jit(solution)/shard_map/ppermute | solution.py:347
  73.1 17.5 %collective-permute-start.16 = (bf16[512,256]{1,0:T(8,128)(2,1)S(1)}, bf16[512,256]{1,0:T(8,128)(2,1)S(1)}, u32[]{:S(2)}, u32[]{:S(2)}) collective-permute-start(bf16[512,256]{1,0:T(8,128)(2,1)S(1)} %shard_map.104.own1), channel_id=1, source_target_pairs={{0,1},{1,2},{2,3},{3,0},{4,5},{5,6},{6,7},{7,4},{8,9},{9,10},{10,1... | collective-permute-start | bytes 786440 | tf_op jit(solution)/shard_map/ppermute | solution.py:347
  79.7 10.9 %collective-permute-start.17 = (bf16[512,256]{1,0:T(8,128)(2,1)S(1)}, bf16[512,256]{1,0:T(8,128)(2,1)S(1)}, u32[]{:S(2)}, u32[]{:S(2)}) collective-permute-start(bf16[512,256]{1,0:T(8,128)(2,1)S(1)} %shard_map.104.own1), channel_id=1, source_target_pairs={{0,2},{1,3},{2,0},{3,1},{4,6},{5,7},{6,4},{7,5},{8,10},{9,11},{10,... | collective-permute-start | bytes 786440 | tf_op jit(solution)/shard_map/ppermute | solution.py:347
  79.7 11.5 %collective-permute-start.18 = (bf16[512,256]{1,0:T(8,128)(2,1)S(1)}, bf16[512,256]{1,0:T(8,128)(2,1)S(1)}, u32[]{:S(2)}, u32[]{:S(2)}) collective-permute-start(bf16[512,256]{1,0:T(8,128)(2,1)S(1)} %shard_map.104.own1), channel_id=1, source_target_pairs={{0,3},{1,0},{2,1},{3,2},{4,7},{5,4},{6,5},{7,6},{8,11},{9,8},{10,9... | collective-permute-start | bytes 786440 | tf_op jit(solution)/shard_map/ppermute | solution.py:347
  (4 other events, 17.3 us)

commit v6 on v5

--- a/solution.py
+++ b/solution.py
@@ -74,30 +74,24 @@
                 total_out[:, lanes] = jnp.broadcast_to(total, (8, HEAD_SIZE))
 
 
-def cut_kernel(index, group, key_matrix, value_matrix, ready, near, far, near_rows, far_rows, arrivals, departures):
+def cut_kernel(index, group, key_matrix, value_matrix, ready, sent, rows, arrivals, departures):
     half = HALF_ROWS
     core = index[0] & 1
-    begins = (
-        pl.multiple_of(((group[0] + 1 + 2 * core) & 3) * (2 * half), 16),
-        pl.multiple_of(((group[0] + 2) & 3) * (2 * half) + core * half, 16),
-    )
+    near_begin = pl.multiple_of(((group[0] + 1 + 2 * core) & 3) * (2 * half), 16)
+    far_begin = pl.multiple_of(((group[0] + 2) & 3) * (2 * half) + core * half, 16)
     incoming, outgoing = [], []
-    for at, (begin, count, kept, target) in enumerate(
-        ((begins[0], 2 * half, near_rows, near), (begins[1], half, far_rows, far))
-    ):
-        for part, matrix in enumerate((key_matrix, value_matrix)):
-            incoming.append(
-                pltpu.make_async_copy(
-                    matrix.at[pl.ds(begin, count), :], kept.at[pl.ds(part * count, count), :], arrivals.at[2 * at + part]
-                )
-            )
-        outgoing.append(pltpu.make_async_copy(kept, target, departures.at[at]))
+    first = 0
+    for begin, count in ((near_begin, 2 * half), (far_begin, half)):
+        for matrix in (key_matrix, value_matrix):
+            at, there = len(incoming), pl.ds(first, count)
+            incoming.append(pltpu.make_async_copy(matrix.at[pl.ds(begin, count), :], rows.at[there, :], arrivals.at[at]))
+            outgoing.append(pltpu.make_async_copy(rows.at[there, :], sent.at[there, :], departures.at[at]))
+            first += count
     for copy in incoming:
         copy.start()
-    for at in range(2):
-        incoming[2 * at].wait()
-        incoming[2 * at + 1].wait()
-        outgoing[at].start()
+    for arrived, leaving in zip(incoming, outgoing):
+        arrived.wait()
+        leaving.start()
     for copy in outgoing:
         copy.wait()
 
@@ -358,16 +352,15 @@
     last_total = onward(key_total, 1)
 
 
-    near_sent, far_sent = pl.pallas_call(
+    near_sent = pl.pallas_call(
         cut_kernel,
-        out_shape=(shape_of(2 * model_rows, 256), shape_of(model_rows, 256)),
+        out_shape=shape_of(3 * model_rows, 256),
         in_specs=[SMEM, SMEM, HBM, HBM, pl.BlockSpec(memory_space=pl.ANY)],
-        out_specs=(HBM,) * 2,
+        out_specs=HBM,
         scratch_shapes=[
-            pltpu.VMEM((2 * model_rows, 256), jnp.bfloat16),
-            pltpu.VMEM((model_rows, 256), jnp.bfloat16),
+            pltpu.VMEM((3 * model_rows, 256), jnp.bfloat16),
             pltpu.SemaphoreType.DMA((4,)),
-            pltpu.SemaphoreType.DMA((2,)),
+            pltpu.SemaphoreType.DMA((4,)),
         ],
         cost_estimate=pl.CostEstimate(flops=1, bytes_accessed=1, transcendentals=0),
         compiler_params=pltpu.CompilerParams(vmem_limit_bytes=CUT_LIMIT * MEBI),
@@ -409,7 +402,8 @@
         )
         query_grads.append(query_part)
         if head == 0:
-            far = along_head(lax.optimization_barrier((far_sent, grad1))[0], 2)
+            passed_on, _ = lax.optimization_barrier((near, grad1))
+            far = lax.ppermute(passed_on[2 * model_rows :], ("seq", "head"), near_pairs)
         sibling_grad = to_sibling(grad1)
         if head == 1:
             grad2, _ = lax.optimization_barrier((grad2, gathered[0][0]))

time: 94.1 us -> 90.1 us (0.957)
  waiting for transfers between devices: 50.1 us -> 40.8 us
  starting transfers between devices: 21.3 us -> 24.8 us
  local copies, waits for them, and re-layouts: 0.04 us -> 2.15 us
    ppermute x7 -> x6, waiting for transfers between devices: 22.4 us -> 16.6 us  [along_head(): lax.ppermute(value, 'head', [(at, (at + steps) % groups) for at in range(...]
    ppermute x6, waiting for transfers between devices: 24.1 us -> 20.4 us  [onward(): return lax.ppermute(value, 'seq', shift_pairs(count, steps))]
    ppermute x6, starting transfers between devices: 15.4 us -> 18 us  [onward(): return lax.ppermute(value, 'seq', shift_pairs(count, steps))]
    unnamed x18 -> x16, local copies, waits for them, and re-layouts: 0.04 us -> 2.1 us
    ppermute x0 -> x1, waiting for transfers between devices: none -> 1.12 us  [local(): far = lax.ppermute(passed_on[2 * model_rows:], ('seq', 'head'), near_pairs)]
    ppermute x5, waiting for transfers between devices: 3.61 us -> 2.66 us  [to_sibling(): return lax.ppermute(value, 'seq', siblings)]
    ppermute x7 -> x6, starting transfers between devices: 3.49 us -> 3.6 us  [along_head(): lax.ppermute(value, 'head', [(at, (at + steps) % groups) for at in range(...]
  transfers between devices with their start and end apart: 19 -> 19, of which waited for: 13 -> 13; matrix products, arithmetic and copies ran while one was open for 1% -> 1% of each run, Pallas kernels for 11% -> 12%
where the time goes in v6:
time: 90.1 us; the launch traced here: 89.7 us
  waiting for transfers between devices  40.8 us (45%)
  starting transfers between devices  24.8 us (28%)
  Pallas kernels  20.2 us (22%)
  local copies, waits for them, and re-layouts  2.15 us (2%)
  other arithmetic  0.95 us (1%)
    ppermute x6, waiting for transfers between devices, onward(): return lax.ppermute(value, 'seq', shift_pairs(count, steps))  20.4 us
    ppermute x6, starting transfers between devices, onward(): return lax.ppermute(value, 'seq', shift_pairs(count, steps))  18 us
    pallas_call x11, Pallas kernels, vmem_call(): pl.pallas_call(kernel, out_shape=out_shapes, in_specs=in_specs if in_spec...  17.6 us
    ppermute x6, waiting for transfers between devices, along_head(): lax.ppermute(value, 'head', [(at, (at + steps) % groups) for at in range(...  16.6 us
    ppermute x6, starting transfers between devices, along_head(): lax.ppermute(value, 'head', [(at, (at + steps) % groups) for at in range(...  3.6 us
    ppermute x5, waiting for transfers between devices, to_sibling(): return lax.ppermute(value, 'seq', siblings)  2.66 us
    pallas_call x1, Pallas kernels, local(): pl.pallas_call(cut_kernel, out_shape=shape_of(3 * model_rows, 256), in_sp...  2.56 us
    unnamed x16, local copies, waits for them, and re-layouts  2.1 us
  transfers between devices with their start and end apart: 19, of which 13 were waited for; matrix products, arithmetic and copies ran while one was open for 1% of the time, Pallas kernels for 12%

profile of v6, /device:TPU:128, one launch (start us, length us, event | category | flops | bytes accessed | tf_op | source)
XLA Modules:
  0.0 89.7 jit_solution(6018851669025127727)
XLA Ops:
  0.7 2.6 %shard_map.98 = bf16[4032,256]{1,0:T(8,128)(2,1)} custom-call(s32[1]{0:T(128)} %bitcast.place.index, s32[1]{0:T(128)} %bitcast.3.group, bf16[5376,256]{1,0:T(8,128)(2,1)} %keys.3, bf16[5376,256]{1,0:T(8,128)(2,1)} %values.3, bf16[512,256]{1,0:T(8,128)(2,1)} %ready.1), custom_call_target="tpu_custom_call" | custom-call | flops 1 | bytes 1 | tf_op jit(solution)/shard_map/pallas_call | solution.py:355
  3.2 1.6 %collective-permute-start.2 = (bf16[4032,256]{1,0:T(8,128)(2,1)}, bf16[4032,256]{1,0:T(8,128)(2,1)S(1)}, u32[]{:S(2)}, u32[]{:S(2)}) collective-permute-start(bf16[4032,256]{1,0:T(8,128)(2,1)} %shard_map.98), channel_id=1, source_target_pairs={{0,1},{1,2},{2,3},{3,0},{4,7},{5,4},{6,5},{7,6},{8,9},{9,10},{10,1... | collective-permute-start | bytes 6193160 | tf_op jit(solution)/shard_map/ppermute | solution.py:378
  5.5 3.5 %collective-permute-start = (bf16[512,256]{1,0:T(8,128)(2,1)S(1)}, bf16[512,256]{1,0:T(8,128)(2,1)S(1)}, u32[]{:S(2)}, u32[]{:S(2)}) collective-permute-start(bf16[512,256]{1,0:T(8,128)(2,1)S(1)} %get-tuple-element.25.own), channel_id=1, source_target_pairs={{0,8},{4,12},{8,16},{12,20},{16,24},{20,28},{24,32},{28,36},{32,40... | collective-permute-start | bytes 786440 | tf_op jit(solution)/shard_map/ppermute | solution.py:338
  9.0 2.5 %collective-permute-start.1 = (f32[8,256]{1,0:T(8,128)S(1)}, f32[8,256]{1,0:T(8,128)S(1)}, u32[]{:S(2)}, u32[]{:S(2)}) collective-permute-start(f32[8,256]{1,0:T(8,128)S(1)} %get-tuple-element.26), channel_id=1, source_target_pairs={{0,4},{4,8},{8,12},{12,16},{16,20},{20,24},{24,28},{28,32},{32,36}... | collective-permute-start | bytes 24584 | tf_op jit(solution)/shard_map/ppermute | solution.py:338
  11.5 3.5 %collective-permute-start.4 = (bf16[512,256]{1,0:T(8,128)(2,1)S(1)}, bf16[512,256]{1,0:T(8,128)(2,1)S(1)}, u32[]{:S(2)}, u32[]{:S(2)}) collective-permute-start(bf16[512,256]{1,0:T(8,128)(2,1)S(1)} %get-tuple-element.31.values0), channel_id=1, source_target_pairs={{0,8},{4,12},{8,16},{12,20},{16,24},{20,28},{24,32},{28,36},{32,40... | collective-permute-start | bytes 786440 | tf_op jit(solution)/shard_map/ppermute | solution.py:338
  15.0 4.8 %collective-permute-done.1.total = f32[8,256]{1,0:T(8,128)S(1)} collective-permute-done((f32[8,256]{1,0:T(8,128)S(1)}, f32[8,256]{1,0:T(8,128)S(1)}, u32[]{:S(2)}, u32[]{:S(2)}) %collective-permute-start.1) | collective-permute-done | bytes 8224 | tf_op jit(solution)/shard_map/ppermute | solution.py:338
  20.3 1.9 %collective-permute-start.3 = (bf16[512,256]{1,0:T(8,128)(2,1)S(1)}, bf16[512,256]{1,0:T(8,128)(2,1)S(1)}, u32[]{:S(2)}, u32[]{:S(2)}) collective-permute-start(bf16[512,256]{1,0:T(8,128)(2,1)S(1)} %shard_map.96.ready.keys0), channel_id=1, source_target_pairs={{0,8},{4,12},{8,16},{12,20},{16,24},{20,28},{24,32},{28,36},{32,40... | collective-permute-start | bytes 786440 | tf_op jit(solution)/shard_map/ppermute | solution.py:338
  22.2 3.4 %collective-permute-done.4.values2 = bf16[512,256]{1,0:T(8,128)(2,1)S(1)} collective-permute-done((bf16[512,256]{1,0:T(8,128)(2,1)S(1)}, bf16[512,256]{1,0:T(8,128)(2,1)S(1)}, u32[]{:S(2)}, u32[]{:S(2)}) %collective-permute-start.4) | collective-permute-done | bytes 262176 | tf_op jit(solution)/shard_map/ppermute | solution.py:338
  25.7 7.9 %collective-permute-done.3.keys2 = bf16[512,256]{1,0:T(8,128)(2,1)S(1)} collective-permute-done((bf16[512,256]{1,0:T(8,128)(2,1)S(1)}, bf16[512,256]{1,0:T(8,128)(2,1)S(1)}, u32[]{:S(2)}, u32[]{:S(2)}) %collective-permute-start.3) | collective-permute-done | bytes 262176 | tf_op jit(solution)/shard_map/ppermute | solution.py:338
  34.9 1.0 %copy-done.4 = bf16[512,512]{1,0:T(8,128)(2,1)S(1)} copy-done((bf16[512,512]{1,0:T(8,128)(2,1)S(1)}, bf16[512,512]{1,0:T(8,128)(2,1)}, u32[]{:S(2)}) %copy-start.4) | copy-done | bytes 524312
  36.3 4.8 %shard_map.99 = (bf16[512,256]{1,0:T(8,128)(2,1)S(1)}, f32[512,256]{1,0:T(8,128)S(1)}, bf16[512,256]{1,0:T(8,128)(2,1)S(1)}, f32[512,256]{1,0:T(8,128)S(1)}) custom-call(s32[1]{0:T(128)} %bitcast.place.index, bf16[512,512]{1,0:T(8,128)(2,1)S(1)} %get-tuple-element.38.queries, bf16[512,512]{1,0:T(8,128)(2,1)S(1)} %get-tuple-element.29.grads, ...), custom_call_target="tpu_custom_call" | custom-call | flops 1 | bytes 1 | tf_op jit(solution)/shard_map/pallas_call | solution.py:32
  41.7 1.2 %collective-permute-done.6.arrived.sibling = bf16[512,256]{1,0:T(8,128)(2,1)S(1)} collective-permute-done((bf16[512,256]{1,0:T(8,128)(2,1)S(1)}, bf16[512,256]{1,0:T(8,128)(2,1)S(1)}, u32[]{:S(2)}, u32[]{:S(2)}) %collective-permute-start.6) | collective-permute-done | bytes 262176 | tf_op jit(solution)/shard_map/ppermute | solution.py:335
  43.5 2.1 %collective-permute-start.8 = (bf16[512,256]{1,0:T(8,128)(2,1)S(1)}, bf16[512,256]{1,0:T(8,128)(2,1)S(1)}, u32[]{:S(2)}, u32[]{:S(2)}) collective-permute-start(bf16[512,256]{1,0:T(8,128)(2,1)S(1)} %shard_map.100), channel_id=1, source_target_pairs={{8,0},{12,4},{16,8},{20,12},{24,16},{28,20},{32,24},{36,28},{40,32... | collective-permute-start | bytes 786440 | tf_op jit(solution)/shard_map/ppermute | solution.py:338
  45.6 1.5 %collective-permute-done.7.rest_4_ = bf16[4032,256]{1,0:T(8,128)(2,1)S(1)} collective-permute-done((bf16[4032,256]{1,0:T(8,128)(2,1)S(1)}, bf16[4032,256]{1,0:T(8,128)(2,1)S(1)}, u32[]{:S(2)}, u32[]{:S(2)}) %collective-permute-start.7) | collective-permute-done | bytes 2064416 | tf_op jit(solution)/shard_map/ppermute | solution.py:335
  47.1 4.7 %shard_map.101 = (bf16[512,256]{1,0:T(8,128)(2,1)S(1)}, f32[512,256]{1,0:T(8,128)S(1)}, bf16[512,256]{1,0:T(8,128)(2,1)S(1)}, f32[512,256]{1,0:T(8,128)S(1)}) custom-call(s32[1]{0:T(128)} %bitcast.place.index, bf16[512,512]{1,0:T(8,128)(2,1)S(1)} %get-tuple-element.38.queries, bf16[512,512]{1,0:T(8,128)(2,1)S(1)} %get-tuple-element.29.grads, ...), custom_call_target="tpu_custom_call" | custom-call | flops 1 | bytes 1 | tf_op jit(solution)/shard_map/pallas_call | solution.py:32
  52.3 1.4 %collective-permute-done.8.later = bf16[512,256]{1,0:T(8,128)(2,1)S(1)} collective-permute-done((bf16[512,256]{1,0:T(8,128)(2,1)S(1)}, bf16[512,256]{1,0:T(8,128)(2,1)S(1)}, u32[]{:S(2)}, u32[]{:S(2)}) %collective-permute-start.8) | collective-permute-done | bytes 262176 | tf_op jit(solution)/shard_map/ppermute | solution.py:338
  54.5 1.1 %collective-permute-done.14.rest_5_ = bf16[1344,256]{1,0:T(8,128)(2,1)S(1)} collective-permute-done((bf16[1344,256]{1,0:T(8,128)(2,1)S(1)}, bf16[1344,256]{1,0:T(8,128)(2,1)S(1)}, u32[]{:S(2)}, u32[]{:S(2)}) %collective-permute-start.14) | collective-permute-done | bytes 688160 | tf_op jit(solution)/shard_map/ppermute | solution.py:406
  55.6 4.5 %collective-permute-start.10 = (bf16[512,256]{1,0:T(8,128)(2,1)S(1)}, bf16[512,256]{1,0:T(8,128)(2,1)S(1)}, u32[]{:S(2)}, u32[]{:S(2)}) collective-permute-start(bf16[512,256]{1,0:T(8,128)(2,1)S(1)} %shard_map.103), channel_id=1, source_target_pairs={{8,0},{12,4},{16,8},{20,12},{24,16},{28,20},{32,24},{36,28},{40,32... | collective-permute-start | bytes 786440 | tf_op jit(solution)/shard_map/ppermute | solution.py:338
  60.8 1.9 %collective-permute-start.12 = (bf16[512,256]{1,0:T(8,128)(2,1)S(1)}, bf16[512,256]{1,0:T(8,128)(2,1)S(1)}, u32[]{:S(2)}, u32[]{:S(2)}) collective-permute-start(bf16[512,256]{1,0:T(8,128)(2,1)S(1)} %shard_map.102.own0), channel_id=1, source_target_pairs={{0,2},{1,3},{2,0},{3,1},{4,6},{5,7},{6,4},{7,5},{8,10},{9,11},{10,... | collective-permute-start | bytes 786440 | tf_op jit(solution)/shard_map/ppermute | solution.py:341
  63.6 2.7 %collective-permute-done.10.later = bf16[512,256]{1,0:T(8,128)(2,1)S(1)} collective-permute-done((bf16[512,256]{1,0:T(8,128)(2,1)S(1)}, bf16[512,256]{1,0:T(8,128)(2,1)S(1)}, u32[]{:S(2)}, u32[]{:S(2)}) %collective-permute-start.10) | collective-permute-done | bytes 262176 | tf_op jit(solution)/shard_map/ppermute | solution.py:338
  67.2 8.9 %collective-permute-done.11.rest_0_ = bf16[512,256]{1,0:T(8,128)(2,1)S(1)} collective-permute-done((bf16[512,256]{1,0:T(8,128)(2,1)S(1)}, bf16[512,256]{1,0:T(8,128)(2,1)S(1)}, u32[]{:S(2)}, u32[]{:S(2)}) %collective-permute-start.11) | collective-permute-done | bytes 262176 | tf_op jit(solution)/shard_map/ppermute | solution.py:341
  77.1 2.7 %shard_map.105.early = f32[1344,512]{1,0:T(8,128)S(1)} custom-call(s32[1]{0:T(128)} %bitcast.place.index, s32[1]{0:T(128)} %bitcast.3.group, bf16[5376,256]{1,0:T(8,128)(2,1)S(1)} %copy-done, bf16[5376,256]{1,0:T(8,128)(2,1)S(1)} %copy-done.1, bf16[512,256]{1,0:T(8,128)(2,1)S(1)} %shard_map.102.own0, bf16[512,256]{1,0:T(8,128)(2,1)S(1)} %shard_map.104.own1, ...), custom_call_target="tpu_custom_call" | custom-call | flops 1 | bytes 1 | tf_op jit(solution)/shard_map/pallas_call | solution.py:32
  79.9 6.8 %collective-permute-done.16.rest_0_ = bf16[512,256]{1,0:T(8,128)(2,1)S(1)} collective-permute-done((bf16[512,256]{1,0:T(8,128)(2,1)S(1)}, bf16[512,256]{1,0:T(8,128)(2,1)S(1)}, u32[]{:S(2)}, u32[]{:S(2)}) %collective-permute-start.16) | collective-permute-done | bytes 262176 | tf_op jit(solution)/shard_map/ppermute | solution.py:341
  87.4 2.4 %shard_map.106 = bf16[1344,512]{1,0:T(8,128)(2,1)} custom-call(s32[1]{0:T(128)} %bitcast.place.index, f32[1344,512]{1,0:T(8,128)S(1)} %shard_map.105.early, bf16[512,256]{1,0:T(8,128)(2,1)S(1)} %collective-permute-done.16.rest_0_, bf16[512,256]{1,0:T(8,128)(2,1)S(1)} %collective-permute-done.17.rest_1_, ...), custom_call_target="tpu_custom_call" | custom-call | flops 1 | bytes 1 | tf_op jit(solution)/shard_map/pallas_call | solution.py:32
  (45 shorter events, 9.3 us)
Async XLA Ops:
  0.6 4.2 %copy-start.2 = (bf16[512,256]{1,0:T(8,128)(2,1)S(1)}, bf16[512,256]{1,0:T(8,128)(2,1)}, u32[]{:S(2)}) copy-start(bf16[512,256]{1,0:T(8,128)(2,1)} %ready.1) | copy-start | bytes 786436
  0.6 4.2 %copy-start.5 = (bf16[512,256]{1,0:T(8,128)(2,1)S(1)}, bf16[512,256]{1,0:T(8,128)(2,1)}, u32[]{:S(2)}) copy-start(bf16[512,256]{1,0:T(8,128)(2,1)} %values.2) | copy-start | bytes 786436
  0.7 4.2 %copy-start.6 = (s32[4,2]{0,1:T(2,128)S(1)}, s32[4,2]{0,1:T(2,128)}, u32[]{:S(2)}) copy-start(s32[4,2]{0,1:T(2,128)} %param.12) | copy-start | bytes 100
  3.2 33.1 %collective-permute-start.2 = (bf16[4032,256]{1,0:T(8,128)(2,1)}, bf16[4032,256]{1,0:T(8,128)(2,1)S(1)}, u32[]{:S(2)}, u32[]{:S(2)}) collective-permute-start(bf16[4032,256]{1,0:T(8,128)(2,1)} %shard_map.98), channel_id=1, source_target_pairs={{0,1},{1,2},{2,3},{3,0},{4,7},{5,4},{6,5},{7,6},{8,9},{9,10},{10,1... | collective-permute-start | bytes 6193160 | tf_op jit(solution)/shard_map/ppermute | solution.py:378
  5.5 14.3 %collective-permute-start = (bf16[512,256]{1,0:T(8,128)(2,1)S(1)}, bf16[512,256]{1,0:T(8,128)(2,1)S(1)}, u32[]{:S(2)}, u32[]{:S(2)}) collective-permute-start(bf16[512,256]{1,0:T(8,128)(2,1)S(1)} %get-tuple-element.25.own), channel_id=1, source_target_pairs={{0,8},{4,12},{8,16},{12,20},{16,24},{20,28},{24,32},{28,36},{32,40... | collective-permute-start | bytes 786440 | tf_op jit(solution)/shard_map/ppermute | solution.py:338
  9.0 10.8 %collective-permute-start.1 = (f32[8,256]{1,0:T(8,128)S(1)}, f32[8,256]{1,0:T(8,128)S(1)}, u32[]{:S(2)}, u32[]{:S(2)}) collective-permute-start(f32[8,256]{1,0:T(8,128)S(1)} %get-tuple-element.26), channel_id=1, source_target_pairs={{0,4},{4,8},{8,12},{12,16},{16,20},{20,24},{24,28},{28,32},{32,36}... | collective-permute-start | bytes 24584 | tf_op jit(solution)/shard_map/ppermute | solution.py:338
  11.5 14.2 %collective-permute-start.4 = (bf16[512,256]{1,0:T(8,128)(2,1)S(1)}, bf16[512,256]{1,0:T(8,128)(2,1)S(1)}, u32[]{:S(2)}, u32[]{:S(2)}) collective-permute-start(bf16[512,256]{1,0:T(8,128)(2,1)S(1)} %get-tuple-element.31.values0), channel_id=1, source_target_pairs={{0,8},{4,12},{8,16},{12,20},{16,24},{20,28},{24,32},{28,36},{32,40... | collective-permute-start | bytes 786440 | tf_op jit(solution)/shard_map/ppermute | solution.py:338
  20.3 13.3 %collective-permute-start.3 = (bf16[512,256]{1,0:T(8,128)(2,1)S(1)}, bf16[512,256]{1,0:T(8,128)(2,1)S(1)}, u32[]{:S(2)}, u32[]{:S(2)}) collective-permute-start(bf16[512,256]{1,0:T(8,128)(2,1)S(1)} %shard_map.96.ready.keys0), channel_id=1, source_target_pairs={{0,8},{4,12},{8,16},{12,20},{16,24},{20,28},{24,32},{28,36},{32,40... | collective-permute-start | bytes 786440 | tf_op jit(solution)/shard_map/ppermute | solution.py:338
  33.7 2.6 %collective-permute-start.5 = (bf16[512,512]{1,0:T(8,128)(2,1)S(1)}, bf16[512,512]{1,0:T(8,128)(2,1)S(1)}, u32[]{:S(2)}, u32[]{:S(2)}) collective-permute-start(bf16[512,512]{1,0:T(8,128)(2,1)S(1)} %maximum_select_fusion), channel_id=1, source_target_pairs={{0,4},{4,0},{8,12},{12,8},{16,20},{20,16},{24,28},{28,24},{32,36},... | collective-permute-start | bytes 1572872 | tf_op jit(solution)/shard_map/ppermute | solution.py:335
  41.1 1.7 %collective-permute-start.6 = (bf16[512,256]{1,0:T(8,128)(2,1)S(1)}, bf16[512,256]{1,0:T(8,128)(2,1)S(1)}, u32[]{:S(2)}, u32[]{:S(2)}) collective-permute-start(bf16[512,256]{1,0:T(8,128)(2,1)S(1)} %get-tuple-element.34), channel_id=1, source_target_pairs={{0,4},{4,0},{8,12},{12,8},{16,20},{20,16},{24,28},{28,24},{32,36},... | collective-permute-start | bytes 786440 | tf_op jit(solution)/shard_map/ppermute | solution.py:335
  42.9 4.2 %collective-permute-start.7 = (bf16[4032,256]{1,0:T(8,128)(2,1)S(1)}, bf16[4032,256]{1,0:T(8,128)(2,1)S(1)}, u32[]{:S(2)}, u32[]{:S(2)}) collective-permute-start(bf16[4032,256]{1,0:T(8,128)(2,1)S(1)} %collective-permute-done.2.rest_3_), channel_id=1, source_target_pairs={{0,4},{4,0},{8,12},{12,8},{16,20},{20,16},{24,28},{28,24},{32,36},... | collective-permute-start | bytes 6193160 | tf_op jit(solution)/shard_map/ppermute | solution.py:335
  43.4 12.2 %collective-permute-start.14 = (bf16[1344,256]{1,0:T(8,128)(2,1)S(1)}, bf16[1344,256]{1,0:T(8,128)(2,1)S(1)}, u32[]{:S(2)}, u32[]{:S(2)}) collective-permute-start(bf16[1344,256]{1,0:T(8,128)(2,1)S(1)} %slice.3), channel_id=1, source_target_pairs={{0,1},{1,2},{2,3},{3,0},{4,7},{5,4},{6,5},{7,6},{8,9},{9,10},{10,1... | collective-permute-start | bytes 2064392 | tf_op jit(solution)/shard_map/ppermute | solution.py:406
  43.5 10.2 %collective-permute-start.8 = (bf16[512,256]{1,0:T(8,128)(2,1)S(1)}, bf16[512,256]{1,0:T(8,128)(2,1)S(1)}, u32[]{:S(2)}, u32[]{:S(2)}) collective-permute-start(bf16[512,256]{1,0:T(8,128)(2,1)S(1)} %shard_map.100), channel_id=1, source_target_pairs={{8,0},{12,4},{16,8},{20,12},{24,16},{28,20},{32,24},{36,28},{40,32... | collective-permute-start | bytes 786440 | tf_op jit(solution)/shard_map/ppermute | solution.py:338
  47.1 30.0 %copy-start.1 = (bf16[5376,256]{1,0:T(8,128)(2,1)S(1)}, bf16[5376,256]{1,0:T(8,128)(2,1)}, u32[]{:S(2)}) copy-start(bf16[5376,256]{1,0:T(8,128)(2,1)} %values.3) | copy-start | bytes 8257540
  51.8 2.6 %collective-permute-start.9 = (bf16[512,256]{1,0:T(8,128)(2,1)S(1)}, bf16[512,256]{1,0:T(8,128)(2,1)S(1)}, u32[]{:S(2)}, u32[]{:S(2)}) collective-permute-start(bf16[512,256]{1,0:T(8,128)(2,1)S(1)} %get-tuple-element.42), channel_id=1, source_target_pairs={{0,4},{4,0},{8,12},{12,8},{16,20},{20,16},{24,28},{28,24},{32,36},... | collective-permute-start | bytes 786440 | tf_op jit(solution)/shard_map/ppermute | solution.py:335
  53.7 23.4 %copy-start = (bf16[5376,256]{1,0:T(8,128)(2,1)S(1)}, bf16[5376,256]{1,0:T(8,128)(2,1)}, u32[]{:S(2)}) copy-start(bf16[5376,256]{1,0:T(8,128)(2,1)} %keys.3) | copy-start | bytes 8257540
  55.6 21.5 %collective-permute-start.15 = (bf16[1344,256]{1,0:T(8,128)(2,1)S(1)}, bf16[1344,256]{1,0:T(8,128)(2,1)S(1)}, u32[]{:S(2)}, u32[]{:S(2)}) collective-permute-start(bf16[1344,256]{1,0:T(8,128)(2,1)S(1)} %collective-permute-done.14.rest_5_), channel_id=1, source_target_pairs={{0,4},{4,0},{8,12},{12,8},{16,20},{20,16},{24,28},{28,24},{32,36},... | collective-permute-start | bytes 2064392 | tf_op jit(solution)/shard_map/ppermute | solution.py:335
  55.6 10.7 %collective-permute-start.10 = (bf16[512,256]{1,0:T(8,128)(2,1)S(1)}, bf16[512,256]{1,0:T(8,128)(2,1)S(1)}, u32[]{:S(2)}, u32[]{:S(2)}) collective-permute-start(bf16[512,256]{1,0:T(8,128)(2,1)S(1)} %shard_map.103), channel_id=1, source_target_pairs={{8,0},{12,4},{16,8},{20,12},{24,16},{28,20},{32,24},{36,28},{40,32... | collective-permute-start | bytes 786440 | tf_op jit(solution)/shard_map/ppermute | solution.py:338
  60.1 16.0 %collective-permute-start.11 = (bf16[512,256]{1,0:T(8,128)(2,1)S(1)}, bf16[512,256]{1,0:T(8,128)(2,1)S(1)}, u32[]{:S(2)}, u32[]{:S(2)}) collective-permute-start(bf16[512,256]{1,0:T(8,128)(2,1)S(1)} %shard_map.102.own0), channel_id=1, source_target_pairs={{0,1},{1,2},{2,3},{3,0},{4,5},{5,6},{6,7},{7,4},{8,9},{9,10},{10,1... | collective-permute-start | bytes 786440 | tf_op jit(solution)/shard_map/ppermute | solution.py:341
  60.8 15.4 %collective-permute-start.12 = (bf16[512,256]{1,0:T(8,128)(2,1)S(1)}, bf16[512,256]{1,0:T(8,128)(2,1)S(1)}, u32[]{:S(2)}, u32[]{:S(2)}) collective-permute-start(bf16[512,256]{1,0:T(8,128)(2,1)S(1)} %shard_map.102.own0), channel_id=1, source_target_pairs={{0,2},{1,3},{2,0},{3,1},{4,6},{5,7},{6,4},{7,5},{8,10},{9,11},{10,... | collective-permute-start | bytes 786440 | tf_op jit(solution)/shard_map/ppermute | solution.py:341
  62.6 14.4 %collective-permute-start.13 = (bf16[512,256]{1,0:T(8,128)(2,1)S(1)}, bf16[512,256]{1,0:T(8,128)(2,1)S(1)}, u32[]{:S(2)}, u32[]{:S(2)}) collective-permute-start(bf16[512,256]{1,0:T(8,128)(2,1)S(1)} %shard_map.102.own0), channel_id=1, source_target_pairs={{0,3},{1,0},{2,1},{3,2},{4,7},{5,4},{6,5},{7,6},{8,11},{9,8},{10,9... | collective-permute-start | bytes 786440 | tf_op jit(solution)/shard_map/ppermute | solution.py:341
  67.0 19.7 %collective-permute-start.16 = (bf16[512,256]{1,0:T(8,128)(2,1)S(1)}, bf16[512,256]{1,0:T(8,128)(2,1)S(1)}, u32[]{:S(2)}, u32[]{:S(2)}) collective-permute-start(bf16[512,256]{1,0:T(8,128)(2,1)S(1)} %shard_map.104.own1), channel_id=1, source_target_pairs={{0,1},{1,2},{2,3},{3,0},{4,5},{5,6},{6,7},{7,4},{8,9},{9,10},{10,1... | collective-permute-start | bytes 786440 | tf_op jit(solution)/shard_map/ppermute | solution.py:341
  76.1 10.6 %collective-permute-start.17 = (bf16[512,256]{1,0:T(8,128)(2,1)S(1)}, bf16[512,256]{1,0:T(8,128)(2,1)S(1)}, u32[]{:S(2)}, u32[]{:S(2)}) collective-permute-start(bf16[512,256]{1,0:T(8,128)(2,1)S(1)} %shard_map.104.own1), channel_id=1, source_target_pairs={{0,2},{1,3},{2,0},{3,1},{4,6},{5,7},{6,4},{7,5},{8,10},{9,11},{10,... | collective-permute-start | bytes 786440 | tf_op jit(solution)/shard_map/ppermute | solution.py:341
  76.1 11.2 %collective-permute-start.18 = (bf16[512,256]{1,0:T(8,128)(2,1)S(1)}, bf16[512,256]{1,0:T(8,128)(2,1)S(1)}, u32[]{:S(2)}, u32[]{:S(2)}) collective-permute-start(bf16[512,256]{1,0:T(8,128)(2,1)S(1)} %shard_map.104.own1), channel_id=1, source_target_pairs={{0,3},{1,0},{2,1},{3,2},{4,7},{5,4},{6,5},{7,6},{8,11},{9,8},{10,9... | collective-permute-start | bytes 786440 | tf_op jit(solution)/shard_map/ppermute | solution.py:341
  (3 other events, 6.2 us)

commit v7 on v6

--- a/solution.py
+++ b/solution.py
@@ -396,7 +396,7 @@
     query_grads, gathered = [], []
     for head in range(2):
         if head == 1:
-            queries, _, other_near = lax.optimization_barrier((queries, back, other_near))
+            queries, _ = lax.optimization_barrier((queries, back))
         query_part, grad2, grad1, grad0 = attend_call(
             head, place, queries, output_gradient, grad_cols, older_smooth, last, smooth, older_values, exact_values
         )
@@ -406,7 +406,7 @@
             far = lax.ppermute(passed_on[2 * model_rows :], ("seq", "head"), near_pairs)
         sibling_grad = to_sibling(grad1)
         if head == 1:
-            grad2, _ = lax.optimization_barrier((grad2, gathered[0][0]))
+            grad2, other_near, _ = lax.optimization_barrier((grad2, other_near, gathered[0][0]))
         back = vmem_call(merge_kernel, shape_of(BLOCK, 256), (place, grad2, sibling_grad), in_specs=[SMEM, VMEM, VMEM])
         if head == 0:
             back, near_now = lax.optimization_barrier((back, near))

time: 90.1 us -> 90.5 us (level)
  starting transfers between devices: 24.8 us -> 28.7 us
  waiting for transfers between devices: 40.8 us -> 37.2 us
    ppermute x6, waiting for transfers between devices: 16.6 us -> 12 us  [along_head(): lax.ppermute(value, 'head', [(at, (at + steps) % groups) for at in range(...]
    ppermute x6, starting transfers between devices: 3.6 us -> 7.7 us  [along_head(): lax.ppermute(value, 'head', [(at, (at + steps) % groups) for at in range(...]
    ppermute x6, waiting for transfers between devices: 20.4 us -> 22.9 us  [onward(): return lax.ppermute(value, 'seq', shift_pairs(count, steps))]
    ppermute x5, waiting for transfers between devices: 2.66 us -> 1.17 us  [to_sibling(): return lax.ppermute(value, 'seq', siblings)]
  transfers between devices with their start and end apart: 19 -> 19, of which waited for: 13 -> 14; matrix products, arithmetic and copies ran while one was open for 1% -> 1% of each run, Pallas kernels for 12% -> 12%
where the time goes in v7:
time: 90.5 us; the launch traced here: 90.1 us
  waiting for transfers between devices  37.2 us (41%)
  starting transfers between devices  28.7 us (32%)
  Pallas kernels  20.2 us (22%)
  local copies, waits for them, and re-layouts  2.15 us (2%)
  other arithmetic  0.95 us (1%)
    ppermute x6, waiting for transfers between devices, onward(): return lax.ppermute(value, 'seq', shift_pairs(count, steps))  22.9 us
    ppermute x6, starting transfers between devices, onward(): return lax.ppermute(value, 'seq', shift_pairs(count, steps))  18 us
    pallas_call x11, Pallas kernels, vmem_call(): pl.pallas_call(kernel, out_shape=out_shapes, in_specs=in_specs if in_spec...  17.6 us
    ppermute x6, waiting for transfers between devices, along_head(): lax.ppermute(value, 'head', [(at, (at + steps) % groups) for at in range(...  12 us
    ppermute x6, starting transfers between devices, along_head(): lax.ppermute(value, 'head', [(at, (at + steps) % groups) for at in range(...  7.7 us
    pallas_call x1, Pallas kernels, local(): pl.pallas_call(cut_kernel, out_shape=shape_of(3 * model_rows, 256), in_sp...  2.56 us
    unnamed x16, local copies, waits for them, and re-layouts  2.1 us
  transfers between devices with their start and end apart: 19, of which 14 were waited for; matrix products, arithmetic and copies ran while one was open for 1% of the time, Pallas kernels for 12%

profile of v7, /device:TPU:128, one launch (start us, length us, event | category | flops | bytes accessed | tf_op | source)
XLA Modules:
  0.0 90.1 jit_solution(5756588913599949613)
XLA Ops:
  0.7 2.6 %shard_map.98 = bf16[4032,256]{1,0:T(8,128)(2,1)} custom-call(s32[1]{0:T(128)} %bitcast.place.index, s32[1]{0:T(128)} %bitcast.3.group, bf16[5376,256]{1,0:T(8,128)(2,1)} %keys.3, bf16[5376,256]{1,0:T(8,128)(2,1)} %values.3, bf16[512,256]{1,0:T(8,128)(2,1)} %ready.1), custom_call_target="tpu_custom_call" | custom-call | flops 1 | bytes 1 | tf_op jit(solution)/shard_map/pallas_call | solution.py:355
  3.2 1.6 %collective-permute-start.2 = (bf16[4032,256]{1,0:T(8,128)(2,1)}, bf16[4032,256]{1,0:T(8,128)(2,1)S(1)}, u32[]{:S(2)}, u32[]{:S(2)}) collective-permute-start(bf16[4032,256]{1,0:T(8,128)(2,1)} %shard_map.98), channel_id=1, source_target_pairs={{0,1},{1,2},{2,3},{3,0},{4,7},{5,4},{6,5},{7,6},{8,9},{9,10},{10,1... | collective-permute-start | bytes 6193160 | tf_op jit(solution)/shard_map/ppermute | solution.py:378
  5.5 3.5 %collective-permute-start = (bf16[512,256]{1,0:T(8,128)(2,1)S(1)}, bf16[512,256]{1,0:T(8,128)(2,1)S(1)}, u32[]{:S(2)}, u32[]{:S(2)}) collective-permute-start(bf16[512,256]{1,0:T(8,128)(2,1)S(1)} %get-tuple-element.25.own), channel_id=1, source_target_pairs={{0,8},{4,12},{8,16},{12,20},{16,24},{20,28},{24,32},{28,36},{32,40... | collective-permute-start | bytes 786440 | tf_op jit(solution)/shard_map/ppermute | solution.py:338
  9.0 2.5 %collective-permute-start.1 = (f32[8,256]{1,0:T(8,128)S(1)}, f32[8,256]{1,0:T(8,128)S(1)}, u32[]{:S(2)}, u32[]{:S(2)}) collective-permute-start(f32[8,256]{1,0:T(8,128)S(1)} %get-tuple-element.26), channel_id=1, source_target_pairs={{0,4},{4,8},{8,12},{12,16},{16,20},{20,24},{24,28},{28,32},{32,36}... | collective-permute-start | bytes 24584 | tf_op jit(solution)/shard_map/ppermute | solution.py:338
  11.5 3.5 %collective-permute-start.4 = (bf16[512,256]{1,0:T(8,128)(2,1)S(1)}, bf16[512,256]{1,0:T(8,128)(2,1)S(1)}, u32[]{:S(2)}, u32[]{:S(2)}) collective-permute-start(bf16[512,256]{1,0:T(8,128)(2,1)S(1)} %get-tuple-element.31.values0), channel_id=1, source_target_pairs={{0,8},{4,12},{8,16},{12,20},{16,24},{20,28},{24,32},{28,36},{32,40... | collective-permute-start | bytes 786440 | tf_op jit(solution)/shard_map/ppermute | solution.py:338
  15.0 4.8 %collective-permute-done.1.total = f32[8,256]{1,0:T(8,128)S(1)} collective-permute-done((f32[8,256]{1,0:T(8,128)S(1)}, f32[8,256]{1,0:T(8,128)S(1)}, u32[]{:S(2)}, u32[]{:S(2)}) %collective-permute-start.1) | collective-permute-done | bytes 8224 | tf_op jit(solution)/shard_map/ppermute | solution.py:338
  20.3 1.9 %collective-permute-start.3 = (bf16[512,256]{1,0:T(8,128)(2,1)S(1)}, bf16[512,256]{1,0:T(8,128)(2,1)S(1)}, u32[]{:S(2)}, u32[]{:S(2)}) collective-permute-start(bf16[512,256]{1,0:T(8,128)(2,1)S(1)} %shard_map.96.ready.keys0), channel_id=1, source_target_pairs={{0,8},{4,12},{8,16},{12,20},{16,24},{20,28},{24,32},{28,36},{32,40... | collective-permute-start | bytes 786440 | tf_op jit(solution)/shard_map/ppermute | solution.py:338
  22.2 3.4 %collective-permute-done.4.values2 = bf16[512,256]{1,0:T(8,128)(2,1)S(1)} collective-permute-done((bf16[512,256]{1,0:T(8,128)(2,1)S(1)}, bf16[512,256]{1,0:T(8,128)(2,1)S(1)}, u32[]{:S(2)}, u32[]{:S(2)}) %collective-permute-start.4) | collective-permute-done | bytes 262176 | tf_op jit(solution)/shard_map/ppermute | solution.py:338
  25.7 7.9 %collective-permute-done.3.keys2 = bf16[512,256]{1,0:T(8,128)(2,1)S(1)} collective-permute-done((bf16[512,256]{1,0:T(8,128)(2,1)S(1)}, bf16[512,256]{1,0:T(8,128)(2,1)S(1)}, u32[]{:S(2)}, u32[]{:S(2)}) %collective-permute-start.3) | collective-permute-done | bytes 262176 | tf_op jit(solution)/shard_map/ppermute | solution.py:338
  36.3 4.8 %shard_map.99 = (bf16[512,256]{1,0:T(8,128)(2,1)S(1)}, f32[512,256]{1,0:T(8,128)S(1)}, bf16[512,256]{1,0:T(8,128)(2,1)S(1)}, f32[512,256]{1,0:T(8,128)S(1)}) custom-call(s32[1]{0:T(128)} %bitcast.place.index, bf16[512,512]{1,0:T(8,128)(2,1)S(1)} %get-tuple-element.37.queries, bf16[512,512]{1,0:T(8,128)(2,1)S(1)} %get-tuple-element.29.grads, ...), custom_call_target="tpu_custom_call" | custom-call | flops 1 | bytes 1 | tf_op jit(solution)/shard_map/pallas_call | solution.py:32
  43.5 2.1 %collective-permute-start.7 = (bf16[512,256]{1,0:T(8,128)(2,1)S(1)}, bf16[512,256]{1,0:T(8,128)(2,1)S(1)}, u32[]{:S(2)}, u32[]{:S(2)}) collective-permute-start(bf16[512,256]{1,0:T(8,128)(2,1)S(1)} %shard_map.100), channel_id=1, source_target_pairs={{8,0},{12,4},{16,8},{20,12},{24,16},{28,20},{32,24},{36,28},{40,32... | collective-permute-start | bytes 786440 | tf_op jit(solution)/shard_map/ppermute | solution.py:338
  45.6 4.8 %shard_map.101 = (bf16[512,256]{1,0:T(8,128)(2,1)S(1)}, f32[512,256]{1,0:T(8,128)S(1)}, bf16[512,256]{1,0:T(8,128)(2,1)S(1)}, f32[512,256]{1,0:T(8,128)S(1)}) custom-call(s32[1]{0:T(128)} %bitcast.place.index, bf16[512,512]{1,0:T(8,128)(2,1)S(1)} %get-tuple-element.37.queries, bf16[512,512]{1,0:T(8,128)(2,1)S(1)} %get-tuple-element.29.grads, ...), custom_call_target="tpu_custom_call" | custom-call | flops 1 | bytes 1 | tf_op jit(solution)/shard_map/pallas_call | solution.py:32
  50.6 3.1 %collective-permute-done.7.later = bf16[512,256]{1,0:T(8,128)(2,1)S(1)} collective-permute-done((bf16[512,256]{1,0:T(8,128)(2,1)S(1)}, bf16[512,256]{1,0:T(8,128)(2,1)S(1)}, u32[]{:S(2)}, u32[]{:S(2)}) %collective-permute-start.7) | collective-permute-done | bytes 262176 | tf_op jit(solution)/shard_map/ppermute | solution.py:338
  55.6 4.5 %collective-permute-start.10 = (bf16[512,256]{1,0:T(8,128)(2,1)S(1)}, bf16[512,256]{1,0:T(8,128)(2,1)S(1)}, u32[]{:S(2)}, u32[]{:S(2)}) collective-permute-start(bf16[512,256]{1,0:T(8,128)(2,1)S(1)} %shard_map.103), channel_id=1, source_target_pairs={{8,0},{12,4},{16,8},{20,12},{24,16},{28,20},{32,24},{36,28},{40,32... | collective-permute-start | bytes 786440 | tf_op jit(solution)/shard_map/ppermute | solution.py:338
  61.2 1.6 %collective-permute-start.12 = (bf16[512,256]{1,0:T(8,128)(2,1)S(1)}, bf16[512,256]{1,0:T(8,128)(2,1)S(1)}, u32[]{:S(2)}, u32[]{:S(2)}) collective-permute-start(bf16[512,256]{1,0:T(8,128)(2,1)S(1)} %shard_map.102.own0), channel_id=1, source_target_pairs={{0,2},{1,3},{2,0},{3,1},{4,6},{5,7},{6,4},{7,5},{8,10},{9,11},{10,... | collective-permute-start | bytes 786440 | tf_op jit(solution)/shard_map/ppermute | solution.py:341
  62.8 3.5 %collective-permute-done.10.later = bf16[512,256]{1,0:T(8,128)(2,1)S(1)} collective-permute-done((bf16[512,256]{1,0:T(8,128)(2,1)S(1)}, bf16[512,256]{1,0:T(8,128)(2,1)S(1)}, u32[]{:S(2)}, u32[]{:S(2)}) %collective-permute-start.10) | collective-permute-done | bytes 262176 | tf_op jit(solution)/shard_map/ppermute | solution.py:338
  68.1 1.3 %collective-permute-done.13.rest_2_ = bf16[512,256]{1,0:T(8,128)(2,1)S(1)} collective-permute-done((bf16[512,256]{1,0:T(8,128)(2,1)S(1)}, bf16[512,256]{1,0:T(8,128)(2,1)S(1)}, u32[]{:S(2)}, u32[]{:S(2)}) %collective-permute-start.13) | collective-permute-done | bytes 262176 | tf_op jit(solution)/shard_map/ppermute | solution.py:341
  70.1 1.8 %collective-permute-done.12.rest_1_ = bf16[512,256]{1,0:T(8,128)(2,1)S(1)} collective-permute-done((bf16[512,256]{1,0:T(8,128)(2,1)S(1)}, bf16[512,256]{1,0:T(8,128)(2,1)S(1)}, u32[]{:S(2)}, u32[]{:S(2)}) %collective-permute-start.12) | collective-permute-done | bytes 262176 | tf_op jit(solution)/shard_map/ppermute | solution.py:341
  71.9 3.3 %collective-permute-start.16 = (bf16[512,256]{1,0:T(8,128)(2,1)S(1)}, bf16[512,256]{1,0:T(8,128)(2,1)S(1)}, u32[]{:S(2)}, u32[]{:S(2)}) collective-permute-start(bf16[512,256]{1,0:T(8,128)(2,1)S(1)} %shard_map.104.own1), channel_id=1, source_target_pairs={{0,1},{1,2},{2,3},{3,0},{4,5},{5,6},{6,7},{7,4},{8,9},{9,10},{10,1... | collective-permute-start | bytes 786440 | tf_op jit(solution)/shard_map/ppermute | solution.py:341
  76.0 1.6 %collective-permute-done.11.rest_0_ = bf16[512,256]{1,0:T(8,128)(2,1)S(1)} collective-permute-done((bf16[512,256]{1,0:T(8,128)(2,1)S(1)}, bf16[512,256]{1,0:T(8,128)(2,1)S(1)}, u32[]{:S(2)}, u32[]{:S(2)}) %collective-permute-start.11) | collective-permute-done | bytes 262176 | tf_op jit(solution)/shard_map/ppermute | solution.py:341
  77.6 2.8 %shard_map.105.early = f32[1344,512]{1,0:T(8,128)S(1)} custom-call(s32[1]{0:T(128)} %bitcast.place.index, s32[1]{0:T(128)} %bitcast.3.group, bf16[5376,256]{1,0:T(8,128)(2,1)S(1)} %copy-done, bf16[5376,256]{1,0:T(8,128)(2,1)S(1)} %copy-done.1, bf16[512,256]{1,0:T(8,128)(2,1)S(1)} %shard_map.102.own0, bf16[512,256]{1,0:T(8,128)(2,1)S(1)} %shard_map.104.own1, ...), custom_call_target="tpu_custom_call" | custom-call | flops 1 | bytes 1 | tf_op jit(solution)/shard_map/pallas_call | solution.py:32
  80.7 2.5 %collective-permute-done.17.rest_1_ = bf16[512,256]{1,0:T(8,128)(2,1)S(1)} collective-permute-done((bf16[512,256]{1,0:T(8,128)(2,1)S(1)}, bf16[512,256]{1,0:T(8,128)(2,1)S(1)}, u32[]{:S(2)}, u32[]{:S(2)}) %collective-permute-start.17) | collective-permute-done | bytes 262176 | tf_op jit(solution)/shard_map/ppermute | solution.py:341
  83.2 4.5 %collective-permute-done.16.rest_0_ = bf16[512,256]{1,0:T(8,128)(2,1)S(1)} collective-permute-done((bf16[512,256]{1,0:T(8,128)(2,1)S(1)}, bf16[512,256]{1,0:T(8,128)(2,1)S(1)}, u32[]{:S(2)}, u32[]{:S(2)}) %collective-permute-start.16) | collective-permute-done | bytes 262176 | tf_op jit(solution)/shard_map/ppermute | solution.py:341
  87.7 2.4 %shard_map.106 = bf16[1344,512]{1,0:T(8,128)(2,1)} custom-call(s32[1]{0:T(128)} %bitcast.place.index, f32[1344,512]{1,0:T(8,128)S(1)} %shard_map.105.early, bf16[512,256]{1,0:T(8,128)(2,1)S(1)} %collective-permute-done.16.rest_0_, bf16[512,256]{1,0:T(8,128)(2,1)S(1)} %collective-permute-done.17.rest_1_, ...), custom_call_target="tpu_custom_call" | custom-call | flops 1 | bytes 1 | tf_op jit(solution)/shard_map/pallas_call | solution.py:32
  (45 shorter events, 13.0 us)
Async XLA Ops:
  0.6 4.2 %copy-start.2 = (bf16[512,256]{1,0:T(8,128)(2,1)S(1)}, bf16[512,256]{1,0:T(8,128)(2,1)}, u32[]{:S(2)}) copy-start(bf16[512,256]{1,0:T(8,128)(2,1)} %ready.1) | copy-start | bytes 786436
  0.6 4.2 %copy-start.5 = (bf16[512,256]{1,0:T(8,128)(2,1)S(1)}, bf16[512,256]{1,0:T(8,128)(2,1)}, u32[]{:S(2)}) copy-start(bf16[512,256]{1,0:T(8,128)(2,1)} %values.2) | copy-start | bytes 786436
  0.7 4.2 %copy-start.6 = (s32[4,2]{0,1:T(2,128)S(1)}, s32[4,2]{0,1:T(2,128)}, u32[]{:S(2)}) copy-start(s32[4,2]{0,1:T(2,128)} %param.12) | copy-start | bytes 100
  3.2 33.1 %collective-permute-start.2 = (bf16[4032,256]{1,0:T(8,128)(2,1)}, bf16[4032,256]{1,0:T(8,128)(2,1)S(1)}, u32[]{:S(2)}, u32[]{:S(2)}) collective-permute-start(bf16[4032,256]{1,0:T(8,128)(2,1)} %shard_map.98), channel_id=1, source_target_pairs={{0,1},{1,2},{2,3},{3,0},{4,7},{5,4},{6,5},{7,6},{8,9},{9,10},{10,1... | collective-permute-start | bytes 6193160 | tf_op jit(solution)/shard_map/ppermute | solution.py:378
  5.5 14.3 %collective-permute-start = (bf16[512,256]{1,0:T(8,128)(2,1)S(1)}, bf16[512,256]{1,0:T(8,128)(2,1)S(1)}, u32[]{:S(2)}, u32[]{:S(2)}) collective-permute-start(bf16[512,256]{1,0:T(8,128)(2,1)S(1)} %get-tuple-element.25.own), channel_id=1, source_target_pairs={{0,8},{4,12},{8,16},{12,20},{16,24},{20,28},{24,32},{28,36},{32,40... | collective-permute-start | bytes 786440 | tf_op jit(solution)/shard_map/ppermute | solution.py:338
  9.0 10.8 %collective-permute-start.1 = (f32[8,256]{1,0:T(8,128)S(1)}, f32[8,256]{1,0:T(8,128)S(1)}, u32[]{:S(2)}, u32[]{:S(2)}) collective-permute-start(f32[8,256]{1,0:T(8,128)S(1)} %get-tuple-element.26), channel_id=1, source_target_pairs={{0,4},{4,8},{8,12},{12,16},{16,20},{20,24},{24,28},{28,32},{32,36}... | collective-permute-start | bytes 24584 | tf_op jit(solution)/shard_map/ppermute | solution.py:338
  11.5 14.2 %collective-permute-start.4 = (bf16[512,256]{1,0:T(8,128)(2,1)S(1)}, bf16[512,256]{1,0:T(8,128)(2,1)S(1)}, u32[]{:S(2)}, u32[]{:S(2)}) collective-permute-start(bf16[512,256]{1,0:T(8,128)(2,1)S(1)} %get-tuple-element.31.values0), channel_id=1, source_target_pairs={{0,8},{4,12},{8,16},{12,20},{16,24},{20,28},{24,32},{28,36},{32,40... | collective-permute-start | bytes 786440 | tf_op jit(solution)/shard_map/ppermute | solution.py:338
  20.3 13.3 %collective-permute-start.3 = (bf16[512,256]{1,0:T(8,128)(2,1)S(1)}, bf16[512,256]{1,0:T(8,128)(2,1)S(1)}, u32[]{:S(2)}, u32[]{:S(2)}) collective-permute-start(bf16[512,256]{1,0:T(8,128)(2,1)S(1)} %shard_map.96.ready.keys0), channel_id=1, source_target_pairs={{0,8},{4,12},{8,16},{12,20},{16,24},{20,28},{24,32},{28,36},{32,40... | collective-permute-start | bytes 786440 | tf_op jit(solution)/shard_map/ppermute | solution.py:338
  33.7 2.6 %collective-permute-start.5 = (bf16[512,512]{1,0:T(8,128)(2,1)S(1)}, bf16[512,512]{1,0:T(8,128)(2,1)S(1)}, u32[]{:S(2)}, u32[]{:S(2)}) collective-permute-start(bf16[512,512]{1,0:T(8,128)(2,1)S(1)} %maximum_select_fusion), channel_id=1, source_target_pairs={{0,4},{4,0},{8,12},{12,8},{16,20},{20,16},{24,28},{28,24},{32,36},... | collective-permute-start | bytes 1572872 | tf_op jit(solution)/shard_map/ppermute | solution.py:335
  41.1 1.7 %collective-permute-start.6 = (bf16[512,256]{1,0:T(8,128)(2,1)S(1)}, bf16[512,256]{1,0:T(8,128)(2,1)S(1)}, u32[]{:S(2)}, u32[]{:S(2)}) collective-permute-start(bf16[512,256]{1,0:T(8,128)(2,1)S(1)} %get-tuple-element.34), channel_id=1, source_target_pairs={{0,4},{4,0},{8,12},{12,8},{16,20},{20,16},{24,28},{28,24},{32,36},... | collective-permute-start | bytes 786440 | tf_op jit(solution)/shard_map/ppermute | solution.py:335
  42.9 11.5 %collective-permute-start.9 = (bf16[4032,256]{1,0:T(8,128)(2,1)S(1)}, bf16[4032,256]{1,0:T(8,128)(2,1)S(1)}, u32[]{:S(2)}, u32[]{:S(2)}) collective-permute-start(bf16[4032,256]{1,0:T(8,128)(2,1)S(1)} %collective-permute-done.2.rest_3_), channel_id=1, source_target_pairs={{0,4},{4,0},{8,12},{12,8},{16,20},{20,16},{24,28},{28,24},{32,36},... | collective-permute-start | bytes 6193160 | tf_op jit(solution)/shard_map/ppermute | solution.py:335
  43.4 12.2 %collective-permute-start.14 = (bf16[1344,256]{1,0:T(8,128)(2,1)S(1)}, bf16[1344,256]{1,0:T(8,128)(2,1)S(1)}, u32[]{:S(2)}, u32[]{:S(2)}) collective-permute-start(bf16[1344,256]{1,0:T(8,128)(2,1)S(1)} %slice.3), channel_id=1, source_target_pairs={{0,1},{1,2},{2,3},{3,0},{4,7},{5,4},{6,5},{7,6},{8,9},{9,10},{10,1... | collective-permute-start | bytes 2064392 | tf_op jit(solution)/shard_map/ppermute | solution.py:406
  43.5 10.2 %collective-permute-start.7 = (bf16[512,256]{1,0:T(8,128)(2,1)S(1)}, bf16[512,256]{1,0:T(8,128)(2,1)S(1)}, u32[]{:S(2)}, u32[]{:S(2)}) collective-permute-start(bf16[512,256]{1,0:T(8,128)(2,1)S(1)} %shard_map.100), channel_id=1, source_target_pairs={{8,0},{12,4},{16,8},{20,12},{24,16},{28,20},{32,24},{36,28},{40,32... | collective-permute-start | bytes 786440 | tf_op jit(solution)/shard_map/ppermute | solution.py:338
  45.6 32.0 %copy-start.1 = (bf16[5376,256]{1,0:T(8,128)(2,1)S(1)}, bf16[5376,256]{1,0:T(8,128)(2,1)}, u32[]{:S(2)}) copy-start(bf16[5376,256]{1,0:T(8,128)(2,1)} %values.3) | copy-start | bytes 8257540
  50.4 4.1 %collective-permute-start.8 = (bf16[512,256]{1,0:T(8,128)(2,1)S(1)}, bf16[512,256]{1,0:T(8,128)(2,1)S(1)}, u32[]{:S(2)}, u32[]{:S(2)}) collective-permute-start(bf16[512,256]{1,0:T(8,128)(2,1)S(1)} %get-tuple-element.41), channel_id=1, source_target_pairs={{0,4},{4,0},{8,12},{12,8},{16,20},{20,16},{24,28},{28,24},{32,36},... | collective-permute-start | bytes 786440 | tf_op jit(solution)/shard_map/ppermute | solution.py:335
  53.7 23.9 %copy-start = (bf16[5376,256]{1,0:T(8,128)(2,1)S(1)}, bf16[5376,256]{1,0:T(8,128)(2,1)}, u32[]{:S(2)}) copy-start(bf16[5376,256]{1,0:T(8,128)(2,1)} %keys.3) | copy-start | bytes 8257540
  55.6 22.0 %collective-permute-start.15 = (bf16[1344,256]{1,0:T(8,128)(2,1)S(1)}, bf16[1344,256]{1,0:T(8,128)(2,1)S(1)}, u32[]{:S(2)}, u32[]{:S(2)}) collective-permute-start(bf16[1344,256]{1,0:T(8,128)(2,1)S(1)} %collective-permute-done.14.rest_5_), channel_id=1, source_target_pairs={{0,4},{4,0},{8,12},{12,8},{16,20},{20,16},{24,28},{28,24},{32,36},... | collective-permute-start | bytes 2064392 | tf_op jit(solution)/shard_map/ppermute | solution.py:335
  55.6 10.7 %collective-permute-start.10 = (bf16[512,256]{1,0:T(8,128)(2,1)S(1)}, bf16[512,256]{1,0:T(8,128)(2,1)S(1)}, u32[]{:S(2)}, u32[]{:S(2)}) collective-permute-start(bf16[512,256]{1,0:T(8,128)(2,1)S(1)} %shard_map.103), channel_id=1, source_target_pairs={{8,0},{12,4},{16,8},{20,12},{24,16},{28,20},{32,24},{36,28},{40,32... | collective-permute-start | bytes 786440 | tf_op jit(solution)/shard_map/ppermute | solution.py:338
  60.2 9.2 %collective-permute-start.13 = (bf16[512,256]{1,0:T(8,128)(2,1)S(1)}, bf16[512,256]{1,0:T(8,128)(2,1)S(1)}, u32[]{:S(2)}, u32[]{:S(2)}) collective-permute-start(bf16[512,256]{1,0:T(8,128)(2,1)S(1)} %shard_map.102.own0), channel_id=1, source_target_pairs={{0,3},{1,0},{2,1},{3,2},{4,7},{5,4},{6,5},{7,6},{8,11},{9,8},{10,9... | collective-permute-start | bytes 786440 | tf_op jit(solution)/shard_map/ppermute | solution.py:341
  61.2 10.7 %collective-permute-start.12 = (bf16[512,256]{1,0:T(8,128)(2,1)S(1)}, bf16[512,256]{1,0:T(8,128)(2,1)S(1)}, u32[]{:S(2)}, u32[]{:S(2)}) collective-permute-start(bf16[512,256]{1,0:T(8,128)(2,1)S(1)} %shard_map.102.own0), channel_id=1, source_target_pairs={{0,2},{1,3},{2,0},{3,1},{4,6},{5,7},{6,4},{7,5},{8,10},{9,11},{10,... | collective-permute-start | bytes 786440 | tf_op jit(solution)/shard_map/ppermute | solution.py:341
  62.8 14.8 %collective-permute-start.11 = (bf16[512,256]{1,0:T(8,128)(2,1)S(1)}, bf16[512,256]{1,0:T(8,128)(2,1)S(1)}, u32[]{:S(2)}, u32[]{:S(2)}) collective-permute-start(bf16[512,256]{1,0:T(8,128)(2,1)S(1)} %shard_map.102.own0), channel_id=1, source_target_pairs={{0,1},{1,2},{2,3},{3,0},{4,5},{5,6},{6,7},{7,4},{8,9},{9,10},{10,1... | collective-permute-start | bytes 786440 | tf_op jit(solution)/shard_map/ppermute | solution.py:341
  67.0 13.6 %collective-permute-start.18 = (bf16[512,256]{1,0:T(8,128)(2,1)S(1)}, bf16[512,256]{1,0:T(8,128)(2,1)S(1)}, u32[]{:S(2)}, u32[]{:S(2)}) collective-permute-start(bf16[512,256]{1,0:T(8,128)(2,1)S(1)} %shard_map.104.own1), channel_id=1, source_target_pairs={{0,3},{1,0},{2,1},{3,2},{4,7},{5,4},{6,5},{7,6},{8,11},{9,8},{10,9... | collective-permute-start | bytes 786440 | tf_op jit(solution)/shard_map/ppermute | solution.py:341
  69.4 13.8 %collective-permute-start.17 = (bf16[512,256]{1,0:T(8,128)(2,1)S(1)}, bf16[512,256]{1,0:T(8,128)(2,1)S(1)}, u32[]{:S(2)}, u32[]{:S(2)}) collective-permute-start(bf16[512,256]{1,0:T(8,128)(2,1)S(1)} %shard_map.104.own1), channel_id=1, source_target_pairs={{0,2},{1,3},{2,0},{3,1},{4,6},{5,7},{6,4},{7,5},{8,10},{9,11},{10,... | collective-permute-start | bytes 786440 | tf_op jit(solution)/shard_map/ppermute | solution.py:341
  71.9 15.8 %collective-permute-start.16 = (bf16[512,256]{1,0:T(8,128)(2,1)S(1)}, bf16[512,256]{1,0:T(8,128)(2,1)S(1)}, u32[]{:S(2)}, u32[]{:S(2)}) collective-permute-start(bf16[512,256]{1,0:T(8,128)(2,1)S(1)} %shard_map.104.own1), channel_id=1, source_target_pairs={{0,1},{1,2},{2,3},{3,0},{4,5},{5,6},{6,7},{7,4},{8,9},{9,10},{10,1... | collective-permute-start | bytes 786440 | tf_op jit(solution)/shard_map/ppermute | solution.py:341
  (3 other events, 6.2 us)
